TPU v7x, 32 devices: a whole 2x2x4 slice. The times are simulated.
32 devices in a mesh: dp: 16 (over z, x, core), mp: 2 (over y).
Axes of the slice: x: 2, y: 2, z: 4, core: 2. Of those that a mesh axis runs over, the one named last changes fastest.
Arguments:
- patches: bfloat16 [40960, 512], P(('dp', 'mp')), may hold values from -6 to 6
- cotangent: bfloat16 [40960, 512], P(('dp', 'mp')), may hold values from -6 to 6
- key_count: int32 [80], P('dp'), may hold values from 64 to 512, as said below
- w_qkv: float32 [3, 512, 512], P(None, None, 'mp')
- w_proj: float32 [512, 512], P('mp'), may hold values from -1 to 1
- w_up: float32 [512, 2048], P(None, 'mp')
- w_down: float32 [2048, 512], P('mp'), may hold values from -0.125 to 0.125
- qv_bias: float32 [2, 512], P(None, 'mp'), may hold values from -3 to 3
- up_bias: float32 [2048], P('mp'), may hold values from -3 to 3
- vec_params: float32 [6, 512], replicated
- first_qkv: float32 [3, 512, 512], P(None, None, 'mp'), may hold values from -0.00028163442 to 0.00028163442
- second_qkv: float32 [3, 512, 512], P(None, None, 'mp'), may hold values from 1.6815404e-08 to 6.6627074e-08
- first_proj: float32 [512, 512], P('mp'), may hold values from -0.00028163442 to 0.00028163442
- second_proj: float32 [512, 512], P('mp'), may hold values from 1.6815404e-08 to 6.6627074e-08
- first_up: float32 [512, 2048], P(None, 'mp'), may hold values from -0.00028163442 to 0.00028163442
- second_up: float32 [512, 2048], P(None, 'mp'), may hold values from 1.6815404e-08 to 6.6627074e-08
- first_down: float32 [2048, 512], P('mp'), may hold values from -0.00028163442 to 0.00028163442
- second_down: float32 [2048, 512], P('mp'), may hold values from 1.6815404e-08 to 6.6627074e-08
- first_qv_bias: float32 [2, 512], P(None, 'mp'), may hold values from -0.00056326884 to 0.00056326884
- second_qv_bias: float32 [2, 512], P(None, 'mp'), may hold values from 6.6627074e-08 to 2.665083e-07
- first_up_bias: float32 [2048], P('mp'), may hold values from -0.00056326884 to 0.00056326884
- second_up_bias: float32 [2048], P('mp'), may hold values from 9.518153e-09 to 3.8072614e-08
- first_vec: float32 [6, 512], replicated, may hold values from -0.00056326884 to 0.00056326884
- second_vec: float32 [6, 512], replicated, may hold values from 6.6627074e-08 to 2.665083e-07
Outputs:
- activations: bfloat16 [40960, 512], P(('dp', 'mp'))
- input_grad: float32 [40960, 512], P(('dp', 'mp'))
- grad_norm: float32 [], replicated
- qkv_new: float32 [3, 512, 512], P(None, None, 'mp')
- qkv_first: float32 [3, 512, 512], P(None, None, 'mp')
- qkv_second: float32 [3, 512, 512], P(None, None, 'mp')
- proj_new: float32 [512, 512], P('mp')
- proj_first: float32 [512, 512], P('mp')
- proj_second: float32 [512, 512], P('mp')
- up_new: float32 [512, 2048], P(None, 'mp')
- up_first: float32 [512, 2048], P(None, 'mp')
- up_second: float32 [512, 2048], P(None, 'mp')
- down_new: float32 [2048, 512], P('mp')
- down_first: float32 [2048, 512], P('mp')
- down_second: float32 [2048, 512], P('mp')
- qv_bias_new: float32 [2, 512], P(None, 'mp')
- qv_bias_first: float32 [2, 512], P(None, 'mp')
- qv_bias_second: float32 [2, 512], P(None, 'mp')
- up_bias_new: float32 [2048], P('mp')
- up_bias_first: float32 [2048], P('mp')
- up_bias_second: float32 [2048], P('mp')
- vec_new: float32 [6, 512], replicated
- vec_first: float32 [6, 512], replicated
- vec_second: float32 [6, 512], replicated
Inputs may be any that keep to these rules, and one draw needn't show every extreme that they name: `key_count`: each group's count is 512 (a full field) or between 64 and 512 // 4 (a small field padded); group 0 is full.
All inputs are finite; a program needn't handle non-finite values.
Results may differ from a plain program's by a relative error of at most 0.025.
Values may be sent and summed in bfloat16 or wider, within the bound.
A program may use at most 256 MiB of HBM per device.

v0:
```python
import jax
import jax.numpy as jnp
from jax import lax
from jax.sharding import PartitionSpec as P

HD = 32
ADAM_STEP = 10


NORM_EPS = 1e-06
BETA_FIRST = 0.9
BETA_SECOND = 0.95
ADAM_EPS = 1e-08
DECAY_RATE = 0.05
MATRIX_RATE = 0.1
VECTOR_RATE = 0.8
CLIP_NORM = 1.0
MASK_FILL = -1e30


def norm_forward(values, norm_gain, norm_shift):
    row_mean = jnp.mean(values, axis=-1, keepdims=True)
    centred = values - row_mean
    inverse = lax.rsqrt(jnp.mean(centred * centred, axis=-1, keepdims=True) + NORM_EPS)
    normed = centred * inverse
    return (normed * norm_gain + norm_shift, normed, inverse)


def norm_backward(grad_rows, normed, inverse, norm_gain):
    scaled = grad_rows * norm_gain
    centre_term = jnp.mean(scaled, axis=-1, keepdims=True)
    slope_term = jnp.mean(scaled * normed, axis=-1, keepdims=True)
    return inverse * (scaled - centre_term - normed * slope_term)


def exact_gelu(values):
    return jax.nn.gelu(values, approximate=False)


def key_mask(key_count, length):
    position = lax.broadcasted_iota(jnp.int32, (1, 1, 1, length), 3)
    return position < key_count[:, None, None, None]


def masked_scores(queries, key_rows, key_count):
    raw_scores = jnp.einsum(
        "sqhe,skhe->shqk", queries, key_rows, preferred_element_type=jnp.float32
    )
    scaled = raw_scores * queries.shape[-1] ** (-0.5)
    return jnp.where(key_mask(key_count, key_rows.shape[1]), scaled, MASK_FILL)


def attend_backward(queries, key_rows, value_rows, key_count, log_total, attended_grad):
    scores = masked_scores(queries, key_rows, key_count)
    probs = jnp.exp(scores - log_total)
    probs_low = probs.astype(jnp.bfloat16)
    probs_grad = jnp.einsum(
        "sqhe,skhe->shqk", attended_grad, value_rows, preferred_element_type=jnp.float32
    )
    score_grad = probs * (probs_grad - jnp.sum(probs_grad * probs, axis=-1, keepdims=True))
    visible = key_mask(key_count, key_rows.shape[1])
    raw_grad = jnp.where(visible, score_grad * queries.shape[-1] ** (-0.5), 0.0).astype(
        jnp.bfloat16
    )
    query_grad = jnp.einsum(
        "shqk,skhe->sqhe", raw_grad, key_rows, preferred_element_type=jnp.float32
    )
    key_grad = jnp.einsum("shqk,sqhe->skhe", raw_grad, queries, preferred_element_type=jnp.float32)
    value_grad = jnp.einsum(
        "shqk,sqhe->skhe", probs_low, attended_grad, preferred_element_type=jnp.float32
    )
    return jnp.stack([query_grad, key_grad, value_grad])


def own_slice(values, own_start, own_rows):
    return lax.dynamic_slice_in_dim(values, own_start, own_rows, 0)


def contract_rows(left, right):
    return lax.dot_general(
        left, right, (((0,), (0,)), ((), ())), preferred_element_type=jnp.float32
    )


def contract_cols(left, right):
    return lax.dot_general(
        left, right, (((1,), (1,)), ((), ())), preferred_element_type=jnp.float32
    )


def adam_update(weight, gradient, moment_one, moment_two, step_rate, decay_rate):
    first_new = BETA_FIRST * moment_one + (1.0 - BETA_FIRST) * gradient
    second_new = BETA_SECOND * moment_two + (1.0 - BETA_SECOND) * gradient * gradient
    first_hat = first_new / (1.0 - BETA_FIRST**ADAM_STEP)
    second_hat = second_new / (1.0 - BETA_SECOND**ADAM_STEP)
    weight_new = weight - step_rate * (
        first_hat / (jnp.sqrt(second_hat) + ADAM_EPS) + decay_rate * weight
    )
    return (weight_new, first_new, second_new)


def local(
    patches,
    cotangent,
    key_count,
    w_qkv,
    w_proj,
    w_up,
    w_down,
    qv_bias,
    up_bias,
    vec_params,
    first_qkv,
    second_qkv,
    first_proj,
    second_proj,
    first_up,
    second_up,
    first_down,
    second_down,
    first_qv_bias,
    second_qv_bias,
    first_up_bias,
    second_up_bias,
    first_vec,
    second_vec,
):
    own_rows = patches.shape[0]
    seq_count = key_count.shape[0]
    own_start = lax.axis_index("mp") * own_rows
    local_width = w_proj.shape[0]
    local_heads = local_width // HD
    own_grad = cotangent.astype(jnp.float32)
    qkv_low = w_qkv.astype(jnp.bfloat16)
    proj_low = w_proj.astype(jnp.bfloat16)
    up_low = w_up.astype(jnp.bfloat16)
    down_low = w_down.astype(jnp.bfloat16)
    gain_one, shift_one = (vec_params[0], vec_params[1])
    gain_two, shift_two = (vec_params[2], vec_params[3])
    proj_shift, down_shift = (vec_params[4], vec_params[5])
    qkv_shift = jnp.stack([qv_bias[0], jnp.zeros_like(qv_bias[0]), qv_bias[1]])[:, None, :]
    gathered, grad_all = (
        lax.all_gather(patches, "mp", axis=0, tiled=True),
        lax.all_gather(cotangent, "mp", axis=0, tiled=True),
    )
    whole_rows = gathered.astype(jnp.float32)
    normed_all, unit_one, inverse_one = norm_forward(whole_rows, gain_one, shift_one)
    norm_one = normed_all.astype(jnp.bfloat16)
    projected = (
        jnp.einsum("td,cde->cte", norm_one, qkv_low, preferred_element_type=jnp.float32) + qkv_shift
    )
    shaped = projected.astype(jnp.bfloat16).reshape(3, seq_count, -1, local_heads, HD)
    queries, key_rows, value_rows = (shaped[0], shaped[1], shaped[2])
    scores = masked_scores(queries, key_rows, key_count)
    top_score = jnp.max(scores, axis=-1, keepdims=True)
    log_total = top_score + jnp.log(jnp.sum(jnp.exp(scores - top_score), axis=-1, keepdims=True))
    probs_low = jnp.exp(scores - log_total).astype(jnp.bfloat16)
    attended = jnp.einsum(
        "shqk,skhe->sqhe", probs_low, value_rows, preferred_element_type=jnp.float32
    )
    attended_low = attended.astype(jnp.bfloat16).reshape(-1, local_width)
    proj_part = jnp.dot(attended_low, proj_low, preferred_element_type=jnp.float32)
    resid_all = whole_rows + lax.psum(proj_part, "mp") + proj_shift
    mid_all, unit_two, inverse_two = norm_forward(resid_all, gain_two, shift_two)
    norm_two = mid_all.astype(jnp.bfloat16)
    up_pre = jnp.dot(norm_two, up_low, preferred_element_type=jnp.float32) + up_bias
    hidden_full, gelu_pull = jax.vjp(exact_gelu, up_pre)
    hidden_low = hidden_full.astype(jnp.bfloat16)
    down_part = jnp.dot(hidden_low, down_low, preferred_element_type=jnp.float32)
    out_all = (
        resid_all + lax.psum(down_part.astype(jnp.bfloat16), "mp").astype(jnp.float32) + down_shift
    )
    block_out = own_slice(out_all, own_start, own_rows)
    activations = block_out.astype(jnp.bfloat16)
    down_grad = contract_rows(hidden_low, grad_all)
    hidden_grad = contract_cols(grad_all, down_low)
    up_grad_rows = gelu_pull(hidden_grad)[0].astype(jnp.bfloat16)
    up_grad = contract_rows(norm_two, up_grad_rows)
    up_bias_grad = jnp.sum(up_grad_rows.astype(jnp.float32), axis=0)
    mid_part = contract_cols(up_grad_rows, up_low)
    mid_all_grad = lax.psum(mid_part.astype(jnp.bfloat16), "mp").astype(jnp.float32)
    resid_all_grad = grad_all.astype(jnp.float32) + norm_backward(
        mid_all_grad, unit_two, inverse_two, gain_two
    )
    branch_low = resid_all_grad.astype(jnp.bfloat16)
    own_branch = own_slice(branch_low, own_start, own_rows)
    mid_grad = own_slice(mid_all_grad, own_start, own_rows)
    mid_unit = own_slice(unit_two, own_start, own_rows)
    proj_grad = contract_rows(attended_low, branch_low)
    attended_grad = (
        contract_cols(branch_low, proj_low)
        .astype(jnp.bfloat16)
        .reshape(seq_count, -1, local_heads, HD)
    )
    qkv_grads = attend_backward(queries, key_rows, value_rows, key_count, log_total, attended_grad)
    qkv_grad_rows = qkv_grads.reshape(3, -1, local_width).astype(jnp.bfloat16)
    qkv_grad = jnp.einsum(
        "td,cte->cde", norm_one, qkv_grad_rows, preferred_element_type=jnp.float32
    )
    qkv_grad_sums = jnp.sum(qkv_grad_rows.astype(jnp.float32), axis=1)
    qv_bias_grad = jnp.stack([qkv_grad_sums[0], qkv_grad_sums[2]])
    first_part = jnp.einsum(
        "cte,cde->td", qkv_grad_rows, qkv_low, preferred_element_type=jnp.float32
    )
    first_all = lax.psum(first_part.astype(jnp.bfloat16), "mp").astype(jnp.float32)
    input_all = resid_all_grad + norm_backward(first_all, unit_one, inverse_one, gain_one)
    input_grad = own_slice(input_all, own_start, own_rows)
    own_first_grad = own_slice(first_all, own_start, own_rows)
    own_unit_one = own_slice(unit_one, own_start, own_rows)
    vec_grad = jnp.stack(
        [
            jnp.sum(own_first_grad * own_unit_one, axis=0),
            jnp.sum(own_first_grad, axis=0),
            jnp.sum(mid_grad * mid_unit, axis=0),
            jnp.sum(mid_grad, axis=0),
            jnp.sum(own_branch.astype(jnp.float32), axis=0),
            jnp.sum(own_grad, axis=0),
        ]
    )
    summed = (
        lax.psum(qkv_grad.astype(jnp.bfloat16), "dp").astype(jnp.float32),
        lax.psum(proj_grad.astype(jnp.bfloat16), "dp").astype(jnp.float32),
        lax.psum(up_grad.astype(jnp.bfloat16), "dp").astype(jnp.float32),
        lax.psum(down_grad.astype(jnp.bfloat16), "dp").astype(jnp.float32),
        lax.psum(qv_bias_grad.astype(jnp.bfloat16), "dp").astype(jnp.float32),
        lax.psum(up_bias_grad.astype(jnp.bfloat16), "dp").astype(jnp.float32),
        lax.psum(vec_grad.astype(jnp.bfloat16), "dp").astype(jnp.float32),
    )
    split_square = jnp.float32(0.0)
    for gradient in summed[:6]:
        split_square = split_square + jnp.sum(gradient * gradient)
    vec_total, split_total = lax.psum((summed[6], split_square), "mp")
    grad_norm = jnp.sqrt(split_total + jnp.sum(vec_total * vec_total))
    factor = jnp.minimum(1.0, CLIP_NORM / (grad_norm + 1e-06))
    qkv_new, qkv_first, qkv_second = adam_update(
        w_qkv, summed[0] * factor, first_qkv, second_qkv, MATRIX_RATE, DECAY_RATE
    )
    proj_new, proj_first, proj_second = adam_update(
        w_proj, summed[1] * factor, first_proj, second_proj, MATRIX_RATE, DECAY_RATE
    )
    up_new, up_first, up_second = adam_update(
        w_up, summed[2] * factor, first_up, second_up, MATRIX_RATE, DECAY_RATE
    )
    down_new, down_first, down_second = adam_update(
        w_down, summed[3] * factor, first_down, second_down, MATRIX_RATE, DECAY_RATE
    )
    qvb_new, qvb_first, qvb_second = adam_update(
        qv_bias, summed[4] * factor, first_qv_bias, second_qv_bias, VECTOR_RATE, 0.0
    )
    upb_new, upb_first, upb_second = adam_update(
        up_bias, summed[5] * factor, first_up_bias, second_up_bias, VECTOR_RATE, 0.0
    )
    vec_new, vec_first, vec_second = adam_update(
        vec_params, vec_total * factor, first_vec, second_vec, VECTOR_RATE, 0.0
    )
    return (
        activations,
        input_grad,
        grad_norm,
        qkv_new,
        qkv_first,
        qkv_second,
        proj_new,
        proj_first,
        proj_second,
        up_new,
        up_first,
        up_second,
        down_new,
        down_first,
        down_second,
        qvb_new,
        qvb_first,
        qvb_second,
        upb_new,
        upb_first,
        upb_second,
        vec_new,
        vec_first,
        vec_second,
    )


def solution(mesh):
    return jax.shard_map(
        local,
        mesh=mesh,
        in_specs=(
            P(("dp", "mp"), None),
            P(("dp", "mp"), None),
            P("dp"),
            P(None, None, "mp"),
            P("mp", None),
            P(None, "mp"),
            P("mp", None),
            P(None, "mp"),
            P("mp"),
            P(),
            P(None, None, "mp"),
            P(None, None, "mp"),
            P("mp", None),
            P("mp", None),
            P(None, "mp"),
            P(None, "mp"),
            P("mp", None),
            P("mp", None),
            P(None, "mp"),
            P(None, "mp"),
            P("mp"),
            P("mp"),
            P(),
            P(),
        ),
        out_specs=(
            P(("dp", "mp"), None),
            P(("dp", "mp"), None),
            P(),
            P(None, None, "mp"),
            P(None, None, "mp"),
            P(None, None, "mp"),
            P("mp", None),
            P("mp", None),
            P("mp", None),
            P(None, "mp"),
            P(None, "mp"),
            P(None, "mp"),
            P("mp", None),
            P("mp", None),
            P("mp", None),
            P(None, "mp"),
            P(None, "mp"),
            P(None, "mp"),
            P("mp"),
            P("mp"),
            P("mp"),
            P(),
            P(),
            P(),
        ),
        check_vma=False,
    )
```

profile of v0, /device:TPU:1, one launch (start us, length us, event | category | flops | bytes accessed | tf_op | source)
XLA Modules:
  0.0 943.1 jit_solution(12365071723800339372)
XLA Ops:
  11.1 39.6 %all-gather.3.cloned.1.call-done = bf16[2560,512]{1,0:T(8,128)(2,1)} async-done(((bf16[1280,512]{1,0:T(8,128)(2,1)}), bf16[2560,512]{1,0:T(8,128)(2,1)}) %all-gather.3.cloned.1.call-update) | async-done | bytes 2621456 | tf_op jit(solution)/shard_map/all_gather | solution.py:143
  63.6 4.1 squeeze.10
  70.1 4.1 squeeze.11
  76.6 4.1 squeeze.9
  80.7 20.5 %fusion.2 = (f32[5,8,512]{2,1,0:T(8,128)S(1)}, f32[5,8,512,512]{2,3,1,0:T(8,128)}) fusion(pred[5,512]{1,0:T(8,128)(4,1)S(1)} %iota_compare_fusion, bf16[5,512,8,32]{1,0,3,2:T(8,128)(2,1)} %squeeze.11, bf16[5,512,8,32]{1,0,3,2:T(8,128)(2,1)} %squeeze.10), kind=kOutput, calls=%fused_computation.7 | convolution fusion | flops 702525440 | bytes 44648960 | tf_op jit(solution)/shard_map/sqhe,skhe->shqk/dot_general | solution.py:46
  101.1 17.9 %exponential_reduce_fusion = f32[5,8,512]{2,1,0:T(8,128)S(1)} fusion(f32[5,8,512,512]{2,3,1,0:T(8,128)} %get-tuple-element.135, f32[5,8,512]{2,1,0:T(8,128)S(1)} %get-tuple-element.134, pred[5,512]{1,0:T(8,128)(4,1)S(1)} %iota_compare_fusion), kind=kLoop, calls=%fused_computation.5 | loop fusion | flops 41922560 | bytes 42109440 | tf_op jit(solution)/shard_map/reduce_sum | solution.py:156
  119.1 19.3 %fusion.64 = bf16[5,512,8,32]{1,3,2,0:T(8,128)(2,1)} fusion(bf16[5,512,8,32]{1,0,3,2:T(8,128)(2,1)} %squeeze.9, f32[5,8,512,512]{2,3,1,0:T(8,128)} %get-tuple-element.135, f32[5,8,512]{2,1,0:T(8,128)S(1)} %log_add_fusion, pred[5,512]{1,0:T(8,128)(4,1)S(1)} %iota_compare_fusion), kind=kOutput, calls=%fused_computation.103 | convolution fusion | flops 713687040 | bytes 44648960 | tf_op jit(solution)/shard_map/shqk,skhe->sqhe/dot_general | solution.py:158
  146.3 129.9 %all-reduce.9.cloned.1.call-done = f32[2560,512]{1,0:T(8,128)} async-done(((f32[2560,512]{1,0:T(8,128)}), f32[2560,512]{1,0:T(8,128)}) %all-reduce.9.cloned.1.call-update) | async-done | bytes 5242896 | tf_op jit(solution)/shard_map/psum | solution.py:163
  284.5 26.6 %multiply_convert_fusion = (bf16[2560,1024]{1,0:T(8,128)(2,1)}, f32[2560,1024]{1,0:T(8,128)}, f32[2560,1024]{1,0:T(8,128)}) fusion(f32[1024]{0:T(1024)S(1)} %copy-done.48, f32[512,1024]{1,0:T(8,128)S(1)} %copy-done.29, f32[2560,512]{1,0:T(8,128)S(1)} %subtract_multiply_fusion, f32[512]{0:T(512)S(1)} %bitcast.72, f32[512]{0:T(512)S(1)} %bitcast.61), kind=kOutput, calls=%fused_computation.24 | convolution fusion | flops 2861826048 | bytes 33562624 | tf_op jit(solution)/shard_map/dot_general | solution.py:166
  311.0 5.8 all-gather.5.cloned.1.call-done
  316.9 12.5 %fusion.149 = (bf16[1024]{0:T(1024)(128)(2,1)}, bf16[2560,1024]{1,0:T(8,128)(2,1)S(1)}) fusion(f32[2560,1024]{1,0:T(8,128)} %get-tuple-element.113, bf16[2560,512]{1,0:T(8,128)(2,1)} %all-gather.5.cloned.1.call-done, f32[1024,512]{1,0:T(8,128)S(1)} %copy-done.25, f32[2560,1024]{1,0:T(8,128)} %get-tuple-element.136, f32[1024]{0:T(1024)S(1)} %copy-done.48), kind=kOutput, calls=%fused_computation.190 | convolution fusion | flops 2726820864 | bytes 30939136 | tf_op jit(solution)/shard_map/dot_general | solution.py:86
  331.8 4.4 convolution_convert_fusion
  336.3 7.3 convolution_convert_fusion.5
  343.6 6.4 convolution_convert_fusion.6
  350.0 60.7 %all-reduce.11.cloned.1.call-done = bf16[2560,512]{1,0:T(8,128)(2,1)} async-done(((bf16[2560,512]{1,0:T(8,128)(2,1)}), bf16[2560,512]{1,0:T(8,128)(2,1)}) %all-reduce.11.cloned.1.call-update) | async-done | bytes 2621456 | tf_op jit(solution)/shard_map/psum | solution.py:181
  410.7 5.3 multiply_reduce_fusion.4
  416.0 6.5 fusion.142
  427.3 16.6 %fusion.65 = bf16[5,512,8,32]{1,3,2,0:T(8,128)(2,1)S(1)} fusion(bf16[5,512,8,32]{1,0,3,2:T(8,128)(2,1)S(1)} %reshape.145, f32[5,8,512,512]{2,3,1,0:T(8,128)} %get-tuple-element.135, f32[5,8,512]{2,1,0:T(8,128)S(1)} %log_add_fusion, pred[5,512]{1,0:T(8,128)(4,1)S(1)} %iota_compare_fusion), kind=kOutput, calls=%fused_computation.104 | convolution fusion | flops 713687040 | bytes 44648960 | tf_op jit(solution)/shard_map/shqk,sqhe->skhe/dot_general | solution.py:69
  443.9 16.2 %fusion.75 = f32[5,8,512,512]{2,3,1,0:T(8,128)} fusion(bf16[5,512,8,32]{1,0,3,2:T(8,128)(2,1)S(1)} %reshape.145, bf16[5,512,8,32]{1,0,3,2:T(8,128)(2,1)S(1)} %copy-done.13), kind=kOutput, calls=%fused_computation.114 | convolution fusion | flops 671088640 | bytes 44564480 | tf_op jit(solution)/shard_map/sqhe,skhe->shqk/dot_general | solution.py:57
  460.1 54.0 %fusion.69 = bf16[5,512,8,32]{1,3,2,0:T(8,128)(2,1)} fusion(f32[5,8,512,512]{2,3,1,0:T(8,128)} %fusion.75, f32[5,8,512,512]{2,3,1,0:T(8,128)} %get-tuple-element.135, f32[5,8,512]{2,1,0:T(8,128)S(1)} %log_add_fusion, pred[5,512]{1,0:T(8,128)(4,1)S(1)} %iota_compare_fusion, bf16[5,512,8,32]{1,0,3,2:T(8,128)(2,1)} %squeeze.11), kind=kOutput, calls=%fused_computation.106 | convolution fusion | flops 797594112 | bytes 86592000 | tf_op jit(solution)/shard_map/shqk,skhe->sqhe/dot_general | solution.py:65
  514.1 53.4 %fusion.66 = bf16[5,512,8,32]{1,3,2,0:T(8,128)(2,1)} fusion(f32[5,8,512,512]{2,3,1,0:T(8,128)} %fusion.75, f32[5,8,512,512]{2,3,1,0:T(8,128)} %get-tuple-element.135, f32[5,8,512]{2,1,0:T(8,128)S(1)} %log_add_fusion, pred[5,512]{1,0:T(8,128)(4,1)S(1)} %iota_compare_fusion, bf16[5,512,8,32]{1,0,3,2:T(8,128)(2,1)S(1)} %copy-done.9), kind=kOutput, calls=%fused_computation.105 | convolution fusion | flops 797594112 | bytes 86592000 | tf_op jit(solution)/shard_map/shqk,sqhe->skhe/dot_general | solution.py:68
  580.3 4.1 stack.48
  587.0 5.6 fusion.73
  592.7 7.7 convolution_convert_fusion.1
  622.1 73.2 %all-reduce.13.cloned.1.call-done = (bf16[3,512,256]{1,2,0:T(8,128)(2,1)}, bf16[256,512]{1,0:T(8,128)(2,1)}, bf16[512,1024]{1,0:T(8,128)(2,1)}, bf16[1024,512]{1,0:T(8,128)(2,1)}) async-done(((bf16[3,512,256]{1,2,0:T(8,128)(2,1)}, bf16[256,512]{1,0:T(8,128)(2,1)}, bf16[512,1024]{1,0:T(8,128)(2,1)}, bf16[1024,512]{1,0:T(8,128)(2,1)}), (bf16[3,512,256]{1,2,0:T(8,128)(2,1)}, bf16[256,512]{1,0:T(8,128)(2,1)}, ...) | async-done | bytes 3145744 | tf_op jit(solution)/shard_map/psum | solution.py:221
  706.8 122.6 %all-reduce.15.cloned.1.call-done = (bf16[2560,512]{1,0:T(8,128)(2,1)}, bf16[2560,512]{1,0:T(8,128)(2,1)}) async-done(((bf16[2560,512]{1,0:T(8,128)(2,1)}, bf16[2560,512]{1,0:T(8,128)(2,1)}), (bf16[2560,512]{1,0:T(8,128)(2,1)}, bf16[2560,512]{1,0:T(8,128)(2,1)})) %all-reduce.15.cloned.1.call-update) | async-done | bytes 5242896 | tf_op jit(solution)/shard_map/psum | solution.py:205
  837.2 56.9 %all-reduce.1 = (bf16[6,512]{1,0:T(8,128)(2,1)S(1)}, bf16[2,256]{1,0:T(2,128)(2,1)S(1)}, bf16[1024]{0:T(1024)(128)(2,1)S(1)}) all-reduce(bf16[6,512]{1,0:T(8,128)(2,1)S(1)} %stack.59, bf16[2,256]{1,0:T(2,128)(2,1)S(1)} %pad_maximum_fusion.2, bf16[1024]{0:T(1024)(128)(2,1)S(1)} %copy-done.56), channel_id=1, replica_groups=mesh['dp'=16,'mp'=2] {'dp'}, use_global_device_ids=true, to_apply=%region_36.37 | all-reduce | flops 4608 | bytes 18432 | tf_op jit(solution)/shard_map/psum | solution.py:227
  896.5 5.8 all-reduce
  904.4 4.7 multiply_subtract_fusion.2
  917.0 3.8 fusion.45
  925.4 4.0 multiply_subtract_fusion
  930.8 3.9 multiply_subtract_fusion.1
  (214 shorter events, 114.1 us)
Async XLA Ops:
  7.2 43.5 %all-gather.3.cloned.1.call-start = ((), (), s32[]{:S(2)}) async-start(), calls=%async_computation | async-start | bytes 3932160 | tf_op jit(solution)/shard_map/all_gather | solution.py:143
  7.9 268.3 %all-reduce.9.cloned.1.call-start = ((), (), s32[]{:S(2)}) async-start(), calls=%async_computation.1 | async-start | bytes 10485760 | tf_op jit(solution)/shard_map/psum | solution.py:163
  11.1 48.0 %copy-start.45 = (f32[1,512]{1,0:T(1,128)}, f32[1,512]{1,0:T(1,128)S(1)}, u32[]{:S(2)}) copy-start(f32[1,512]{1,0:T(1,128)S(1)} %get-tuple-element.128) | copy-start | bytes 6148
  11.1 48.0 %copy-start.54 = (f32[1,512]{1,0:T(1,128)}, f32[1,512]{1,0:T(1,128)S(1)}, u32[]{:S(2)}) copy-start(f32[1,512]{1,0:T(1,128)S(1)} %get-tuple-element.127) | copy-start | bytes 6148
  145.5 171.4 %all-gather.5.cloned.1.call-start = ((), (), s32[]{:S(2)}) async-start(), calls=%async_computation.2 | async-start | bytes 3932160 | tf_op jit(solution)/shard_map/all_gather | solution.py:144
  146.2 264.4 %all-reduce.11.cloned.1.call-start = ((), (), s32[]{:S(2)}) async-start(), calls=%async_computation.3 | async-start | bytes 5242880 | tf_op jit(solution)/shard_map/psum | solution.py:181
  284.5 32.4 %copy-start.25 = (f32[1024,512]{1,0:T(8,128)S(1)}, f32[1024,512]{1,0:T(8,128)}, u32[]{:S(2)}) copy-start(f32[1024,512]{1,0:T(8,128)} %param.30) | copy-start | bytes 6291460
  316.9 14.9 %copy-start.30 = (f32[512,1024]{1,0:T(8,128)S(1)}, f32[512,1024]{1,0:T(8,128)}, u32[]{:S(2)}) copy-start(f32[512,1024]{1,0:T(8,128)} %param.29) | copy-start | bytes 6291460
  336.2 359.2 %all-reduce.13.cloned.1.call-start = ((), (), s32[]{:S(2)}) async-start(), calls=%async_computation.4 | async-start | bytes 6291456 | tf_op jit(solution)/shard_map/psum | solution.py:221
  350.0 66.1 %copy-start.24 = (bf16[2560,512]{1,0:T(8,128)(2,1)S(1)}, bf16[2560,512]{1,0:T(8,128)(2,1)}, u32[]{:S(2)}) copy-start(bf16[2560,512]{1,0:T(8,128)(2,1)} %all-gather.5.cloned.1.call-done) | copy-start | bytes 7864324
  427.3 16.6 %copy-start.13 = (bf16[5,512,8,32]{1,0,3,2:T(8,128)(2,1)S(1)}, bf16[5,512,8,32]{1,0,3,2:T(8,128)(2,1)}, u32[]{:S(2)}) copy-start(bf16[5,512,8,32]{1,0,3,2:T(8,128)(2,1)} %squeeze.9) | copy-start | bytes 3932164
  460.1 54.0 %copy-start.9 = (bf16[5,512,8,32]{1,0,3,2:T(8,128)(2,1)S(1)}, bf16[5,512,8,32]{1,0,3,2:T(8,128)(2,1)}, u32[]{:S(2)}) copy-start(bf16[5,512,8,32]{1,0,3,2:T(8,128)(2,1)} %squeeze.10) | copy-start | bytes 3932164
  576.6 10.4 %copy-start.2 = (bf16[2560,512]{1,0:T(8,128)(2,1)S(1)}, bf16[2560,512]{1,0:T(8,128)(2,1)}, u32[]{:S(2)}) copy-start(bf16[2560,512]{1,0:T(8,128)(2,1)} %all-gather.3.cloned.1.call-done) | copy-start | bytes 7864324
  576.6 10.4 %copy-start.38 = (f32[2560]{0:T(1024)S(1)}, f32[2560]{0:T(1024)}, u32[]{:S(2)}) copy-start(f32[2560]{0:T(1024)} %copy-done.37) | copy-start | bytes 30724
  576.6 10.4 %copy-start.40 = (f32[2560]{0:T(1024)S(1)}, f32[2560]{0:T(1024)}, u32[]{:S(2)}) copy-start(f32[2560]{0:T(1024)} %copy-done.39) | copy-start | bytes 30724
  576.6 10.4 %copy-start.46 = (f32[1,512]{1,0:T(1,128)S(1)}, f32[1,512]{1,0:T(1,128)}, u32[]{:S(2)}) copy-start(f32[1,512]{1,0:T(1,128)} %copy-done.45) | copy-start | bytes 6148
  576.6 10.4 %copy-start.55 = (f32[1,512]{1,0:T(1,128)S(1)}, f32[1,512]{1,0:T(1,128)}, u32[]{:S(2)}) copy-start(f32[1,512]{1,0:T(1,128)} %copy-done.54) | copy-start | bytes 6148
  592.6 236.8 %all-reduce.15.cloned.1.call-start = ((), (), s32[]{:S(2)}) async-start(), calls=%async_computation.5 | async-start | bytes 10485760 | tf_op jit(solution)/shard_map/psum | solution.py:205
  834.8 69.6 %copy-start.10 = (f32[3,512,256]{1,2,0:T(8,128)S(1)}, f32[3,512,256]{1,2,0:T(8,128)}, u32[]{:S(2)}) copy-start(f32[3,512,256]{1,2,0:T(8,128)} %copy.95) | copy-start | bytes 4718596
  834.8 69.6 %copy-start.11 = (f32[3,512,256]{1,2,0:T(8,128)S(1)}, f32[3,512,256]{1,2,0:T(8,128)}, u32[]{:S(2)}) copy-start(f32[3,512,256]{1,2,0:T(8,128)} %copy.92) | copy-start | bytes 4718596
  912.2 8.6 copy-start.47
  912.2 8.6 copy-start.52
  912.2 8.6 copy-start.53
  912.2 9.2 copy-start.49
  912.2 9.2 copy-start.50
  912.2 9.2 copy-start.51
  912.3 9.8 %copy-start.41 = (f32[6,512]{1,0:T(8,128)S(1)}, f32[6,512]{1,0:T(8,128)}, u32[]{:S(2)}) copy-start(f32[6,512]{1,0:T(8,128)} %param.33) | copy-start | bytes 36868
  912.3 9.8 %copy-start.42 = (f32[6,512]{1,0:T(8,128)S(1)}, f32[6,512]{1,0:T(8,128)}, u32[]{:S(2)}) copy-start(f32[6,512]{1,0:T(8,128)} %param.46) | copy-start | bytes 36868
  912.3 9.8 %copy-start.43 = (f32[6,512]{1,0:T(8,128)S(1)}, f32[6,512]{1,0:T(8,128)}, u32[]{:S(2)}) copy-start(f32[6,512]{1,0:T(8,128)} %param.47) | copy-start | bytes 36868
  912.3 10.4 %copy-start.21 = (f32[256,512]{1,0:T(8,128)S(1)}, f32[256,512]{1,0:T(8,128)}, u32[]{:S(2)}) copy-start(f32[256,512]{1,0:T(8,128)} %param.28) | copy-start | bytes 1572868
  912.3 10.4 %copy-start.36 = (bf16[256,512]{1,0:T(8,128)(2,1)S(1)}, bf16[256,512]{1,0:T(8,128)(2,1)}, u32[]{:S(2)}) copy-start(bf16[256,512]{1,0:T(8,128)(2,1)} %get-tuple-element.86) | copy-start | bytes 786436
  915.4 9.9 %copy-start.23 = (bf16[1024,512]{1,0:T(8,128)(2,1)S(1)}, bf16[1024,512]{1,0:T(8,128)(2,1)}, u32[]{:S(2)}) copy-start(bf16[1024,512]{1,0:T(8,128)(2,1)} %get-tuple-element.88) | copy-start | bytes 3145732
  (36 other events, 184.2 us)
Sparse Core Ops, SparseCore 0:
  9.6 41.0 all-gather.2
  145.6 130.5 all-reduce.8
  277.8 39.0 all-gather.4
  336.3 74.3 all-reduce.10
  592.7 102.5 all-reduce.12
  698.3 131.0 all-reduce.14
where the time goes:
time: 961 us; the launch traced here: 943 us
  waiting for transfers between devices  433 us (45%)
  matrix products  263 us (27%)
  other arithmetic  89.4 us (9%)
  local copies, waits for them, and re-layouts  73.1 us (8%)
  blocking collectives  62.7 us (7%)
  between operations  21.8 us (2%)
    psum x1, waiting for transfers between devices, local(): resid_all = whole_rows + lax.psum(proj_part, 'mp') + proj_shift  130 us
    psum x1, waiting for transfers between devices, local(): lax.psum(first_part.astype(jnp.bfloat16), 'mp').astype(jnp.float32)  123 us
    psum x1, waiting for transfers between devices, local(): lax.psum(qkv_grad.astype(jnp.bfloat16), 'dp').astype(jnp.float32)  73.2 us
    psum x1, waiting for transfers between devices, local(): lax.psum(mid_part.astype(jnp.bfloat16), 'mp').astype(jnp.float32)  60.7 us
    psum x1, blocking collectives, local(): lax.psum(vec_grad.astype(jnp.bfloat16), 'dp').astype(jnp.float32)  56.9 us
    dot_general x1, matrix products, attend_backward(): jnp.einsum('shqk,skhe->sqhe', raw_grad, key_rows, preferred_element_type=...  54 us
    dot_general x1, matrix products, attend_backward(): jnp.einsum('shqk,sqhe->skhe', raw_grad, queries, preferred_element_type=j...  53.4 us
    all_gather x1, waiting for transfers between devices, local(): lax.all_gather(patches, 'mp', axis=0, tiled=True)  39.6 us
  transfers between devices with their start and end apart: 6, of which 6 were waited for; matrix products, arithmetic and copies ran while one was open for 9% of the time, Pallas kernels for 0%

commit v1 on v0

--- a/solution.py
+++ b/solution.py
@@ -1,6 +1,8 @@
 import jax
 import jax.numpy as jnp
 from jax import lax
+from jax.experimental import pallas as pl
+from jax.experimental.pallas import tpu as pltpu
 from jax.sharding import PartitionSpec as P
 
 HD = 32
@@ -16,6 +18,56 @@
 VECTOR_RATE = 0.8
 CLIP_NORM = 1.0
 MASK_FILL = -1e30
+LOG2E = 1.4426950408889634
+BF = jnp.bfloat16
+F32 = jnp.float32
+MESH = pl.DeviceIdType.MESH
+SEQ = 512
+HALF = 256
+VMEM_LIMIT = 58 * 1024 * 1024
+
+
+def mm_nn(left, right):
+    return lax.dot_general(left, right, (((1,), (0,)), ((), ())), preferred_element_type=F32)
+
+
+def mm_nt(left, right):
+    return lax.dot_general(left, right, (((1,), (1,)), ((), ())), preferred_element_type=F32)
+
+
+def mm_tn(left, right):
+    return lax.dot_general(left, right, (((0,), (0,)), ((), ())), preferred_element_type=F32)
+
+
+def partners(dp):
+    core = dp + 1 - 2 * lax.rem(dp, 2)
+    x_side = dp + 2 - 4 * lax.rem(lax.div(dp, 2), 2)
+    z_near = dp + 4 - 8 * lax.rem(lax.div(dp, 4), 2)
+    z_far = dp + 8 - 16 * lax.rem(lax.div(dp, 8), 2)
+    return core, x_side, z_near, z_far
+
+
+def greet(targets):
+    barrier = pltpu.get_barrier_semaphore()
+    for target in targets:
+        pl.semaphore_signal(barrier, inc=1, device_id=target, device_id_type=MESH)
+    pl.semaphore_wait(barrier, len(targets))
+
+
+def full_spec(shape):
+    return pl.BlockSpec(shape, lambda *_: (0,) * len(shape))
+
+
+def sds(shape, dtype):
+    return jax.ShapeDtypeStruct(shape, dtype)
+
+
+def row_block(index, mp):
+    return pl.multiple_of(lax.rem(index + 4 * (1 - mp), 5) * HALF, HALF)
+
+
+def ext_cols(index):
+    return pl.multiple_of(jnp.where(index == 0, 0, HALF + HALF * index), HALF)
 
 
 def norm_forward(values, norm_gain, norm_shift):
@@ -281,11 +333,687 @@
     )
 
 
-def solution(mesh):
-    return jax.shard_map(
-        local,
-        mesh=mesh,
-        in_specs=(
+def gather_kernel(
+    qkv_ref, proj_ref, up_ref, down_ref, small_ref, rows_ref,
+    wt_ref, wp_ref, wu_ref, wd_ref, sm_ref, other_ref,
+    send_sem, recv_sem,
+):
+    dp, mp = lax.axis_index("dp"), lax.axis_index("mp")
+    peer = 1 - mp
+    core, x_side, _, _ = partners(dp)
+    quarter = lax.rem(dp, 4)
+    x_quarter = lax.rem(quarter + 2, 4)
+    greet([{"mp": peer}, {"dp": core}, {"dp": x_side}])
+
+    full = [wt_ref, wp_ref, wu_ref, wd_ref]
+
+    def piece(ref, side, part):
+        rows = ref.shape[-2] // 4
+        where = pl.ds(pl.multiple_of(part * rows, rows), rows)
+        return ref.at[side, :, where, :] if len(ref.shape) == 4 else ref.at[side, where, :]
+
+    def send(src, dst, index, target):
+        copy = pltpu.make_async_remote_copy(
+            src_ref=src, dst_ref=dst, send_sem=send_sem.at[index], recv_sem=recv_sem.at[index],
+            device_id=target, device_id_type=MESH,
+        )
+        copy.start()
+        return copy
+
+    copies = []
+    own = pl.multiple_of((1 - mp) * 4 * HALF, HALF)
+    copies.append(send(rows_ref.at[pl.ds(own, HALF), :], other_ref, 0, {"mp": peer}))
+    sm_ref[mp] = small_ref[...]
+    copies.append(send(sm_ref.at[mp], sm_ref.at[mp], 1, {"mp": peer}))
+    first = []
+    for index in range(4):
+        if index == 0:
+            for part in range(3):
+                wt_ref[mp, part] = qkv_ref[part].T.astype(BF)
+        else:
+            full[index][mp] = (None, proj_ref, up_ref, down_ref)[index][...].astype(BF)
+        src = piece(full[index], mp, quarter)
+        first.append(send(src, src, 2 + index, {"mp": peer}))
+    second, third = [], []
+    for index in range(4):
+        first[index].wait_recv()
+        src = piece(full[index], peer, quarter)
+        second.append(send(src, src, 6 + index, {"dp": x_side}))
+        third.append(send(src, src, 10 + index, {"dp": core}))
+    for index in range(4):
+        second[index].wait_recv()
+        src = piece(full[index], peer, x_quarter)
+        third.append(send(src, src, 14 + index, {"dp": core}))
+    for copy in copies + third:
+        copy.wait_recv()
+    for copy in copies + first + second + third:
+        copy.wait_send()
+
+
+def gather_weights(w_qkv, w_proj, w_up, w_down, small, patches):
+    vmem = pl.BlockSpec(memory_space=pltpu.VMEM)
+    return pl.pallas_call(
+        gather_kernel,
+        out_shape=[
+            sds((2, 3, 256, 512), BF), sds((2, 256, 512), BF), sds((2, 512, 1024), BF),
+            sds((2, 1024, 512), BF), sds((2, 8, 1024), F32), sds((HALF, 512), BF),
+        ],
+        in_specs=[vmem] * 6,
+        out_specs=[vmem] * 6,
+        scratch_shapes=[pltpu.SemaphoreType.DMA((18,)), pltpu.SemaphoreType.DMA((18,))],
+        compiler_params=pltpu.CompilerParams(
+            collective_id=0, has_side_effects=True, vmem_limit_bytes=VMEM_LIMIT
+        ),
+        name="gather_weights",
+    )(w_qkv, w_proj, w_up, w_down, small, patches)
+
+
+def layer_norm_rows(rows, gain, shift):
+    centred = rows - jnp.mean(rows, axis=-1, keepdims=True)
+    inverse = lax.rsqrt(jnp.mean(centred * centred, axis=-1, keepdims=True) + NORM_EPS)
+    unit = centred * inverse
+    return unit * gain + shift, unit, inverse
+
+
+def layer_norm_back(grad, unit, inverse, gain):
+    scaled = grad * gain
+    centre = jnp.mean(scaled, axis=-1, keepdims=True)
+    slope = jnp.mean(scaled * unit, axis=-1, keepdims=True)
+    return inverse * (scaled - centre - unit * slope)
+
+
+def head_rows(block, sub):
+    return pl.ds(pl.multiple_of(block * 128 + sub * HD, HD), HD)
+
+
+def head_cols(block):
+    return pl.ds(pl.multiple_of(block * 128, 128), 128)
+
+
+def key_bias(shape, mp, count, shared):
+    slot = lax.broadcasted_iota(jnp.int32, shape, 0)
+    if shared:
+        slot = lax.rem(slot + HALF * mp, SEQ)
+    return jnp.where(slot < count, 0.0, MASK_FILL).astype(BF)
+
+
+def widen(rows, sub):
+    zeros = jnp.zeros_like(rows)
+    row = lax.broadcasted_iota(jnp.int32, rows.shape, 0)
+    ones = jnp.where(row == 0, 1.0, 0.0).astype(BF)
+    parts = [zeros] * 4
+    parts[sub] = rows
+    parts[(sub + 1) % 4] = ones
+    return jnp.concatenate(parts, axis=0)
+
+
+def widen_plain(rows, sub):
+    parts = [jnp.zeros_like(rows)] * 4
+    parts[sub] = rows
+    return jnp.concatenate(parts, axis=0)
+
+
+def score_tile(key_block, bias, query_rows, sub):
+    lane = lax.broadcasted_iota(jnp.int32, key_block.shape, 1)
+    keys = jnp.where(lane // HD == (sub + 1) % 4, bias, key_block)
+    return mm_nn(keys, widen(query_rows, sub))
+
+
+def attend_kernel(
+    count_ref, x_ref, other_ref, wt_ref, vec_ref, small_ref,
+    nt_ref, qt_ref, kt_ref, k_ref, v_ref, ot_ref, lse_ref,
+    vt_ref, bias_ref, s_ref,
+):
+    group = pl.program_id(0)
+    mp = lax.axis_index("mp")
+    gain, shift = vec_ref[0:1, :], vec_ref[1:2, :]
+
+    def as_column(row):
+        return jnp.broadcast_to(row, (8, row.shape[1])).T[:, 0:1]
+
+    def project(norm, base):
+        width = norm.shape[0]
+        at = slice(base, base + width)
+        nt_ref[:, at] = norm.T
+        for side in range(2):
+            own = slice(side * 256, side * 256 + 256)
+            q_bias, v_bias = small_ref[side, 1:2, 0:256], small_ref[side, 2:3, 0:256]
+            scale = LOG2E * HD ** (-0.5)
+            qt_ref[own, at] = ((mm_nt(wt_ref[side, 0], norm) + as_column(q_bias)) * scale).astype(BF)
+            kt_ref[own, at] = mm_nt(wt_ref[side, 1], norm).astype(BF)
+            vt_ref[own, at] = (mm_nt(wt_ref[side, 2], norm) + as_column(v_bias)).astype(BF)
+            k_ref[at, own] = mm_nt(norm, wt_ref[side, 1]).astype(BF)
+            v_ref[at, own] = (mm_nt(norm, wt_ref[side, 2]) + v_bias).astype(BF)
+
+    def norm_of(ref, start):
+        rows = ref[pl.ds(start, HALF), :].astype(F32)
+        return layer_norm_rows(rows, gain, shift)[0].astype(BF)
+
+    def attend(queries):
+        bias = bias_ref[...]
+
+        def scores(block, sub):
+            return score_tile(
+                k_ref[:, head_cols(block)], bias, qt_ref[head_rows(block, sub), :queries], sub
+            )
+
+        s_ref[0, :, :queries] = scores(0, 0)
+
+        def body(block, carry):
+            for sub in range(4):
+                following = (block, sub + 1) if sub < 3 else (lax.rem(block + 1, 4), 0)
+                s_ref[(sub + 1) % 2, :, :queries] = scores(*following)
+                tile = s_ref[sub % 2, :, :queries]
+                top = jnp.max(tile, axis=0, keepdims=True)
+                weights = jnp.exp2(tile - top)
+                rows = head_rows(block, sub)
+                values = jnp.concatenate([vt_ref[rows, :], jnp.ones((16, SEQ), BF)], axis=0)
+                mixed = mm_nn(values, weights.astype(BF))
+                total = mixed[HD : HD + 1]
+                ot_ref[rows, :queries] = (mixed[:HD] * (1.0 / total)).astype(BF)
+                lse_ref[0, block, sub : sub + 1, :queries] = top + jnp.log2(total)
+            return carry
+
+        lax.fori_loop(0, 4, body, 0)
+
+    @pl.when(group == 0)
+    def _():
+        bias_ref[...] = key_bias(bias_ref.shape, mp, count_ref[2], True)
+        project(norm_of(x_ref, row_block(0, mp)), 0)
+        project(norm_of(other_ref, 0), HALF)
+        attend(HALF)
+
+    @pl.when(group > 0)
+    def _():
+        bias_ref[...] = key_bias(bias_ref.shape, mp, count_ref[3 * mp + group - 1], False)
+        for part in range(2):
+            project(norm_of(x_ref, row_block(2 * group - 1 + part, mp)), part * HALF)
+        attend(SEQ)
+
+
+def attend_forward(key_count, patches, other, wt, vec_params, small):
+    tall = pl.BlockSpec((512, SEQ), lambda g: (0, g))
+    wide = pl.BlockSpec((SEQ, 512), lambda g: (g, 0))
+    ext = 3 * SEQ
+    return pl.pallas_call(
+        attend_kernel,
+        grid=(3,),
+        out_shape=[
+            sds((512, ext), BF), sds((512, ext), BF), sds((512, ext), BF), sds((ext, 512), BF),
+            sds((ext, 512), BF), sds((512, ext), BF), sds((3, 4, 8, SEQ), F32),
+        ],
+        in_specs=[
+            pl.BlockSpec(memory_space=pltpu.SMEM), full_spec(patches.shape), full_spec(other.shape),
+            full_spec(wt.shape), full_spec(vec_params.shape), full_spec(small.shape),
+        ],
+        out_specs=[
+            tall, tall, tall, wide, wide, tall,
+            pl.BlockSpec((1, 4, 8, SEQ), lambda g: (g, 0, 0, 0)),
+        ],
+        scratch_shapes=[
+            pltpu.VMEM((512, SEQ), BF), pltpu.VMEM((SEQ, 128), BF), pltpu.VMEM((2, SEQ, SEQ), F32)
+        ],
+        compiler_params=pltpu.CompilerParams(vmem_limit_bytes=VMEM_LIMIT),
+        name="attend_forward",
+    )(key_count, patches, other, wt, vec_params, small)
+
+
+def mlp_kernel(
+    x_ref, dy_ref, ot_ref, wp_ref, wu_ref, wd_ref, vec_ref, small_ref,
+    act_ref, dres_ref, dot_ref, gd_ref, gu_ref, gp_ref, vsum_ref, bsum_ref,
+    res_ref, n2_ref, out_ref, dn_ref, hid_ref, dup_ref, dyc_ref, br_ref,
+):
+    step = pl.program_id(0)
+    mp = lax.axis_index("mp")
+    gain, shift = vec_ref[2:3, :], vec_ref[3:4, :]
+    w_proj = wp_ref[...].reshape(512, 512)
+
+    def rows(index):
+        return pl.ds(pl.multiple_of(index * HALF, HALF), HALF)
+
+    @pl.when(step == 0)
+    def _():
+        def body(index, carry):
+            x_rows = x_ref[pl.ds(row_block(index, mp), HALF), :].astype(F32)
+            mixed = ot_ref[:, pl.ds(ext_cols(index), HALF)]
+            resid = x_rows + mm_tn(mixed, w_proj) + vec_ref[4:5, :]
+            res_ref[rows(index), :] = resid
+            n2_ref[rows(index), :] = layer_norm_rows(resid, gain, shift)[0].astype(BF)
+            out_ref[rows(index), :] = resid + vec_ref[5:6, :]
+            dn_ref[rows(index), :] = jnp.zeros((HALF, 512), F32)
+            dyc_ref[rows(index), :] = dy_ref[pl.ds(row_block(index, mp), HALF), :]
+            return carry
+
+        lax.fori_loop(0, 5, body, 0)
+
+    w_up, w_down = wu_ref[0], wd_ref[0]
+    up_bias = small_ref[step // 2, 0:1, pl.ds(pl.multiple_of(lax.rem(step, 2) * 512, 512), 512)]
+
+    def body(index, total):
+        at = rows(index)
+        up_pre = mm_nn(n2_ref[at, :], w_up) + up_bias
+        cumulative = 0.5 * (1.0 + lax.erf(up_pre * (0.5**0.5)))
+        density = jnp.exp(-0.5 * up_pre * up_pre) * 0.3989422804014327
+        hidden = (up_pre * cumulative).astype(BF)
+        hid_ref[at, :] = hidden
+        out_ref[at, :] += mm_nn(hidden, w_down)
+        slope = cumulative + up_pre * density
+        dup = (mm_nt(dyc_ref[at, :], w_down) * slope).astype(BF)
+        dup_ref[at, :] = dup
+        dn_ref[at, :] += mm_nt(dup, w_up)
+        return total + jnp.sum(dup.astype(F32).reshape(HALF // 8, 8, 512), axis=0)
+
+    total = lax.fori_loop(0, 5, body, jnp.zeros((8, 512), F32))
+    bsum_ref[0] = total
+    gd_ref[0] = mm_tn(hid_ref[...], dyc_ref[...]).astype(BF)
+    gu_ref[0] = mm_tn(n2_ref[...], dup_ref[...]).astype(BF)
+
+    @pl.when(step == 3)
+    def _():
+        vsum_ref[...] = jnp.zeros_like(vsum_ref)
+
+        def body(index, carry):
+            at = rows(index)
+            act_ref[pl.ds(row_block(index, mp), HALF), :] = out_ref[at, :].astype(BF)
+            _, unit, inverse = layer_norm_rows(res_ref[at, :], gain, shift)
+            dn = dn_ref[at, :]
+            dy = dyc_ref[at, :].astype(F32)
+            dres = dy + layer_norm_back(dn, unit, inverse, gain)
+            dres_ref[at, :] = dres
+            branch = dres.astype(BF)
+            br_ref[at, :] = branch
+            dot_ref[:, pl.ds(ext_cols(index), HALF)] = mm_nt(w_proj, branch).astype(BF)
+            sums = [dn * unit, dn, branch.astype(F32), dy]
+            for place, value in enumerate(sums):
+                vsum_ref[place] += jnp.sum(value.reshape(HALF // 8, 8, 512), axis=0)
+            return carry
+
+        lax.fori_loop(0, 5, body, 0)
+        mixed = jnp.concatenate([ot_ref[:, 0:HALF], ot_ref[:, SEQ:]], axis=1)
+        gp_ref[...] = mm_nn(mixed, br_ref[...]).astype(BF).reshape(2, 256, 512)
+
+
+def mlp(patches, cotangent, ot, wp, wu, wd, vec_params, small):
+    rows = patches.shape[0]
+    ext = 3 * SEQ
+    up_spec = pl.BlockSpec((1, 512, 512), lambda f: (f // 2, 0, f % 2))
+    down_spec = pl.BlockSpec((1, 512, 512), lambda f: (f // 2, f % 2, 0))
+    return pl.pallas_call(
+        mlp_kernel,
+        grid=(4,),
+        out_shape=[
+            sds((rows, 512), BF), sds((rows, 512), F32), sds((512, ext), BF), sds((2, 1024, 512), BF),
+            sds((2, 512, 1024), BF), sds((2, 256, 512), BF), sds((4, 8, 512), F32), sds((4, 8, 512), F32),
+        ],
+        in_specs=[
+            full_spec((rows, 512)), full_spec((rows, 512)), full_spec((512, ext)), full_spec(wp.shape),
+            up_spec, down_spec, full_spec(vec_params.shape), full_spec(small.shape),
+        ],
+        out_specs=[
+            full_spec((rows, 512)), full_spec((rows, 512)), full_spec((512, ext)), down_spec, up_spec,
+            full_spec((2, 256, 512)), full_spec((4, 8, 512)), pl.BlockSpec((1, 8, 512), lambda f: (f, 0, 0)),
+        ],
+        scratch_shapes=[
+            pltpu.VMEM((rows, 512), F32), pltpu.VMEM((rows, 512), BF), pltpu.VMEM((rows, 512), F32),
+            pltpu.VMEM((rows, 512), F32), pltpu.VMEM((rows, 512), BF), pltpu.VMEM((rows, 512), BF),
+            pltpu.VMEM((rows, 512), BF), pltpu.VMEM((rows, 512), BF),
+        ],
+        compiler_params=pltpu.CompilerParams(vmem_limit_bytes=VMEM_LIMIT),
+        name="mlp",
+    )(patches, cotangent, ot, wp, wu, wd, vec_params, small)
+
+
+def attend_back_kernel(
+    count_ref, qt_ref, kt_ref, dot_ref, ot_ref, k_ref, v_ref, lse_ref, nt_ref, wt_ref,
+    g_ref, dn_ref, far_ref, bsum_ref,
+    grads_ref, acc_ref, bias_ref, s_ref, dp_ref,
+):
+    step = pl.program_id(0)
+    mp = lax.axis_index("mp")
+
+    @pl.when(step == 0)
+    def _():
+        acc_ref[...] = jnp.zeros_like(acc_ref)
+        grads_ref[0:128, HALF:SEQ] = jnp.zeros((128, HALF), BF)
+        bias_ref[0] = key_bias((SEQ, 128), mp, count_ref[2], True)
+        for group in (1, 2):
+            bias_ref[group] = key_bias((SEQ, 128), mp, count_ref[3 * mp + group - 1], False)
+
+    def heads(group, queries):
+        base = pl.multiple_of(group * SEQ, SEQ)
+        keys_at, queries_at = pl.ds(base, SEQ), pl.ds(base, queries)
+        bias = bias_ref[group]
+
+        def tiles(sub):
+            own = slice(sub * HD, sub * HD + HD)
+            s_ref[sub % 2, :, :queries] = score_tile(
+                k_ref[keys_at, :], bias, qt_ref[own, queries_at], sub
+            )
+            dp_ref[sub % 2, :, :queries] = mm_nn(
+                v_ref[keys_at, :], widen_plain(dot_ref[own, queries_at], sub)
+            )
+
+        tiles(0)
+        for sub in range(4):
+            if sub < 3:
+                tiles(sub + 1)
+            own = slice(sub * HD, sub * HD + HD)
+            q_rows, do_rows = qt_ref[own, queries_at], dot_ref[own, queries_at]
+            delta = jnp.sum(
+                do_rows.astype(F32) * ot_ref[own, queries_at].astype(F32), axis=0, keepdims=True
+            )
+            probs = jnp.exp2(s_ref[sub % 2, :, :queries] - lse_ref[group, 0, sub : sub + 1, :queries])
+            draw = (probs * (dp_ref[sub % 2, :, :queries] - delta)).astype(BF)
+            dq = mm_nn(kt_ref[own, keys_at], draw) * (HD ** (-0.5))
+            grads_ref[own, queries_at] = dq.astype(BF)
+            dk = mm_nt(q_rows, draw) * (1.0 / LOG2E)
+            grads_ref[128 + sub * HD : 160 + sub * HD, keys_at] = dk.astype(BF)
+            dv = mm_nt(do_rows, probs.astype(BF))
+            grads_ref[256 + sub * HD : 288 + sub * HD, keys_at] = dv.astype(BF)
+
+    heads(0, HALF)
+
+    def body(group, carry):
+        heads(group, SEQ)
+        return carry
+
+    lax.fori_loop(1, 3, body, 0)
+    grads = grads_ref[...]
+    for part in range(3):
+        g_ref[0, part] = mm_nt(nt_ref[...], grads[part * 128 : part * 128 + 128]).astype(BF)
+    bsum_ref[0] = mm_nt(jnp.ones((8, grads.shape[1]), BF), grads)
+    acc_ref[...] += mm_tn(grads, wt_ref[0].reshape(384, 512))
+
+    @pl.when(step == 3)
+    def _():
+        dn_ref[0:HALF] = acc_ref[0:HALF]
+        dn_ref[HALF:] = acc_ref[SEQ:]
+        far_ref[...] = acc_ref[HALF:SEQ].astype(BF)
+
+
+def attend_back(key_count, qt, kt, dot, ot, k, v, lse, nt, wt):
+    ext = 3 * SEQ
+    tall = pl.BlockSpec((128, ext), lambda b: (b, 0))
+    wide = pl.BlockSpec((ext, 128), lambda b: (0, b))
+    return pl.pallas_call(
+        attend_back_kernel,
+        grid=(4,),
+        out_shape=[
+            sds((2, 3, 512, 256), BF), sds((ext - HALF, 512), F32), sds((HALF, 512), BF),
+            sds((4, 8, 384), F32),
+        ],
+        in_specs=[
+            pl.BlockSpec(memory_space=pltpu.SMEM), tall, tall, tall, tall, wide, wide,
+            pl.BlockSpec((3, 1, 8, SEQ), lambda b: (0, b, 0, 0)), full_spec((512, ext)),
+            pl.BlockSpec((1, 3, 128, 512), lambda b: (b // 2, 0, b % 2, 0)),
+        ],
+        out_specs=[
+            pl.BlockSpec((1, 3, 512, 128), lambda b: (b // 2, 0, 0, b % 2)),
+            full_spec((ext - HALF, 512)), full_spec((HALF, 512)),
+            pl.BlockSpec((1, 8, 384), lambda b: (b, 0, 0)),
+        ],
+        scratch_shapes=[
+            pltpu.VMEM((384, ext), BF), pltpu.VMEM((ext, 512), F32), pltpu.VMEM((3, SEQ, 128), BF),
+            pltpu.VMEM((2, SEQ, SEQ), F32), pltpu.VMEM((2, SEQ, SEQ), F32),
+        ],
+        compiler_params=pltpu.CompilerParams(vmem_limit_bytes=VMEM_LIMIT),
+        name="attend_back",
+    )(key_count, qt, kt, dot, ot, k, v, lse, nt, wt)
+
+
+def input_grad_kernel(x_ref, dn_ref, far_ref, dres_ref, vec_ref, grad_ref, vsum_ref):
+    mp = lax.axis_index("mp")
+    gain, shift = vec_ref[0:1, :], vec_ref[1:2, :]
+    vsum_ref[...] = jnp.zeros_like(vsum_ref)
+
+    def block(index, dn):
+        at = pl.ds(pl.multiple_of(index * HALF, HALF), HALF)
+        place = pl.ds(row_block(index, mp), HALF)
+        _, unit, inverse = layer_norm_rows(x_ref[place, :].astype(F32), gain, shift)
+        grad_ref[place, :] = dres_ref[at, :] + layer_norm_back(dn, unit, inverse, gain)
+        vsum_ref[0] += jnp.sum((dn * unit).reshape(HALF // 8, 8, 512), axis=0)
+        vsum_ref[1] += jnp.sum(dn.reshape(HALF // 8, 8, 512), axis=0)
+
+    block(0, dn_ref[0:HALF] + far_ref[...].astype(F32))
+
+    def body(index, carry):
+        block(index, dn_ref[pl.ds(pl.multiple_of(index * HALF, HALF), HALF), :])
+        return carry
+
+    lax.fori_loop(1, 5, body, 0)
+
+
+def finish_input(patches, dn, far, dres, vec_params):
+    return pl.pallas_call(
+        input_grad_kernel,
+        out_shape=[sds(patches.shape, F32), sds((2, 8, 512), F32)],
+        compiler_params=pltpu.CompilerParams(vmem_limit_bytes=VMEM_LIMIT),
+        name="finish_input",
+    )(patches, dn, far, dres, vec_params)
+
+
+def reduce_kernel(
+    down_ref, up_ref, proj_ref, qkv_ref, one_ref, two_ref, up_sum_ref, qkv_sum_ref,
+    down_out, up_out, proj_out, qkv_out, small_out, norm_ref,
+    *scratch,
+):
+    sends, scratch = scratch[-2:], scratch[:-2]
+    send_sem, recv_sem = sends
+    dp, mp = lax.axis_index("dp"), lax.axis_index("mp")
+    core, x_side, z_near, z_far = partners(dp)
+    targets = [{"dp": core}, {"mp": 1 - mp}, {"dp": x_side}, {"dp": z_near}, {"dp": z_far}]
+    bits = [lax.rem(dp, 2), None] + [lax.rem(lax.div(dp, size), 2) for size in (2, 4, 8)]
+    greet(targets)
+
+    def send(src, dst, index, stage):
+        copy = pltpu.make_async_remote_copy(
+            src_ref=src, dst_ref=dst, send_sem=send_sem.at[index], recv_sem=recv_sem.at[index],
+            device_id=targets[stage], device_id_type=MESH,
+        )
+        copy.start()
+        return copy
+
+    started = []
+    arrays = []
+    for index, (grad, out) in enumerate(
+        [(down_ref, down_out), (up_ref, up_out), (proj_ref, proj_out), (qkv_ref, qkv_out)]
+    ):
+        fore, own, *landing = scratch[7 * index : 7 * index + 7]
+        arrays.append((grad, out, fore, own, landing, 9 * index))
+    small_bufs = scratch[28]
+    square_bufs = scratch[29]
+
+    def rows(start, size):
+        return pl.ds(pl.multiple_of(start, 16), size)
+
+    def share(total, upto):
+        start, size = 0, total
+        for stage in (0, 2, 3, 4):
+            if stage > upto:
+                break
+            size //= 2
+            start = start + bits[stage] * size
+        return start, size
+
+    live = {}
+
+    def begin(entry, stage):
+        grad, out, fore, own, landing, base = entry
+        total = grad.shape[1]
+        if stage == 0:
+            size = total // 2
+            away = (1 - bits[0]) * size
+            live[base] = send(grad.at[:, rows(away, size), :], landing[0], base, 0)
+        elif stage == 1:
+            live[base] = send(fore, landing[1], base + 1, 1)
+        elif stage <= 4:
+            start, size = share(total, stage)
+            outer, outer_size = share(total, stage - 1)
+            away = (1 - bits[stage]) * size
+            offset = outer - share(total, 0)[0]
+            live[base] = send(own.at[rows(offset + away, size), :], landing[stage], base + stage, stage)
+        else:
+            level = (None, 4, 3, 2, 0)[stage - 4]
+            start, size = share(total, level)
+            where = out.at[rows(start, size), :]
+            live[base] = send(where, where, base + stage, level)
+        started.append(live[base])
+
+    def end(entry, stage):
+        grad, out, fore, own, landing, base = entry
+        total = grad.shape[1]
+        live[base].wait_recv()
+        first = share(total, 0)[0]
+        if stage == 0:
+            size = total // 2
+            at = rows(first, size)
+            fore[...] = grad[1 - mp, at, :] + landing[0][1 - mp]
+            own[...] = grad[mp, at, :] + landing[0][mp]
+        elif stage == 1:
+            own[...] += landing[1][...]
+        elif stage <= 4:
+            start, size = share(total, stage)
+            at = rows(start - first, size)
+            value = own[at, :] + landing[stage][...]
+            if stage < 4:
+                own[at, :] = value
+            else:
+                out[rows(start, size), :] = value
+                wide = value.astype(F32)
+                square = jnp.sum((wide * wide).reshape(-1, 8, wide.shape[1]), axis=0)
+                folded = square[:, 0:128]
+                for lane in range(1, wide.shape[1] // 128):
+                    folded = folded + square[:, lane * 128 : lane * 128 + 128]
+                squares.append(folded)
+
+    squares = []
+    small_live = []
+    square_live = []
+
+    def small_begin(stage):
+        small_live.append(send(small_bufs.at[0, stage], small_bufs.at[1, stage], 36 + stage, stage))
+
+    def small_end(stage):
+        small_live[stage].wait_recv()
+        value = small_bufs[0, stage] + small_bufs[1, stage]
+        if stage < 4:
+            small_bufs[0, stage + 1] = value
+        else:
+            small_out[...] = value
+
+    order = (4, 3, 2, 0, 1)
+
+    def square_begin(place):
+        square_live.append(
+            send(square_bufs.at[0, place], square_bufs.at[1, place], 41 + place, order[place])
+        )
+
+    def square_end(place):
+        square_live[place].wait_recv()
+        value = square_bufs[0, place] + square_bufs[1, place]
+        if place < 4:
+            square_bufs[0, place + 1] = value
+        else:
+            total = jnp.sum(small_out[...] * small_out[...]) + jnp.sum(value)
+            norm_ref[...] = jnp.sqrt(jnp.full((8, 128), total, F32))
+
+    def small_row(place, value):
+        small_bufs[0, 0, place : place + 1, :] = value
+
+    small_bufs[0, 0] = jnp.zeros((16, 512), F32)
+    for block in range(4):
+        lanes = slice(block * 128, block * 128 + 128)
+        small_bufs[0, 0, 0:1, lanes] = qkv_sum_ref[block, 0:1, 0:128]
+        small_bufs[0, 0, 1:2, lanes] = qkv_sum_ref[block, 0:1, 256:384]
+        small_row(2 + block, jnp.sum(up_sum_ref[block], axis=0, keepdims=True))
+        small_row(8 + block, jnp.sum(two_ref[block], axis=0, keepdims=True))
+    for place in range(2):
+        small_row(6 + place, jnp.sum(one_ref[place], axis=0, keepdims=True))
+    small_begin(0)
+    for tick in range(4 + 9):
+        for index, entry in enumerate(arrays):
+            stage = tick - index
+            if stage < 0 or stage > 9:
+                continue
+            if stage > 0:
+                end(entry, stage - 1)
+            if stage < 9:
+                begin(entry, stage)
+            if stage == 5 and index == 3:
+                square_bufs[0, 0] = squares[0] + squares[1] + squares[2] + squares[3]
+                square_begin(0)
+            if stage > 5 and index == 3:
+                square_end(stage - 6)
+                square_begin(stage - 5)
+        if 1 <= tick <= 5:
+            small_end(tick - 1)
+            if tick < 5:
+                small_begin(tick)
+    square_end(4)
+    for copy in started + small_live + square_live:
+        copy.wait_send()
+
+
+def reduce_gradients(down, up, proj, qkv, *sums):
+    vmem = pl.BlockSpec(memory_space=pltpu.VMEM)
+    scratch = []
+    for array in (down, up, proj, qkv):
+        _, rows, width = array.shape
+        scratch += [pltpu.VMEM((rows // 2, width), BF), pltpu.VMEM((rows // 2, width), BF)]
+        scratch += [pltpu.VMEM((2, rows // 2, width), BF), pltpu.VMEM((rows // 2, width), BF)]
+        scratch += [pltpu.VMEM((rows // size, width), BF) for size in (4, 8, 16)]
+    scratch += [pltpu.VMEM((2, 5, 16, 512), F32), pltpu.VMEM((2, 5, 8, 128), F32)]
+    scratch += [pltpu.SemaphoreType.DMA((46,)), pltpu.SemaphoreType.DMA((46,))]
+    return pl.pallas_call(
+        reduce_kernel,
+        out_shape=[sds(array.shape[1:], BF) for array in (down, up, proj, qkv)]
+        + [sds((16, 512), F32), sds((8, 128), F32)],
+        in_specs=[vmem] * 8,
+        out_specs=[vmem] * 6,
+        scratch_shapes=scratch,
+        compiler_params=pltpu.CompilerParams(
+            collective_id=1, has_side_effects=True, vmem_limit_bytes=VMEM_LIMIT
+        ),
+        name="reduce_gradients",
+    )(down, up, proj, qkv, *sums)
+
+
+def adam_kernel(norm_ref, *refs):
+    factor = jnp.minimum(1.0, CLIP_NORM / (norm_ref[0:1, 0:1] + 1e-06))
+    for index in range(4):
+        weight_ref, one_ref, two_ref, grad_ref = refs[4 * index : 4 * index + 4]
+        outs = refs[16 + 3 * index : 19 + 3 * index]
+        results = adam_update(
+            weight_ref[...], grad_ref[...].astype(F32) * factor, one_ref[...], two_ref[...],
+            MATRIX_RATE, DECAY_RATE,
+        )
+        for out, value in zip(outs, results):
+            out[...] = value
+
+
+def adam_matrices(norm, groups):
+    steps = 8
+    in_specs, out_specs, out_shape, args = [full_spec((8, 128))], [], [], [norm]
+    for group in groups:
+        rows, width = group[0].shape
+        spec = pl.BlockSpec((rows // steps, width), lambda i: (i, 0))
+        in_specs += [spec] * 4
+        out_specs += [spec] * 3
+        out_shape += [sds((rows, width), F32)] * 3
+        args += list(group)
+    outs = pl.pallas_call(
+        adam_kernel,
+        grid=(steps,),
+        out_shape=out_shape,
+        in_specs=in_specs,
+        out_specs=out_specs,
+        compiler_params=pltpu.CompilerParams(vmem_limit_bytes=VMEM_LIMIT),
+        name="adam_matrices",
+    )(*args)
+    return [outs[3 * index : 3 * index + 3] for index in range(len(groups))]
+
+
+IN_SPECS = (
             P(("dp", "mp"), None),
             P(("dp", "mp"), None),
             P("dp"),
@@ -310,8 +1038,8 @@
             P("mp"),
             P(),
             P(),
-        ),
-        out_specs=(
+        )
+OUT_SPECS = (
             P(("dp", "mp"), None),
             P(("dp", "mp"), None),
             P(),
@@ -336,6 +1064,61 @@
             P(),
             P(),
             P(),
-        ),
-        check_vma=False,
-    )
+        )
+
+
+def paired(
+    patches, cotangent, key_count, w_qkv, w_proj, w_up, w_down, qv_bias, up_bias, vec_params,
+    first_qkv, second_qkv, first_proj, second_proj, first_up, second_up, first_down, second_down,
+    first_qv_bias, second_qv_bias, first_up_bias, second_up_bias, first_vec, second_vec,
+):
+    mp = lax.axis_index("mp")
+    small = jnp.concatenate(
+        [up_bias[None, :], jnp.pad(qv_bias, ((0, 0), (0, 768))), jnp.zeros((5, 1024), F32)], axis=0
+    )
+    wt, wp, wu, wd, small_all, other = gather_weights(w_qkv, w_proj, w_up, w_down, small, patches)
+    nt, qt, kt, k, v, ot, lse = attend_forward(key_count, patches, other, wt, vec_params, small_all)
+    activations, dres, dot, g_down, g_up, g_proj, vsum_two, up_sums = mlp(
+        patches, cotangent, ot, wp, wu, wd, vec_params, small_all
+    )
+    g_qkv, dn, far, qkv_sums = attend_back(key_count, qt, kt, dot, ot, k, v, lse, nt, wt)
+    arrived = lax.ppermute(far, "mp", [(0, 1), (1, 0)])
+    input_grad, vsum_one = finish_input(patches, dn, arrived, dres, vec_params)
+    down, up, proj, qkv, small_total, norm = reduce_gradients(
+        g_down, g_up, g_proj, g_qkv.reshape(2, 1536, 256), vsum_one, vsum_two, up_sums, qkv_sums
+    )
+    flat = lambda array: array.reshape(-1, array.shape[-1])
+    groups = [
+        (flat(w_qkv), flat(first_qkv), flat(second_qkv), qkv),
+        (w_proj, first_proj, second_proj, proj),
+        (w_up, first_up, second_up, up),
+        (w_down, first_down, second_down, down),
+    ]
+    new_qkv, new_proj, new_up, new_down = adam_matrices(norm, groups)
+    grad_norm = norm[0, 0]
+    factor = jnp.minimum(1.0, CLIP_NORM / (grad_norm + 1e-06))
+    qv_total = lax.dynamic_slice_in_dim(small_total[0:2], mp * 256, 256, 1)
+    up_total = lax.dynamic_slice_in_dim(small_total[2:6].reshape(-1), mp * 1024, 1024, 0)
+    new_qvb = adam_update(qv_bias, qv_total * factor, first_qv_bias, second_qv_bias, VECTOR_RATE, 0.0)
+    new_upb = adam_update(up_bias, up_total * factor, first_up_bias, second_up_bias, VECTOR_RATE, 0.0)
+    new_vec = adam_update(
+        vec_params, small_total[6:12] * factor, first_vec, second_vec, VECTOR_RATE, 0.0
+    )
+    return (
+        activations, input_grad, grad_norm, *[array.reshape(w_qkv.shape) for array in new_qkv],
+        *new_proj, *new_up, *new_down, *new_qvb, *new_upb, *new_vec,
+    )
+
+
+def fits_pairs(mesh, args):
+    if dict(mesh.shape) != {"dp": 16, "mp": 2}:
+        return False
+    return args[0].shape == (40960, 512) and args[2].shape == (80,)
+
+
+def solution(mesh):
+    def run(*args):
+        body = paired if fits_pairs(mesh, args) else local
+        return jax.shard_map(body, mesh=mesh, in_specs=IN_SPECS, out_specs=OUT_SPECS, check_vma=False)(*args)
+
+    return run

time: 961 us -> 274 us (0.29); the launches traced: 943 us -> 273 us
  waiting for transfers between devices: 433 us -> 7.67 us
  matrix products: 263 us -> 0 us
  Pallas kernels: 0 us -> 256 us
  other arithmetic: 89.4 us -> 4.03 us
  local copies, waits for them, and re-layouts: 73.1 us -> 3.46 us
  blocking collectives: 62.7 us -> 0 us
  between operations: 21.8 us -> 1.64 us
    psum x4 -> x0, waiting for transfers between devices: 386 us -> none  [the longest x1 130 us: local(): resid_all = whole_rows + lax.psum(proj_part, 'mp') + proj_shift]
    dot_general x18 -> x0, matrix products: 263 us -> none  [the longest x1 54 us: attend_backward(): jnp.einsum('shqk,skhe->sqhe', raw_grad, key_rows, preferred_element_type=...]
    pallas_call x0 -> x7, Pallas kernels: none -> 256 us  [the longest x1 84.9 us: reduce_gradients(): pl.pallas_call(reduce_kernel, out_shape=[sds(array.shape[1:], BF) for arr...]
    psum x2 -> x0, blocking collectives: 62.7 us -> none  [the longest x1 56.9 us: local(): lax.psum(vec_grad.astype(jnp.bfloat16), 'dp').astype(jnp.float32)]
    reduce_sum x19 -> x0, other arithmetic: 54.3 us -> none  [the longest x1 17.9 us: local(): jnp.sum(jnp.exp(scores - top_score), axis=-1, keepdims=True)]
    all_gather x2 -> x0, waiting for transfers between devices: 45.4 us -> none  [the longest x1 39.6 us: local(): lax.all_gather(patches, 'mp', axis=0, tiled=True)]
    unnamed x131 -> x22, local copies, waits for them, and re-layouts: 25 us -> 1.48 us
    convert_element_type x4 -> x0, other arithmetic: 15.5 us -> none  [the longest x1 6.47 us: local(): branch_low = resid_all_grad.astype(jnp.bfloat16)]
  transfers between devices with their start and end apart: 6 -> 1, of which waited for: 6 -> 1; matrix products, arithmetic and copies ran while one was open for 9% -> 0% of each run, Pallas kernels for 0% -> 0%
where the time goes in v1:
time: 274 us; the launch traced here: 273 us
  Pallas kernels  256 us (93%)
  waiting for transfers between devices  7.67 us (3%)
  other arithmetic  4.03 us (1%)
  local copies, waits for them, and re-layouts  3.46 us (1%)
    pallas_call x1, Pallas kernels, reduce_gradients(): pl.pallas_call(reduce_kernel, out_shape=[sds(array.shape[1:], BF) for arr...  84.9 us
    pallas_call x1, Pallas kernels, attend_back(): pl.pallas_call(attend_back_kernel, grid=(4,), out_shape=[sds((2, 3, 512,...  44.2 us
    pallas_call x1, Pallas kernels, gather_weights(): pl.pallas_call(gather_kernel, out_shape=[sds((2, 3, 256, 512), BF), sds((...  42.3 us
    pallas_call x1, Pallas kernels, mlp(): pl.pallas_call(mlp_kernel, grid=(4,), out_shape=[sds((rows, 512), BF), sd...  38.4 us
    pallas_call x1, Pallas kernels, attend_forward(): pl.pallas_call(attend_kernel, grid=(3,), out_shape=[sds((512, ext), BF),...  22.8 us
    pallas_call x1, Pallas kernels, adam_matrices(): pl.pallas_call(adam_kernel, grid=(steps,), out_shape=out_shape, in_specs=...  16.9 us
    ppermute x1, waiting for transfers between devices, paired(): arrived = lax.ppermute(far, 'mp', [(0, 1), (1, 0)])  7.67 us
    pallas_call x1, Pallas kernels, finish_input(): pl.pallas_call(input_grad_kernel, out_shape=[sds(patches.shape, F32), sds...  6.41 us
  transfers between devices with their start and end apart: 1, of which 1 were waited for; matrix products, arithmetic and copies ran while one was open for 0% of the time, Pallas kernels for 0%

profile of v1, /device:TPU:1, one launch (start us, length us, event | category | flops | bytes accessed | tf_op | source)
XLA Modules:
  0.0 273.2 jit_solution(17856817575566910138)
XLA Ops:
  0.7 0.1 pad.7.clone
  0.7 1.4 fusion.small_ref
  2.1 42.3 %gather_weights.1 = (bf16[2,3,256,512]{3,2,1,0:T(8,128)(2,1)}, bf16[2,256,512]{2,1,0:T(8,128)(2,1)}, bf16[2,512,1024]{2,1,0:T(8,128)(2,1)}, bf16[2,1024,512]{2,1...) custom-call(f32[3,512,256]{2,1,0:T(8,128)} %qkv_ref.1, f32[256,512]{1,0:T(8,128)} %refs_4_.1, ...), custom_call_target="tpu_custom_call" | custom-call | tf_op jit(solution)/shard_map/gather_weights/pallas_call | solution.py:395
  44.4 22.8 %attend_forward.1 = (bf16[512,1536]{1,0:T(8,128)(2,1)}, bf16[512,1536]{1,0:T(8,128)(2,1)}, bf16[512,1536]{1,0:T(8,128)(2,1)}, bf16[1536,512]{1,0:T(8,128)(2,1)},...) custom-call(s32[5]{0:T(128)} %count_ref.3, bf16[1280,512]{1,0:T(8,128)(2,1)} %x_ref.5, ...), custom_call_target="tpu_custom_call" | custom-call | tf_op jit(solution)/shard_map/attend_forward/pallas_call | solution.py:538
  67.2 38.4 %mlp.1 = (bf16[1280,512]{1,0:T(8,128)(2,1)}, f32[1280,512]{1,0:T(8,128)}, bf16[512,1536]{1,0:T(8,128)(2,1)}, bf16[2,1024,512]{2,1,0:T(8,128)(2,1)}, bf16[2,512,1...) custom-call(bf16[1280,512]{1,0:T(8,128)(2,1)} %x_ref.5, ...), custom_call_target="tpu_custom_call" | custom-call | tf_op jit(solution)/shard_map/mlp/pallas_call | solution.py:641
  105.6 44.2 %attend_back.1 = (bf16[2,3,512,256]{3,2,1,0:T(8,128)(2,1)}, f32[1280,512]{1,0:T(8,128)}, bf16[256,512]{1,0:T(8,128)(2,1)}, f32[4,8,384]{2,1,0:T(8,128)}) custom-call(s32[5]{0:T(128)} %count_ref.3, bf16[512,1536]{1,0:T(8,128)(2,1)} %get-tuple-element.77.qt_ref, bf16[512,1536]{1,0:T(8,128)(2,1)} %get-tuple-element.78.kt_ref, ...), custom_call_target="tpu_custom_call" | custom-call | tf_op jit(solution)/shard_map/attend_back/pallas_call | solution.py:738
  149.8 0.5 collective-permute-start
  150.3 7.7 %collective-permute-done.far_ref = bf16[256,512]{1,0:T(8,128)(2,1)S(1)} collective-permute-done((bf16[256,512]{1,0:T(8,128)(2,1)}, bf16[256,512]{1,0:T(8,128)(2,1)S(1)}, u32[]{:S(2)}, u32[]{:S(2)}) %collective-permute-start) | collective-permute-done | bytes 262176 | tf_op jit(solution)/shard_map/ppermute | solution.py:1085
  158.0 0.7 copy-done.1
  158.7 6.4 %finish_input.1 = (f32[1280,512]{1,0:T(8,128)}, f32[2,8,512]{2,1,0:T(8,128)}) custom-call(bf16[1280,512]{1,0:T(8,128)(2,1)} %x_ref.5, f32[1280,512]{1,0:T(8,128)} %get-tuple-element.84.dn_ref, bf16[256,512]{1,0:T(8,128)(2,1)} %copy-done.1, f32[1280,512]{1,0:T(8,128)} %get-tuple-element.86.dres_ref, f32[6,512]{1,0:T(8,128)} %vec_ref.5), custom_call_target="tpu_custom_call" | custom-call | tf_op jit(solution)/shard_map/finish_input/pallas_call | solution.py:787
  165.1 0.0 copy-start.4
  165.1 0.0 copy-start.6
  165.1 0.0 copy-start.7
  165.1 0.0 copy-start.5
  165.2 0.0 copy-start.8
  165.2 0.0 copy-start.9
  165.2 84.9 %reduce_gradients.1 = (bf16[1024,512]{1,0:T(8,128)(2,1)}, bf16[512,1024]{1,0:T(8,128)(2,1)}, bf16[256,512]{1,0:T(8,128)(2,1)}, bf16[1536,256]{1,0:T(8,128)(2,1)}, f32[16,512]{1,0:T(8,128)}, /*index=5*/f32[8,128]{1,0:T(8,128)}) custom-call(bf16[2,1024,512]{2,1,0:T(8,128)(2,1)} %get-tuple-element.88.down_ref, bf16[2,512,1024]{2,1,0:T(8,128)(2,1)} %get-tuple-element.89.up_ref, ...), custom_call_target="tpu_custom_call" | custom-call | tf_op jit(solution)/shard_map/reduce_gradients/pallas_call | solution.py:967
  250.1 0.7 slice_bitcast_fusion
  250.8 0.7 slice.13
  251.5 1.2 slice.12
  253.4 0.0 copy-done
  253.4 0.0 copy-done.2
  253.4 0.0 copy-done.3
  253.4 1.4 multiply_subtract_fusion
  254.8 0.0 copy-done.4
  254.8 0.0 copy-done.6
  254.8 0.0 copy-done.7
  254.8 0.6 multiply_subtract_fusion.1
  255.5 0.0 copy-done.5
  255.5 0.0 copy-done.8
  255.5 0.6 multiply_subtract_fusion.2
  256.1 16.9 %adam_matrices.1 = (f32[1536,256]{1,0:T(8,128)}, f32[1536,256]{1,0:T(8,128)}, f32[1536,256]{1,0:T(8,128)}, f32[256,512]{1,0:T(8,128)}, f32[256,512]{1,0:T(8,128)...) custom-call(f32[8,128]{1,0:T(8,128)} %get-tuple-element.96.norm_ref,, ...), custom_call_target="tpu_custom_call" | custom-call | tf_op jit(solution)/shard_map/adam_matrices/pallas_call | solution.py:1004
  (7 shorter events, 0.0 us)
Async XLA Ops:
  149.8 8.2 %collective-permute-start = (bf16[256,512]{1,0:T(8,128)(2,1)}, bf16[256,512]{1,0:T(8,128)(2,1)S(1)}, u32[]{:S(2)}, u32[]{:S(2)}) collective-permute-start(bf16[256,512]{1,0:T(8,128)(2,1)} %get-tuple-element.85), channel_id=1, source_target_pairs={{0,1},{1,0},{2,3},{3,2},{4,5},{5,4},{6,7},{7,6},{8,9},{9,8},{10,11... | collective-permute-start | bytes 786440 | tf_op jit(solution)/shard_map/ppermute | solution.py:1085
  158.0 0.7 copy-start.1
  165.1 88.3 %copy-start = (f32[6,512]{1,0:T(8,128)S(1)}, f32[6,512]{1,0:T(8,128)}, u32[]{:S(2)}) copy-start(f32[6,512]{1,0:T(8,128)} %vec_ref.5) | copy-start | bytes 36868
  165.1 88.3 %copy-start.2 = (f32[6,512]{1,0:T(8,128)S(1)}, f32[6,512]{1,0:T(8,128)}, u32[]{:S(2)}) copy-start(f32[6,512]{1,0:T(8,128)} %param.46) | copy-start | bytes 36868
  165.1 88.3 %copy-start.3 = (f32[6,512]{1,0:T(8,128)S(1)}, f32[6,512]{1,0:T(8,128)}, u32[]{:S(2)}) copy-start(f32[6,512]{1,0:T(8,128)} %param.47) | copy-start | bytes 36868
  165.1 89.7 %copy-start.4 = (f32[1024]{0:T(1024)S(1)}, f32[1024]{0:T(1024)}, u32[]{:S(2)}) copy-start(f32[1024]{0:T(1024)} %param.32) | copy-start | bytes 12292
  165.1 89.7 %copy-start.6 = (f32[1024]{0:T(1024)S(1)}, f32[1024]{0:T(1024)}, u32[]{:S(2)}) copy-start(f32[1024]{0:T(1024)} %param.44) | copy-start | bytes 12292
  165.1 89.7 %copy-start.7 = (f32[1024]{0:T(1024)S(1)}, f32[1024]{0:T(1024)}, u32[]{:S(2)}) copy-start(f32[1024]{0:T(1024)} %param.45) | copy-start | bytes 12292
  165.1 90.3 %copy-start.5 = (f32[2,256]{1,0:T(2,128)S(1)}, f32[2,256]{1,0:T(2,128)}, u32[]{:S(2)}) copy-start(f32[2,256]{1,0:T(2,128)} %param.31) | copy-start | bytes 6148
  165.2 90.3 %copy-start.8 = (f32[2,256]{1,0:T(2,128)S(1)}, f32[2,256]{1,0:T(2,128)}, u32[]{:S(2)}) copy-start(f32[2,256]{1,0:T(2,128)} %param.42) | copy-start | bytes 6148
  165.2 90.3 %copy-start.9 = (f32[2,256]{1,0:T(2,128)S(1)}, f32[2,256]{1,0:T(2,128)}, u32[]{:S(2)}) copy-start(f32[2,256]{1,0:T(2,128)} %param.43) | copy-start | bytes 6148

commit v2 on v0

--- a/solution.py
+++ b/solution.py
@@ -1,6 +1,8 @@
 import jax
 import jax.numpy as jnp
 from jax import lax
+from jax.experimental import pallas as pl
+from jax.experimental.pallas import tpu as pltpu
 from jax.sharding import PartitionSpec as P
 
 HD = 32
@@ -16,6 +18,56 @@
 VECTOR_RATE = 0.8
 CLIP_NORM = 1.0
 MASK_FILL = -1e30
+LOG2E = 1.4426950408889634
+BF = jnp.bfloat16
+F32 = jnp.float32
+MESH = pl.DeviceIdType.MESH
+SEQ = 512
+HALF = 256
+VMEM_LIMIT = 58 * 1024 * 1024
+
+
+def mm_nn(left, right):
+    return lax.dot_general(left, right, (((1,), (0,)), ((), ())), preferred_element_type=F32)
+
+
+def mm_nt(left, right):
+    return lax.dot_general(left, right, (((1,), (1,)), ((), ())), preferred_element_type=F32)
+
+
+def mm_tn(left, right):
+    return lax.dot_general(left, right, (((0,), (0,)), ((), ())), preferred_element_type=F32)
+
+
+def partners(dp):
+    core = dp + 1 - 2 * lax.rem(dp, 2)
+    x_side = dp + 2 - 4 * lax.rem(lax.div(dp, 2), 2)
+    z_near = dp + 4 - 8 * lax.rem(lax.div(dp, 4), 2)
+    z_far = dp + 8 - 16 * lax.rem(lax.div(dp, 8), 2)
+    return core, x_side, z_near, z_far
+
+
+def greet(targets):
+    barrier = pltpu.get_barrier_semaphore()
+    for target in targets:
+        pl.semaphore_signal(barrier, inc=1, device_id=target, device_id_type=MESH)
+    pl.semaphore_wait(barrier, len(targets))
+
+
+def full_spec(shape):
+    return pl.BlockSpec(shape, lambda *_: (0,) * len(shape))
+
+
+def sds(shape, dtype):
+    return jax.ShapeDtypeStruct(shape, dtype)
+
+
+def row_block(index, mp):
+    return pl.multiple_of(lax.rem(index + 4 * (1 - mp), 5) * HALF, HALF)
+
+
+def ext_cols(index):
+    return pl.multiple_of(jnp.where(index == 0, 0, HALF + HALF * index), HALF)
 
 
 def norm_forward(values, norm_gain, norm_shift):
@@ -281,11 +333,963 @@
     )
 
 
-def solution(mesh):
-    return jax.shard_map(
-        local,
-        mesh=mesh,
-        in_specs=(
+def layer_norm_rows(rows, gain, shift):
+    centred = rows - jnp.mean(rows, axis=-1, keepdims=True)
+    inverse = lax.rsqrt(jnp.mean(centred * centred, axis=-1, keepdims=True) + NORM_EPS)
+    unit = centred * inverse
+    return unit * gain + shift, unit, inverse
+
+
+def layer_norm_back(grad, unit, inverse, gain):
+    scaled = grad * gain
+    centre = jnp.mean(scaled, axis=-1, keepdims=True)
+    slope = jnp.mean(scaled * unit, axis=-1, keepdims=True)
+    return inverse * (scaled - centre - unit * slope)
+
+
+def head_rows(block, sub):
+    return pl.ds(pl.multiple_of(block * 128 + sub * HD, HD), HD)
+
+
+def head_cols(block):
+    return pl.ds(pl.multiple_of(block * 128, 128), 128)
+
+
+def key_bias(shape, mp, count, shared):
+    slot = lax.broadcasted_iota(jnp.int32, shape, 0)
+    if shared:
+        slot = lax.rem(slot + HALF * mp, SEQ)
+    return jnp.where(slot < count, 0.0, MASK_FILL).astype(BF)
+
+
+def widen(rows, sub):
+    zeros = jnp.zeros_like(rows)
+    row = lax.broadcasted_iota(jnp.int32, rows.shape, 0)
+    ones = jnp.where(row == 0, 1.0, 0.0).astype(BF)
+    parts = [zeros] * 4
+    parts[sub] = rows
+    parts[(sub + 1) % 4] = ones
+    return jnp.concatenate(parts, axis=0)
+
+
+def widen_plain(rows, sub):
+    parts = [jnp.zeros_like(rows)] * 4
+    parts[sub] = rows
+    return jnp.concatenate(parts, axis=0)
+
+
+def score_tile(key_block, bias, query_rows, sub):
+    lane = lax.broadcasted_iota(jnp.int32, key_block.shape, 1)
+    keys = jnp.where(lane // HD == (sub + 1) % 4, bias, key_block)
+    return mm_nn(keys, widen(query_rows, sub))
+
+
+def forward_kernel(
+    count_ref, qkv_ref, proj_ref, up_ref, down_ref, small_ref, x_ref, vec_ref,
+    wt_out, wp_out, wu_out, wd_out, sm_out,
+    nt_out, qt_out, kt_out, k_out, v_out, ot_out, lse_out,
+    wt_ref, own_proj, own_up, own_down, sm_ref, other_ref,
+    norm_ref, nt_ref, qt_ref, kt_ref, vt_ref, k_ref, v_ref, ot_ref, lse_ref, bias_ref, s_ref,
+    send_sem, recv_sem, local_sem,
+):
+    dp, mp = lax.axis_index("dp"), lax.axis_index("mp")
+    peer = 1 - mp
+    core, x_side, _, _ = partners(dp)
+    quarter = lax.rem(dp, 4)
+    x_quarter = lax.rem(quarter + 2, 4)
+    gain, shift = vec_ref[0:1, :], vec_ref[1:2, :]
+    greet([{"mp": peer}, {"dp": core}, {"dp": x_side}])
+
+    remote, local = [], []
+
+    class Transfer:
+        def __init__(self, src, dst, target):
+            self.index = len(remote)
+            self.views = (src, dst, target)
+            remote.append(self)
+            self.make().start()
+
+        def make(self):
+            src, dst, target = self.views
+            return pltpu.make_async_remote_copy(
+                src_ref=src(), dst_ref=dst(), send_sem=send_sem.at[self.index],
+                recv_sem=recv_sem.at[self.index], device_id=target, device_id_type=MESH,
+            )
+
+        def wait_recv(self):
+            self.make().wait_recv()
+
+        def wait_send(self):
+            self.make().wait_send()
+
+    def send(src, dst, target):
+        return Transfer(src, dst, target)
+
+    def keep(src, dst):
+        copy = pltpu.make_async_copy(src, dst, local_sem.at[len(local)])
+        copy.start()
+        local.append(copy)
+
+    def span(start, size):
+        return pl.ds(pl.multiple_of(start, 16), size)
+
+    pieces = []
+    for part in range(3):
+        pieces.append((wt_ref.at[mp, part], lambda side, part=part: wt_ref.at[side, part], 64, 0))
+    pieces.append((own_proj, lambda side: wp_out.at[side], 64, 0))
+    for shard, out, rows in ((own_up, wu_out, 128), (own_down, wd_out, 256)):
+        for part in range(2):
+            pieces.append((shard, lambda side, out=out: out.at[side], rows // 2, part * rows * 2))
+
+    def place(ref, index, part):
+        rows, base = pieces[index][2], pieces[index][3]
+        return ref.at[span(base + part * rows, rows), :]
+
+    first, second, third = {}, {}, {}
+
+    def to_peer(index):
+        first[index] = send(
+            lambda: place(pieces[index][0], index, quarter),
+            lambda: place(pieces[index][1](mp), index, quarter), {"mp": peer},
+        )
+
+    def to_sides(index):
+        first[index].wait_recv()
+        at = lambda: place(pieces[index][1](peer), index, quarter)
+        second[index] = send(at, at, {"dp": x_side})
+        third[index] = [send(at, at, {"dp": core})]
+
+    def to_core(index):
+        second[index].wait_recv()
+        at = lambda: place(pieces[index][1](peer), index, x_quarter)
+        third[index].append(send(at, at, {"dp": core}))
+
+    def arrive(index):
+        for copy in third[index]:
+            copy.wait_recv()
+
+    own_half = pl.multiple_of((1 - mp) * 4 * HALF, HALF)
+    for part in range(3):
+        wt_ref[mp, part] = qkv_ref[part].T.astype(BF)
+        to_peer(part)
+    sm_ref[mp] = small_ref[...]
+    small_copy = send(lambda: sm_ref.at[mp], lambda: sm_ref.at[mp], {"mp": peer})
+    own_proj[...] = proj_ref[...].astype(BF)
+    own_up[...] = up_ref[...].astype(BF)
+    own_down[...] = down_ref[...].astype(BF)
+    keep(wt_ref.at[mp], wt_out.at[mp])
+    keep(own_proj, wp_out.at[mp])
+    keep(own_up, wu_out.at[mp])
+    keep(own_down, wd_out.at[mp])
+
+    def as_column(row):
+        return jnp.broadcast_to(row, (8, row.shape[1])).T[:, 0:1]
+
+    def normalise(group, part, rows):
+        base = group * SEQ + part * HALF
+        norm = layer_norm_rows(rows.astype(F32), gain, shift)[0].astype(BF)
+        norm_ref[span(base, HALF), :] = norm
+        nt_ref[:, pl.ds(pl.multiple_of(base, HALF), HALF)] = norm.T
+
+    def project(side, group):
+        base = pl.multiple_of(group * SEQ, SEQ)
+        at = pl.ds(base, SEQ)
+        own = pl.ds(pl.multiple_of(side * 256, 256), 256)
+        norm = norm_ref[at, :]
+        q_bias, v_bias = sm_ref[side, 1:2, 0:256], sm_ref[side, 2:3, 0:256]
+        scale = LOG2E * HD ** (-0.5)
+        qt_ref[own, at] = ((mm_nt(wt_ref[side, 0], norm) + as_column(q_bias)) * scale).astype(BF)
+        kt_ref[own, at] = mm_nt(wt_ref[side, 1], norm).astype(BF)
+        vt_ref[own, :] = (mm_nt(wt_ref[side, 2], norm) + as_column(v_bias)).astype(BF)
+        k_ref[at, own] = mm_nt(norm, wt_ref[side, 1]).astype(BF)
+        v_ref[at, own] = (mm_nt(norm, wt_ref[side, 2]) + v_bias).astype(BF)
+
+    def attend(side, group, queries, between):
+        base = pl.multiple_of(group * SEQ, SEQ)
+        keys_at, queries_at = pl.ds(base, SEQ), pl.ds(base, queries)
+        bias = bias_ref[group]
+
+        def scores(block, sub):
+            return score_tile(
+                k_ref[keys_at, head_cols(block)], bias, qt_ref[head_rows(block, sub), queries_at], sub
+            )
+
+        s_ref[0, :, :queries] = scores(2 * side, 0)
+
+        def body(step, carry):
+            block = 2 * side + step
+            for sub in range(4):
+                following = (block, sub + 1) if sub < 3 else (2 * side + 1, 0)
+                s_ref[(sub + 1) % 2, :, :queries] = scores(*following)
+                tile = s_ref[sub % 2, :, :queries]
+                top = jnp.max(tile, axis=0, keepdims=True)
+                weights = jnp.exp2(tile - top)
+                rows = head_rows(block, sub)
+                values = jnp.concatenate([vt_ref[rows, :], jnp.ones((16, SEQ), BF)], axis=0)
+                mixed = mm_nn(values, weights.astype(BF))
+                total = mixed[HD : HD + 1]
+                ot_ref[rows, queries_at] = (mixed[:HD] * (1.0 / total)).astype(BF)
+                lse_ref[group, block, sub : sub + 1, :queries] = top + jnp.log2(total)
+
+            @pl.when(step == 0)
+            def _():
+                between()
+
+            return carry
+
+        lax.fori_loop(0, 2, body, 0)
+
+    def nothing():
+        pass
+
+    def unit(side, group, queries, early=nothing, between=nothing):
+        project(side, group)
+        early()
+        attend(side, group, queries, between)
+        at = pl.ds(pl.multiple_of(group * SEQ, SEQ), SEQ)
+        own = pl.ds(pl.multiple_of(side * 256, 256), 256)
+        keep(qt_ref.at[own, at], qt_out.at[own, at])
+        keep(kt_ref.at[own, at], kt_out.at[own, at])
+        keep(ot_ref.at[own, at], ot_out.at[own, at])
+        keep(k_ref.at[at, own], k_out.at[at, own])
+        keep(v_ref.at[at, own], v_out.at[at, own])
+
+    def in_turn(*calls):
+        def run():
+            for call, *indices in calls:
+                for index in indices:
+                    call(index)
+
+        return run
+
+    for group in (1, 2):
+        bias_ref[group] = key_bias((SEQ, 128), mp, count_ref[3 * mp + group - 1], False)
+        for part in range(2):
+            normalise(group, part, x_ref[pl.ds(row_block(2 * group - 1 + part, mp), HALF), :])
+        if group == 1:
+            to_peer(3)
+            to_peer(4)
+    bias_ref[0] = key_bias((SEQ, 128), mp, count_ref[2], True)
+    normalise(0, 0, x_ref[pl.ds(row_block(0, mp), HALF), :])
+    for index in range(3):
+        to_sides(index)
+    to_peer(5)
+    unit(mp, 1, SEQ)
+    in_turn((to_sides, 3, 4), (to_peer, 6))()
+    unit(mp, 2, SEQ, between=in_turn((to_core, 0, 1, 2), (to_sides, 5), (to_peer, 7)))
+    small_copy.wait_recv()
+    keep(sm_ref, sm_out)
+    for index in range(3):
+        arrive(index)
+    keep(wt_ref.at[peer], wt_out.at[peer])
+    rows_copy = send(lambda: x_ref.at[pl.ds(own_half, HALF), :], lambda: other_ref, {"mp": peer})
+    unit(peer, 1, SEQ, early=in_turn((to_sides, 6)), between=in_turn((to_core, 3, 4)))
+    in_turn((to_sides, 7))()
+    unit(peer, 2, SEQ, early=in_turn((to_core, 5)), between=in_turn((to_core, 6)))
+    rows_copy.wait_recv()
+    normalise(0, 1, other_ref[...])
+    keep(nt_ref, nt_out)
+    unit(mp, 0, HALF, between=in_turn((to_core, 7)))
+    unit(peer, 0, HALF)
+    keep(lse_ref, lse_out)
+    for index in range(3, 8):
+        arrive(index)
+    for copy in remote:
+        copy.wait_send()
+    for copy in local:
+        copy.wait()
+
+
+def forward(key_count, w_qkv, w_proj, w_up, w_down, small, patches, vec_params):
+    ext = 3 * SEQ
+    vmem, hbm = pl.BlockSpec(memory_space=pltpu.VMEM), pl.BlockSpec(memory_space=pl.ANY)
+    return pl.pallas_call(
+        forward_kernel,
+        out_shape=[
+            sds((2, 3, 256, 512), BF), sds((2, 256, 512), BF), sds((2, 512, 1024), BF),
+            sds((2, 1024, 512), BF), sds((2, 8, 1024), F32),
+            sds((512, ext), BF), sds((512, ext), BF), sds((512, ext), BF), sds((ext, 512), BF),
+            sds((ext, 512), BF), sds((512, ext), BF), sds((3, 4, 8, SEQ), F32),
+        ],
+        in_specs=[pl.BlockSpec(memory_space=pltpu.SMEM)] + [vmem] * 7,
+        out_specs=[hbm] * 12,
+        scratch_shapes=[
+            pltpu.VMEM((2, 3, 256, 512), BF), pltpu.VMEM((256, 512), BF), pltpu.VMEM((512, 1024), BF),
+            pltpu.VMEM((1024, 512), BF), pltpu.VMEM((2, 8, 1024), F32), pltpu.VMEM((HALF, 512), BF),
+            pltpu.VMEM((ext, 512), BF), pltpu.VMEM((512, ext), BF), pltpu.VMEM((512, ext), BF),
+            pltpu.VMEM((512, ext), BF), pltpu.VMEM((512, SEQ), BF), pltpu.VMEM((ext, 512), BF),
+            pltpu.VMEM((ext, 512), BF), pltpu.VMEM((512, ext), BF), pltpu.VMEM((3, 4, 8, SEQ), F32),
+            pltpu.VMEM((3, SEQ, 128), BF), pltpu.VMEM((2, SEQ, SEQ), F32),
+            pltpu.SemaphoreType.DMA((34,)), pltpu.SemaphoreType.DMA((34,)), pltpu.SemaphoreType.DMA((40,)),
+        ],
+        compiler_params=pltpu.CompilerParams(
+            collective_id=0, has_side_effects=True, vmem_limit_bytes=VMEM_LIMIT
+        ),
+        name="forward",
+    )(key_count, w_qkv, w_proj, w_up, w_down, small, patches, vec_params)
+
+
+def mlp_kernel(
+    x_ref, dy_ref, ot_ref, wp_ref, wu_ref, wd_ref, vec_ref, small_ref,
+    act_ref, dres_ref, dot_ref, gd_ref, gu_ref, gp_ref, vsum_ref, bsum_ref,
+    res_ref, n2_ref, out_ref, dn_ref, hid_ref, dup_ref, dyc_ref, br_ref,
+):
+    step = pl.program_id(0)
+    mp = lax.axis_index("mp")
+    gain, shift = vec_ref[2:3, :], vec_ref[3:4, :]
+    w_proj = wp_ref[...].reshape(512, 512)
+
+    def rows(index):
+        return pl.ds(pl.multiple_of(index * HALF, HALF), HALF)
+
+    @pl.when(step == 0)
+    def _():
+        def body(index, carry):
+            x_rows = x_ref[pl.ds(row_block(index, mp), HALF), :].astype(F32)
+            mixed = ot_ref[:, pl.ds(ext_cols(index), HALF)]
+            resid = x_rows + mm_tn(mixed, w_proj) + vec_ref[4:5, :]
+            res_ref[rows(index), :] = resid
+            n2_ref[rows(index), :] = layer_norm_rows(resid, gain, shift)[0].astype(BF)
+            out_ref[rows(index), :] = resid + vec_ref[5:6, :]
+            dn_ref[rows(index), :] = jnp.zeros((HALF, 512), F32)
+            dyc_ref[rows(index), :] = dy_ref[pl.ds(row_block(index, mp), HALF), :]
+            return carry
+
+        lax.fori_loop(0, 5, body, 0)
+
+    w_up, w_down = wu_ref[0], wd_ref[0]
+    up_bias = small_ref[step // 2, 0:1, pl.ds(pl.multiple_of(lax.rem(step, 2) * 512, 512), 512)]
+
+    def body(index, total):
+        at = rows(index)
+        up_pre = mm_nn(n2_ref[at, :], w_up) + up_bias
+        cumulative = 0.5 * (1.0 + lax.erf(up_pre * (0.5**0.5)))
+        density = jnp.exp(-0.5 * up_pre * up_pre) * 0.3989422804014327
+        hidden = (up_pre * cumulative).astype(BF)
+        hid_ref[at, :] = hidden
+        out_ref[at, :] += mm_nn(hidden, w_down)
+        slope = cumulative + up_pre * density
+        dup = (mm_nt(dyc_ref[at, :], w_down) * slope).astype(BF)
+        dup_ref[at, :] = dup
+        dn_ref[at, :] += mm_nt(dup, w_up)
+        return total + jnp.sum(dup.astype(F32).reshape(HALF // 8, 8, 512), axis=0)
+
+    total = lax.fori_loop(0, 5, body, jnp.zeros((8, 512), F32))
+    bsum_ref[0] = total
+    gd_ref[0] = mm_tn(hid_ref[...], dyc_ref[...]).astype(BF)
+    gu_ref[0] = mm_tn(n2_ref[...], dup_ref[...]).astype(BF)
+
+    @pl.when(step == 3)
+    def _():
+        vsum_ref[...] = jnp.zeros_like(vsum_ref)
+
+        def body(index, carry):
+            at = rows(index)
+            act_ref[pl.ds(row_block(index, mp), HALF), :] = out_ref[at, :].astype(BF)
+            _, unit, inverse = layer_norm_rows(res_ref[at, :], gain, shift)
+            dn = dn_ref[at, :]
+            dy = dyc_ref[at, :].astype(F32)
+            dres = dy + layer_norm_back(dn, unit, inverse, gain)
+            dres_ref[at, :] = dres
+            branch = dres.astype(BF)
+            br_ref[at, :] = branch
+            dot_ref[:, pl.ds(ext_cols(index), HALF)] = mm_nt(w_proj, branch).astype(BF)
+            sums = [dn * unit, dn, branch.astype(F32), dy]
+            for place, value in enumerate(sums):
+                vsum_ref[place] += jnp.sum(value.reshape(HALF // 8, 8, 512), axis=0)
+            return carry
+
+        lax.fori_loop(0, 5, body, 0)
+        mixed = jnp.concatenate([ot_ref[:, 0:HALF], ot_ref[:, SEQ:]], axis=1)
+        gp_ref[...] = mm_nn(mixed, br_ref[...]).astype(BF).reshape(2, 256, 512)
+
+
+def mlp(patches, cotangent, ot, wp, wu, wd, vec_params, small):
+    rows = patches.shape[0]
+    ext = 3 * SEQ
+    up_spec = pl.BlockSpec((1, 512, 512), lambda f: (f // 2, 0, f % 2))
+    down_spec = pl.BlockSpec((1, 512, 512), lambda f: (f // 2, f % 2, 0))
+    return pl.pallas_call(
+        mlp_kernel,
+        grid=(4,),
+        out_shape=[
+            sds((rows, 512), BF), sds((rows, 512), F32), sds((512, ext), BF), sds((2, 1024, 512), BF),
+            sds((2, 512, 1024), BF), sds((2, 256, 512), BF), sds((4, 8, 512), F32), sds((4, 8, 512), F32),
+        ],
+        in_specs=[
+            full_spec((rows, 512)), full_spec((rows, 512)), full_spec((512, ext)), full_spec(wp.shape),
+            up_spec, down_spec, full_spec(vec_params.shape), full_spec(small.shape),
+        ],
+        out_specs=[
+            full_spec((rows, 512)), full_spec((rows, 512)), full_spec((512, ext)), down_spec, up_spec,
+            full_spec((2, 256, 512)), full_spec((4, 8, 512)), pl.BlockSpec((1, 8, 512), lambda f: (f, 0, 0)),
+        ],
+        scratch_shapes=[
+            pltpu.VMEM((rows, 512), F32), pltpu.VMEM((rows, 512), BF), pltpu.VMEM((rows, 512), F32),
+            pltpu.VMEM((rows, 512), F32), pltpu.VMEM((rows, 512), BF), pltpu.VMEM((rows, 512), BF),
+            pltpu.VMEM((rows, 512), BF), pltpu.VMEM((rows, 512), BF),
+        ],
+        compiler_params=pltpu.CompilerParams(vmem_limit_bytes=VMEM_LIMIT),
+        name="mlp",
+    )(patches, cotangent, ot, wp, wu, wd, vec_params, small)
+
+
+SCHEDULE = (
+    (
+        ("F", 0, 0), ("F", 1, 0), ("F", 2, 0), ("F", 3, 0), ("F", 4, 0), ("O", 0, 0), ("O", 1, 0),
+        ("O", 2, 0), ("O", 3, 0), ("O", 4, 0),
+    ),
+    (
+        ("F", 0, 1),
+    ),
+    (
+    ),
+    (
+        ("F", 1, 1),
+    ),
+    (
+        ("O", 0, 1),
+    ),
+    (
+    ),
+    (
+        ("F", 2, 1),
+    ),
+    (
+    ),
+    (
+        ("F", 5, 0), ("O", 0, 2), ("O", 1, 1),
+    ),
+    (
+        ("F", 3, 1),
+    ),
+    (
+    ),
+    (
+        ("F", 4, 1), ("O", 0, 3), ("O", 2, 1),
+    ),
+    (
+        ("F", 6, 0), ("O", 1, 2),
+    ),
+    (
+        ("F", 5, 1), ("O", 0, 4), ("O", 2, 2),
+    ),
+    (
+        ("O", 3, 1),
+    ),
+    (
+        ("F", 6, 1), ("O", 1, 3),
+    ),
+    (
+        ("O", 0, 5), ("O", 2, 3), ("O", 4, 1), ("O", 5, 0),
+    ),
+    (
+        ("O", 1, 4),
+    ),
+    (
+        ("O", 3, 2), ("O", 5, 1),
+    ),
+    (
+        ("O", 0, 6), ("O", 4, 2),
+    ),
+    (
+        ("O", 1, 5), ("O", 6, 0),
+    ),
+    (
+    ),
+    (
+        ("O", 2, 4),
+    ),
+    (
+        ("O", 0, 7), ("O", 3, 3), ("O", 6, 1),
+    ),
+    (
+    ),
+    (
+        ("O", 0, 8), ("O", 1, 6), ("O", 4, 3), ("O", 5, 2),
+    ),
+    (
+        ("O", 2, 5), ("O", 6, 2), ("O", 3, 4), ("O", 4, 4), ("small", 0), ("O", 5, 3), ("O", 1, 7),
+        ("O", 2, 6), ("small", 1), ("O", 6, 3), ("O", 1, 8), ("small", 2), ("O", 3, 5), ("O", 4, 5),
+        ("small", 3), ("O", 5, 4), ("O", 2, 7), ("O", 6, 4), "square", ("small", 4), ("O", 2, 8), ("O", 3, 6),
+        ("O", 4, 6), ("square", 0), ("O", 5, 5), ("square", 1), ("O", 6, 5), ("O", 3, 7), ("square", 2),
+        ("O", 5, 6), ("O", 6, 6), ("O", 4, 7), ("O", 3, 8), ("square", 3), ("O", 4, 8), ("square", 4),
+        ("O", 5, 7), ("O", 5, 8), ("O", 6, 7), ("O", 6, 8),
+    ),
+)
+
+
+class Transfers:
+    def __init__(self, send_sem, recv_sem):
+        self.sems = (send_sem, recv_sem)
+        self.all = {}
+
+    def make(self, key):
+        index, src, dst, target = self.all[key]
+        return pltpu.make_async_remote_copy(
+            src_ref=src(), dst_ref=dst(), send_sem=self.sems[0].at[index], recv_sem=self.sems[1].at[index],
+            device_id=target, device_id_type=MESH,
+        )
+
+    def plan(self, key, src, dst, target):
+        self.all[key] = (len(self.all), src, dst, target)
+
+    def start(self, key, *views):
+        if views:
+            self.plan(key, *views)
+        self.make(key).start()
+
+    def arrive(self, key):
+        self.make(key).wait_recv()
+
+    def finish(self):
+        for key in self.all:
+            self.make(key).wait_send()
+
+
+class Loads:
+    def __init__(self, sem):
+        self.sem = sem
+        self.all = {}
+
+    def make(self, key):
+        index, src, dst = self.all[key]
+        return pltpu.make_async_copy(src(), dst(), self.sem.at[index])
+
+    def plan(self, key, src, dst):
+        self.all[key] = (len(self.all), src, dst)
+
+    def start(self, key, *views):
+        if views:
+            self.plan(key, *views)
+        self.make(key).start()
+
+    def wait(self, key):
+        self.make(key).wait()
+
+
+def cut(ref, start, size):
+    rows = pl.ds(pl.multiple_of(start, 16), size)
+    return ref.at[:, rows, :] if len(ref.shape) == 3 else ref.at[rows, :]
+
+
+PIECES = ((512, 512), (512, 512), (512, 512), (512, 512), (256, 512), (3, 512, 128), (3, 512, 128))
+
+
+def piece_rows(index, size):
+    return (*PIECES[index][:-2], PIECES[index][-2] // size, PIECES[index][-1])
+
+
+def backward_kernel(
+    count_ref, qt_in, kt_in, dot_in, ot_in, k_in, v_in, lse_ref, nt_in, wt_in,
+    gd_in, gu_in, gp_in, x_in, dres_in, vec_ref, two_ref, up_sum_ref,
+    grad_out, down_out, up_out, proj_out, qkv_out, small_out, norm_out,
+    qt_ref, kt_ref, dot_ref, ot_ref, k_ref, v_ref, nt_ref, wt_ref, x_ref, dres_ref,
+    shared_ref, grads_ref, acc_ref, bias_ref, s_ref, dp_ref, g_ref, bsum_ref,
+    far_send, far_recv, small_bufs, square_bufs, *rest,
+):
+    buffers, (send_sem, recv_sem, local_sem) = rest[:-3], rest[-3:]
+    dp, mp = lax.axis_index("dp"), lax.axis_index("mp")
+    peer = 1 - mp
+    core, x_side, z_near, z_far = partners(dp)
+    targets = [{"dp": core}, {"mp": peer}, {"dp": x_side}, {"dp": z_near}, {"dp": z_far}]
+    bits = [lax.rem(dp, 2), None] + [lax.rem(lax.div(dp, size), 2) for size in (2, 4, 8)]
+    sent, loads = Transfers(send_sem, recv_sem), Loads(local_sem)
+
+    def block_at(place):
+        return 2 * jnp.where(place < 2, peer, mp) + lax.rem(place, 2)
+
+    def source(index, side):
+        if index < 4:
+            lanes = slice(index // 2 * 512, index // 2 * 512 + 512)
+            return gu_in.at[side, :, lanes] if index % 2 else gd_in.at[side, lanes, :]
+        if index == 4:
+            return gp_in.at[side]
+        return g_ref.at[index - 5 + (0 if side is peer else 2)]
+
+    def result(index):
+        if index < 4:
+            lanes = slice(index // 2 * 512, index // 2 * 512 + 512)
+            return up_out.at[:, lanes] if index % 2 else down_out.at[lanes, :]
+        if index == 4:
+            return proj_out
+        return qkv_out.at[:, :, slice((index - 5) * 128, (index - 5) * 128 + 128)]
+
+    def piece_buffers(index):
+        return buffers[9 * index : 9 * index + 9]
+
+    def share(total, upto):
+        start, size = 0, total
+        for stage in (0, 2, 3, 4):
+            if stage <= upto:
+                size //= 2
+                start = start + bits[stage] * size
+        return start, size
+
+    for place in range(4):
+        block = block_at(place)
+        rows = pl.ds(pl.multiple_of(block * 128, 128), 128)
+        for name, src, dst in (
+            ("qt", qt_in, qt_ref), ("kt", kt_in, kt_ref), ("dot", dot_in, dot_ref), ("ot", ot_in, ot_ref)
+        ):
+            loads.start(
+                (name, place), lambda src=src, rows=rows: src.at[rows, :],
+                lambda dst=dst, place=place: dst.at[place],
+            )
+        for name, src, dst in (("k", k_in, k_ref), ("v", v_in, v_ref)):
+            loads.start(
+                (name, place), lambda src=src, rows=rows: src.at[:, rows],
+                lambda dst=dst, place=place: dst.at[place],
+            )
+        if place == 0:
+            loads.start("wt", lambda: wt_in, lambda: wt_ref)
+    loads.start("nt", lambda: nt_in, lambda: nt_ref)
+    for index in range(5):
+        total = PIECES[index][-2]
+        for side, slot in ((peer, 0), (mp, 2)):
+            loads.start(
+                ("kept", index, slot),
+                lambda index=index, side=side, total=total: cut(
+                    source(index, side), bits[0] * (total // 2), total // 2
+                ),
+                lambda index=index, slot=slot: piece_buffers(index)[slot],
+            )
+    loads.start("x", lambda: x_in, lambda: x_ref)
+    loads.start("dres", lambda: dres_in, lambda: dres_ref)
+    greet(targets)
+
+    def plan_piece(index):
+        total = PIECES[index][-2]
+        half = total // 2
+        kept = bits[0] * half
+        fore, fore_core, own, own_core, own_peer, own_x, own_near, own_far, out = piece_buffers(index)
+        away = (1 - bits[0]) * half
+        sent.plan(("F", index, 0), lambda: cut(source(index, peer), away, half), lambda: fore_core, targets[0])
+        sent.plan(("F", index, 1), lambda: fore, lambda: own_peer, targets[1])
+        sent.plan(("O", index, 0), lambda: cut(source(index, mp), away, half), lambda: own_core, targets[0])
+        for stage, landing in ((1, own_x), (2, own_near), (3, own_far)):
+            level = stage + 1
+            outer, outer_size = share(total, level - 1)
+            size = outer_size // 2
+            start = outer - kept + (1 - bits[level]) * size
+            sent.plan(
+                ("O", index, stage), lambda start=start, size=size: cut(own, start, size),
+                lambda landing=landing: landing, targets[level],
+            )
+        for stage, level in ((4, 4), (5, 3), (6, 2), (7, 0)):
+            start, size = share(total, level)
+            where = lambda start=start, size=size: cut(out, start, size)
+            sent.plan(("O", index, stage), where, where, targets[level])
+        loads.plan(("out", index), lambda: out, lambda: result(index))
+
+    def event(kind, index, stage):
+        total = PIECES[index][-2]
+        half = total // 2
+        kept = bits[0] * half
+        fore, fore_core, own, own_core, own_peer, own_x, own_near, own_far, out = piece_buffers(index)
+        if stage > 0:
+            sent.arrive((kind, index, stage - 1))
+        if kind == "F" and stage == 1:
+            if index < 5:
+                loads.wait(("kept", index, 0))
+                fore[...] += fore_core[...]
+            else:
+                fore[...] = cut(source(index, peer), kept, half)[...] + fore_core[...]
+        elif stage == 1:
+            sent.arrive(("F", index, 1))
+            if index < 5:
+                loads.wait(("kept", index, 2))
+                base = own[...]
+            else:
+                base = cut(source(index, mp), kept, half)[...]
+            own[...] = (base.astype(F32) + own_core[...].astype(F32) + own_peer[...].astype(F32)).astype(BF)
+        elif 2 <= stage <= 4:
+            start, size = share(total, stage)
+            landing = (own_x, own_near, own_far)[stage - 2]
+            value = cut(own, start - kept, size)[...] + landing[...]
+            if stage < 4:
+                cut(own, start - kept, size)[...] = value
+            else:
+                cut(out, start, size)[...] = value
+                wide = value.astype(F32)
+                square = jnp.sum((wide * wide).reshape(-1, 8, wide.shape[-1]), axis=0)
+                folded = square[:, 0:128]
+                for lane in range(1, square.shape[1] // 128):
+                    folded = folded + square[:, lane * 128 : lane * 128 + 128]
+                square_bufs[0, 0] += folded
+        if stage == 8:
+            loads.start(("out", index))
+        else:
+            sent.start((kind, index, stage))
+
+    for index in range(7):
+        plan_piece(index)
+
+    def run(events):
+        for item in events:
+            event(*item)
+
+    square_bufs[0, 0] = jnp.zeros((8, 128), F32)
+    bias_ref[0] = key_bias((SEQ, 128), mp, count_ref[2], True)
+    for group in (1, 2):
+        bias_ref[group] = key_bias((SEQ, 128), mp, count_ref[3 * mp + group - 1], False)
+    run(SCHEDULE[0])
+
+    def heads(place, group, queries, out, out_base, between):
+        block = block_at(place)
+        base = pl.multiple_of(group * SEQ, SEQ)
+        keys_at, queries_at = pl.ds(base, SEQ), pl.ds(base, queries)
+        out_keys = pl.ds(out_base, SEQ)
+        out_queries = pl.ds(out_base, queries)
+        bias = bias_ref[group]
+
+        def tiles(sub):
+            own = slice(sub * HD, sub * HD + HD)
+            s_ref[sub % 2, :, :queries] = score_tile(
+                k_ref[place, keys_at, :], bias, qt_ref[place, own, queries_at], sub
+            )
+            dp_ref[sub % 2, :, :queries] = mm_nn(
+                v_ref[place, keys_at, :], widen_plain(dot_ref[place, own, queries_at], sub)
+            )
+
+        tiles(0)
+        for sub in range(4):
+            if sub < 3:
+                tiles(sub + 1)
+            own = slice(sub * HD, sub * HD + HD)
+            q_rows, do_rows = qt_ref[place, own, queries_at], dot_ref[place, own, queries_at]
+            delta = jnp.sum(
+                do_rows.astype(F32) * ot_ref[place, own, queries_at].astype(F32), axis=0, keepdims=True
+            )
+            probs = jnp.exp2(
+                s_ref[sub % 2, :, :queries] - lse_ref[group, block, sub : sub + 1, :queries]
+            )
+            draw = (probs * (dp_ref[sub % 2, :, :queries] - delta)).astype(BF)
+            dq = mm_nn(kt_ref[place, own, keys_at], draw) * (HD ** (-0.5))
+            out[own, out_queries] = dq.astype(BF)
+            dk = mm_nt(q_rows, draw) * (1.0 / LOG2E)
+            out[128 + sub * HD : 160 + sub * HD, out_keys] = dk.astype(BF)
+            dv = mm_nt(do_rows, probs.astype(BF))
+            out[256 + sub * HD : 288 + sub * HD, out_keys] = dv.astype(BF)
+            if sub == 1:
+                between()
+
+    def weights_of(place):
+        block = block_at(place)
+        side, part = lax.div(block, 2), lax.rem(block, 2)
+        return wt_ref[side, :, pl.ds(pl.multiple_of(part * 128, 128), 128), :].reshape(384, 512)
+
+    acc_ref[...] = jnp.zeros_like(acc_ref)
+    for place in range(4):
+        for name in ("qt", "kt", "dot", "ot", "k", "v"):
+            loads.wait((name, place))
+        if place == 0:
+            loads.wait("wt")
+        shared_ref[place, 0:128, HALF:SEQ] = jnp.zeros((128, HALF), BF)
+
+    def shared_step(place, carry):
+        heads(place, 0, HALF, shared_ref.at[place], 0, lambda: None)
+        acc_ref[0:SEQ] += mm_tn(shared_ref[place], weights_of(place))
+        for turn in range(4):
+
+            @pl.when(place == turn)
+            def _():
+                run(SCHEDULE[1 + turn])
+
+        return carry
+
+    lax.fori_loop(0, 4, shared_step, 0)
+    far_send[...] = acc_ref[HALF:SEQ].astype(BF)
+    sent.start("far", lambda: far_send, lambda: far_recv, targets[1])
+    loads.wait("nt")
+
+    def main_step(step, carry):
+        place, group = lax.div(step, 2), 1 + lax.rem(step, 2)
+
+        def pump(first):
+            for turn in range(8):
+
+                @pl.when(step == turn)
+                def _():
+                    run(SCHEDULE[first + 2 * turn])
+
+        out_base = pl.multiple_of((group - 1) * SEQ, SEQ)
+        heads(place, group, SEQ, grads_ref, out_base, lambda: pump(5))
+
+        @pl.when(group == 2)
+        def _():
+            for part in range(3):
+                rows = slice(part * 128, part * 128 + 128)
+                total = mm_nt(nt_ref[:, 0:SEQ], shared_ref[place, rows, :])
+                total += mm_nt(nt_ref[:, SEQ:], grads_ref[rows, :])
+                g_ref[place, part] = total.astype(BF)
+            ones = jnp.ones((8, 2 * SEQ), BF)
+            bsum_ref[place] = mm_nt(ones[:, :SEQ], shared_ref[place]) + mm_nt(ones, grads_ref[...])
+            acc_ref[SEQ:] += mm_tn(grads_ref[...], weights_of(place))
+
+        pump(6)
+        return carry
+
+    lax.fori_loop(0, 8, main_step, 0)
+
+    gain, shift = vec_ref[0:1, :], vec_ref[1:2, :]
+    loads.wait("x")
+    loads.wait("dres")
+    run(SCHEDULE[21])
+
+    def finish_rows(index, dn, sums):
+        at = pl.ds(pl.multiple_of(index * HALF, HALF), HALF)
+        place = pl.ds(row_block(index, mp), HALF)
+        _, unit, inverse = layer_norm_rows(x_ref[place, :].astype(F32), gain, shift)
+        grad_out[place, :] = dres_ref[at, :] + layer_norm_back(dn, unit, inverse, gain)
+        folded = [jnp.sum(value.reshape(HALF // 8, 8, 512), axis=0) for value in (dn * unit, dn)]
+        return sums[0] + folded[0], sums[1] + folded[1]
+
+    def finish_step(index, sums):
+        sums = finish_rows(
+            index, acc_ref[pl.ds(pl.multiple_of(HALF * index + HALF, HALF), HALF), :], sums
+        )
+        for turn in range(1, 5):
+
+            @pl.when(index == turn)
+            def _():
+                run(SCHEDULE[21 + turn])
+
+        return sums
+
+    zero = jnp.zeros((8, 512), F32)
+    sums = lax.fori_loop(1, 5, finish_step, (zero, zero))
+    sent.arrive("far")
+    sums = finish_rows(0, acc_ref[0:HALF] + far_recv[...].astype(F32), sums)
+
+    def small_row(place, value):
+        small_bufs[0, 0, place : place + 1, :] = value
+
+    small_bufs[0, 0] = jnp.zeros((16, 512), F32)
+    for place in range(4):
+        lanes = pl.ds(pl.multiple_of(block_at(place) * 128, 128), 128)
+        small_bufs[0, 0, 0:1, lanes] = bsum_ref[place, 0:1, 0:128]
+        small_bufs[0, 0, 1:2, lanes] = bsum_ref[place, 0:1, 256:384]
+        small_row(2 + place, jnp.sum(up_sum_ref[place], axis=0, keepdims=True))
+        small_row(8 + place, jnp.sum(two_ref[place], axis=0, keepdims=True))
+    for place in range(2):
+        small_row(6 + place, jnp.sum(sums[place], axis=0, keepdims=True))
+
+    def small_start(stage):
+        sent.start(
+            ("small", stage), lambda: small_bufs.at[0, stage], lambda: small_bufs.at[1, stage], targets[stage]
+        )
+
+    def small_end(stage):
+        sent.arrive(("small", stage))
+        value = small_bufs[0, stage] + small_bufs[1, stage]
+        if stage < 4:
+            small_bufs[0, stage + 1] = value
+            small_start(stage + 1)
+        else:
+            small_out[...] = value
+
+    order = (4, 3, 2, 0, 1)
+
+    def square_start(place):
+        sent.start(
+            ("square", place), lambda: square_bufs.at[0, place], lambda: square_bufs.at[1, place],
+            targets[order[place]],
+        )
+
+    def square_end(place):
+        sent.arrive(("square", place))
+        value = square_bufs[0, place] + square_bufs[1, place]
+        if place < 4:
+            square_bufs[0, place + 1] = value
+            square_start(place + 1)
+        else:
+            total = jnp.sum(small_out[...] * small_out[...]) + jnp.sum(value)
+            norm_out[...] = jnp.sqrt(jnp.full((8, 128), total, F32))
+
+    small_start(0)
+    for item in SCHEDULE[26]:
+        if item == "square":
+            square_start(0)
+        elif item[0] == "small":
+            small_end(item[1])
+        elif item[0] == "square":
+            square_end(item[1])
+        else:
+            event(*item)
+    sent.finish()
+    for index in range(7):
+        loads.wait(("out", index))
+
+
+def backward(key_count, qt, kt, dot, ot, k, v, lse, nt, wt, gd, gu, gp, patches, dres, vec_params, two, ups):
+    ext, rows = 3 * SEQ, patches.shape[0]
+    vmem, hbm = pl.BlockSpec(memory_space=pltpu.VMEM), pl.BlockSpec(memory_space=pl.ANY)
+    buffers = []
+    for index in range(7):
+        for size in (2, 2, 2, 2, 2, 4, 8, 16, 1):
+            buffers.append(pltpu.VMEM(piece_rows(index, size), BF))
+    return pl.pallas_call(
+        backward_kernel,
+        out_shape=[
+            sds((rows, 512), F32), sds((1024, 512), BF), sds((512, 1024), BF), sds((256, 512), BF),
+            sds((3, 512, 256), BF), sds((16, 512), F32), sds((8, 128), F32),
+        ],
+        in_specs=[pl.BlockSpec(memory_space=pltpu.SMEM)] + [hbm] * 6 + [vmem] + [hbm] * 7 + [vmem] * 3,
+        out_specs=[vmem] + [hbm] * 4 + [vmem] * 2,
+        scratch_shapes=[
+            *[pltpu.VMEM((4, 128, ext), BF)] * 4, *[pltpu.VMEM((4, ext, 128), BF)] * 2,
+            pltpu.VMEM((512, ext), BF), pltpu.VMEM((2, 3, 256, 512), BF), pltpu.VMEM((rows, 512), BF),
+            pltpu.VMEM((rows, 512), F32), pltpu.VMEM((4, 384, SEQ), BF), pltpu.VMEM((384, 2 * SEQ), BF),
+            pltpu.VMEM((ext, 512), F32), pltpu.VMEM((3, SEQ, 128), BF), pltpu.VMEM((2, SEQ, SEQ), F32),
+            pltpu.VMEM((2, SEQ, SEQ), F32), pltpu.VMEM((4, 3, 512, 128), BF), pltpu.VMEM((4, 8, 384), F32),
+            pltpu.VMEM((HALF, 512), BF), pltpu.VMEM((HALF, 512), BF), pltpu.VMEM((2, 5, 16, 512), F32),
+            pltpu.VMEM((2, 5, 8, 128), F32), *buffers, pltpu.SemaphoreType.DMA((81,)),
+            pltpu.SemaphoreType.DMA((81,)), pltpu.SemaphoreType.DMA((48,)),
+        ],
+        compiler_params=pltpu.CompilerParams(
+            collective_id=1, has_side_effects=True, vmem_limit_bytes=VMEM_LIMIT
+        ),
+        name="backward",
+    )(key_count, qt, kt, dot, ot, k, v, lse, nt, wt, gd, gu, gp, patches, dres, vec_params, two, ups)
+
+
+def adam_kernel(norm_ref, *refs):
+    factor = jnp.minimum(1.0, CLIP_NORM / (norm_ref[0:1, 0:1] + 1e-06))
+    for index in range(4):
+        weight_ref, one_ref, two_ref, grad_ref = refs[4 * index : 4 * index + 4]
+        outs = refs[16 + 3 * index : 19 + 3 * index]
+        results = adam_update(
+            weight_ref[...], grad_ref[...].astype(F32) * factor, one_ref[...], two_ref[...],
+            MATRIX_RATE, DECAY_RATE,
+        )
+        for out, value in zip(outs, results):
+            out[...] = value
+
+
+def adam_matrices(norm, groups):
+    steps = 8
+    in_specs, out_specs, out_shape, args = [full_spec((8, 128))], [], [], [norm]
+    for group in groups:
+        rows, width = group[0].shape
+        spec = pl.BlockSpec((rows // steps, width), lambda i: (i, 0))
+        in_specs += [spec] * 4
+        out_specs += [spec] * 3
+        out_shape += [sds((rows, width), F32)] * 3
+        args += list(group)
+    outs = pl.pallas_call(
+        adam_kernel,
+        grid=(steps,),
+        out_shape=out_shape,
+        in_specs=in_specs,
+        out_specs=out_specs,
+        compiler_params=pltpu.CompilerParams(vmem_limit_bytes=VMEM_LIMIT),
+        name="adam_matrices",
+    )(*args)
+    return [outs[3 * index : 3 * index + 3] for index in range(len(groups))]
+
+
+IN_SPECS = (
             P(("dp", "mp"), None),
             P(("dp", "mp"), None),
             P("dp"),
@@ -310,8 +1314,8 @@
             P("mp"),
             P(),
             P(),
-        ),
-        out_specs=(
+        )
+OUT_SPECS = (
             P(("dp", "mp"), None),
             P(("dp", "mp"), None),
             P(),
@@ -336,6 +1340,61 @@
             P(),
             P(),
             P(),
-        ),
-        check_vma=False,
-    )
+        )
+
+
+def paired(
+    patches, cotangent, key_count, w_qkv, w_proj, w_up, w_down, qv_bias, up_bias, vec_params,
+    first_qkv, second_qkv, first_proj, second_proj, first_up, second_up, first_down, second_down,
+    first_qv_bias, second_qv_bias, first_up_bias, second_up_bias, first_vec, second_vec,
+):
+    mp = lax.axis_index("mp")
+    small = jnp.concatenate(
+        [up_bias[None, :], jnp.pad(qv_bias, ((0, 0), (0, 768))), jnp.zeros((5, 1024), F32)], axis=0
+    )
+    wt, wp, wu, wd, small_all, nt, qt, kt, k, v, ot, lse = forward(
+        key_count, w_qkv, w_proj, w_up, w_down, small, patches, vec_params
+    )
+    activations, dres, dot, g_down, g_up, g_proj, vsum_two, up_sums = mlp(
+        patches, cotangent, ot, wp, wu, wd, vec_params, small_all
+    )
+    input_grad, down, up, proj, qkv, small_total, norm = backward(
+        key_count, qt, kt, dot, ot, k, v, lse, nt, wt, g_down, g_up, g_proj, patches, dres, vec_params,
+        vsum_two, up_sums,
+    )
+    qkv = qkv.reshape(1536, 256)
+    flat = lambda array: array.reshape(-1, array.shape[-1])
+    groups = [
+        (flat(w_qkv), flat(first_qkv), flat(second_qkv), qkv),
+        (w_proj, first_proj, second_proj, proj),
+        (w_up, first_up, second_up, up),
+        (w_down, first_down, second_down, down),
+    ]
+    new_qkv, new_proj, new_up, new_down = adam_matrices(norm, groups)
+    grad_norm = norm[0, 0]
+    factor = jnp.minimum(1.0, CLIP_NORM / (grad_norm + 1e-06))
+    qv_total = lax.dynamic_slice_in_dim(small_total[0:2], mp * 256, 256, 1)
+    up_total = lax.dynamic_slice_in_dim(small_total[2:6].reshape(-1), mp * 1024, 1024, 0)
+    new_qvb = adam_update(qv_bias, qv_total * factor, first_qv_bias, second_qv_bias, VECTOR_RATE, 0.0)
+    new_upb = adam_update(up_bias, up_total * factor, first_up_bias, second_up_bias, VECTOR_RATE, 0.0)
+    new_vec = adam_update(
+        vec_params, small_total[6:12] * factor, first_vec, second_vec, VECTOR_RATE, 0.0
+    )
+    return (
+        activations, input_grad, grad_norm, *[array.reshape(w_qkv.shape) for array in new_qkv],
+        *new_proj, *new_up, *new_down, *new_qvb, *new_upb, *new_vec,
+    )
+
+
+def fits_pairs(mesh, args):
+    if dict(mesh.shape) != {"dp": 16, "mp": 2}:
+        return False
+    return args[0].shape == (40960, 512) and args[2].shape == (80,)
+
+
+def solution(mesh):
+    def run(*args):
+        body = paired if fits_pairs(mesh, args) else local
+        return jax.shard_map(body, mesh=mesh, in_specs=IN_SPECS, out_specs=OUT_SPECS, check_vma=False)(*args)
+
+    return run

time: 961 us -> 194 us (0.20); the launches traced: 943 us -> 194 us
  waiting for transfers between devices: 433 us -> 0 us
  matrix products: 263 us -> 0 us
  Pallas kernels: 0 us -> 186 us
  other arithmetic: 89.4 us -> 3.27 us
  local copies, waits for them, and re-layouts: 73.1 us -> 2.82 us
  blocking collectives: 62.7 us -> 0 us
  between operations: 21.8 us -> 1.52 us
    psum x4 -> x0, waiting for transfers between devices: 386 us -> none  [the longest x1 130 us: local(): resid_all = whole_rows + lax.psum(proj_part, 'mp') + proj_shift]
    dot_general x18 -> x0, matrix products: 263 us -> none  [the longest x1 54 us: attend_backward(): jnp.einsum('shqk,skhe->sqhe', raw_grad, key_rows, preferred_element_type=...]
    pallas_call x0 -> x4, Pallas kernels: none -> 186 us  [the longest x1 92.2 us: backward(): pl.pallas_call(backward_kernel, out_shape=[sds((rows, 512), F32), sds((10...]
    psum x2 -> x0, blocking collectives: 62.7 us -> none  [the longest x1 56.9 us: local(): lax.psum(vec_grad.astype(jnp.bfloat16), 'dp').astype(jnp.float32)]
    reduce_sum x19 -> x0, other arithmetic: 54.3 us -> none  [the longest x1 17.9 us: local(): jnp.sum(jnp.exp(scores - top_score), axis=-1, keepdims=True)]
    all_gather x2 -> x0, waiting for transfers between devices: 45.4 us -> none  [the longest x1 39.6 us: local(): lax.all_gather(patches, 'mp', axis=0, tiled=True)]
    unnamed x131 -> x25, local copies, waits for them, and re-layouts: 25 us -> 1.56 us
    convert_element_type x4 -> x0, other arithmetic: 15.5 us -> none  [the longest x1 6.47 us: local(): branch_low = resid_all_grad.astype(jnp.bfloat16)]
  transfers between devices with their start and end apart: 6 -> 0, of which waited for: 6 -> 0; matrix products, arithmetic and copies ran while one was open for 9% -> 0% of each run, Pallas kernels for 0% -> 0%
where the time goes in v2:
time: 194 us
  Pallas kernels  186 us (96%)
  other arithmetic  3.27 us (2%)
  local copies, waits for them, and re-layouts  2.82 us (1%)
    pallas_call x1, Pallas kernels, backward(): pl.pallas_call(backward_kernel, out_shape=[sds((rows, 512), F32), sds((10...  92.2 us
    pallas_call x1, Pallas kernels, mlp(): pl.pallas_call(mlp_kernel, grid=(4,), out_shape=[sds((rows, 512), BF), sd...  38.6 us
    pallas_call x1, Pallas kernels, forward(): pl.pallas_call(forward_kernel, out_shape=[sds((2, 3, 256, 512), BF), sds(...  38 us
    pallas_call x1, Pallas kernels, adam_matrices(): pl.pallas_call(adam_kernel, grid=(steps,), out_shape=out_shape, in_specs=...  17.1 us

profile of v2, /device:TPU:1, one launch (start us, length us, event | category | flops | bytes accessed | tf_op | source)
XLA Modules:
  0.0 193.5 jit_solution(14230848513318069281)
XLA Ops:
  0.7 0.1 pad.7.clone
  0.7 1.4 fusion.small_ref
  2.1 38.0 %forward.1 = (bf16[2,3,256,512]{3,2,1,0:T(8,128)(2,1)}, bf16[2,256,512]{2,1,0:T(8,128)(2,1)}, bf16[2,512,1024]{2,1,0:T(8,128)(2,1)}, bf16[2,1024,512]{2,1,0:T(8,...) custom-call(s32[5]{0:T(128)} %count_ref.3, ...), custom_call_target="tpu_custom_call" | custom-call | tf_op jit(solution)/shard_map/forward/pallas_call | solution.py:606
  40.1 38.6 %mlp.1 = (bf16[1280,512]{1,0:T(8,128)(2,1)}, f32[1280,512]{1,0:T(8,128)}, bf16[512,1536]{1,0:T(8,128)(2,1)}, bf16[2,1024,512]{2,1,0:T(8,128)(2,1)}, bf16[2,512,1...) custom-call(bf16[1280,512]{1,0:T(8,128)(2,1)} %x_in.1, ...), custom_call_target="tpu_custom_call" | custom-call | tf_op jit(solution)/shard_map/mlp/pallas_call | solution.py:712
  78.7 92.2 %backward.1 = (f32[1280,512]{1,0:T(8,128)}, bf16[1024,512]{1,0:T(8,128)(2,1)}, bf16[512,1024]{1,0:T(8,128)(2,1)}, bf16[256,512]{1,0:T(8,128)(2,1)}, bf16[3,512,2...) custom-call(s32[5]{0:T(128)} %count_ref.3, bf16[512,1536]{1,0:T(8,128)(2,1)} %get-tuple-element.69.qt_in, ...), custom_call_target="tpu_custom_call" | custom-call | tf_op jit(solution)/shard_map/backward/pallas_call | solution.py:1232
  170.9 1.2 slice.12
  172.1 0.0 copy-start.6
  172.1 0.0 copy-start.9
  172.1 0.0 copy-start.10
  172.1 0.0 copy-start.5
  172.1 0.0 copy-start.7
  172.1 0.0 copy-start.8
  172.2 0.0 copy-start.1
  172.2 0.0 copy-start.3
  172.2 0.0 copy-start.4
  172.2 0.0 copy-start
  172.2 17.1 %adam_matrices.1 = (f32[1536,256]{1,0:T(8,128)}, f32[1536,256]{1,0:T(8,128)}, f32[1536,256]{1,0:T(8,128)}, f32[256,512]{1,0:T(8,128)}, f32[256,512]{1,0:T(8,128)...) custom-call(f32[8,128]{1,0:T(8,128)} %get-tuple-element.84.norm_ref,, ...), custom_call_target="tpu_custom_call" | custom-call | tf_op jit(solution)/shard_map/adam_matrices/pallas_call | solution.py:1280
  190.0 0.0 copy-done.2
  190.0 0.0 copy-done.6
  190.1 0.0 copy-done.9
  190.1 0.0 copy-done.10
  190.1 0.6 multiply_subtract_fusion.2
  190.7 0.0 copy-done.5
  190.7 0.0 copy-done.7
  190.7 0.0 copy-done.8
  190.7 0.6 multiply_subtract_fusion.1
  191.4 0.0 copy-done.1
  191.4 0.0 copy-done.3
  191.4 0.0 copy-done.4
  191.4 0.6 multiply_subtract_fusion
  192.0 0.0 copy-done
  192.0 1.5 copy.50
  (5 shorter events, 0.0 us)
Async XLA Ops:
  172.1 17.9 %copy-start.2 = (f32[16,512]{1,0:T(8,128)S(1)}, f32[16,512]{1,0:T(8,128)}, u32[]{:S(2)}) copy-start(f32[16,512]{1,0:T(8,128)} %get-tuple-element.101) | copy-start | bytes 98308
  172.1 17.9 %copy-start.6 = (f32[2,256]{1,0:T(2,128)S(1)}, f32[2,256]{1,0:T(2,128)}, u32[]{:S(2)}) copy-start(f32[2,256]{1,0:T(2,128)} %param.31) | copy-start | bytes 6148
  172.1 17.9 %copy-start.9 = (f32[2,256]{1,0:T(2,128)S(1)}, f32[2,256]{1,0:T(2,128)}, u32[]{:S(2)}) copy-start(f32[2,256]{1,0:T(2,128)} %param.42) | copy-start | bytes 6148
  172.1 17.9 %copy-start.10 = (f32[2,256]{1,0:T(2,128)S(1)}, f32[2,256]{1,0:T(2,128)}, u32[]{:S(2)}) copy-start(f32[2,256]{1,0:T(2,128)} %param.43) | copy-start | bytes 6148
  172.1 18.6 %copy-start.5 = (f32[1024]{0:T(1024)S(1)}, f32[1024]{0:T(1024)}, u32[]{:S(2)}) copy-start(f32[1024]{0:T(1024)} %param.32) | copy-start | bytes 12292
  172.1 18.6 %copy-start.7 = (f32[1024]{0:T(1024)S(1)}, f32[1024]{0:T(1024)}, u32[]{:S(2)}) copy-start(f32[1024]{0:T(1024)} %param.44) | copy-start | bytes 12292
  172.1 18.6 %copy-start.8 = (f32[1024]{0:T(1024)S(1)}, f32[1024]{0:T(1024)}, u32[]{:S(2)}) copy-start(f32[1024]{0:T(1024)} %param.45) | copy-start | bytes 12292
  172.2 19.2 %copy-start.1 = (f32[6,512]{1,0:T(8,128)S(1)}, f32[6,512]{1,0:T(8,128)}, u32[]{:S(2)}) copy-start(f32[6,512]{1,0:T(8,128)} %vec_ref.5) | copy-start | bytes 36868
  172.2 19.2 %copy-start.3 = (f32[6,512]{1,0:T(8,128)S(1)}, f32[6,512]{1,0:T(8,128)}, u32[]{:S(2)}) copy-start(f32[6,512]{1,0:T(8,128)} %param.46) | copy-start | bytes 36868
  172.2 19.2 %copy-start.4 = (f32[6,512]{1,0:T(8,128)S(1)}, f32[6,512]{1,0:T(8,128)}, u32[]{:S(2)}) copy-start(f32[6,512]{1,0:T(8,128)} %param.47) | copy-start | bytes 36868
  172.2 19.8 %copy-start = (f32[1280,512]{1,0:T(8,128)S(1)}, f32[1280,512]{1,0:T(8,128)}, u32[]{:S(2)}) copy-start(f32[1280,512]{1,0:T(8,128)} %get-tuple-element.136) | copy-start | bytes 7864324

commit v3 on v2

--- a/solution.py
+++ b/solution.py
@@ -333,6 +333,55 @@
     )
 
 
+class Transfers:
+    def __init__(self, send_sem, recv_sem):
+        self.sems = (send_sem, recv_sem)
+        self.all = {}
+
+    def make(self, key):
+        index, src, dst, target = self.all[key]
+        return pltpu.make_async_remote_copy(
+            src_ref=src(), dst_ref=dst(), send_sem=self.sems[0].at[index], recv_sem=self.sems[1].at[index],
+            device_id=target, device_id_type=MESH,
+        )
+
+    def plan(self, key, src, dst, target):
+        self.all[key] = (len(self.all), src, dst, target)
+
+    def start(self, key, *views):
+        if views:
+            self.plan(key, *views)
+        self.make(key).start()
+
+    def arrive(self, key):
+        self.make(key).wait_recv()
+
+    def finish(self):
+        for key in self.all:
+            self.make(key).wait_send()
+
+
+class Loads:
+    def __init__(self, sem):
+        self.sem = sem
+        self.all = {}
+
+    def make(self, key):
+        index, src, dst = self.all[key]
+        return pltpu.make_async_copy(src(), dst(), self.sem.at[index])
+
+    def plan(self, key, src, dst):
+        self.all[key] = (len(self.all), src, dst)
+
+    def start(self, key, *views):
+        if views:
+            self.plan(key, *views)
+        self.make(key).start()
+
+    def wait(self, key):
+        self.make(key).wait()
+
+
 def layer_norm_rows(rows, gain, shift):
     centred = rows - jnp.mean(rows, axis=-1, keepdims=True)
     inverse = lax.rsqrt(jnp.mean(centred * centred, axis=-1, keepdims=True) + NORM_EPS)
@@ -631,11 +680,27 @@
 
 def mlp_kernel(
     x_ref, dy_ref, ot_ref, wp_ref, wu_ref, wd_ref, vec_ref, small_ref,
-    act_ref, dres_ref, dot_ref, gd_ref, gu_ref, gp_ref, vsum_ref, bsum_ref,
+    act_ref, dres_ref, dot_ref, own_out, fore_out, gp_ref, vsum_ref, bsum_ref,
     res_ref, n2_ref, out_ref, dn_ref, hid_ref, dup_ref, dyc_ref, br_ref,
+    g_ref, fore_ref, fore_core, own_core, own_peer, send_sem, recv_sem,
 ):
     step = pl.program_id(0)
-    mp = lax.axis_index("mp")
+    dp, mp = lax.axis_index("dp"), lax.axis_index("mp")
+    peer, core, core_bit = 1 - mp, partners(dp)[0], lax.rem(dp, 2)
+    side, part = jnp.where(step < 2, peer, mp), lax.rem(step, 2)
+    sent = Transfers(send_sem, recv_sem)
+    kept = pl.ds(pl.multiple_of(core_bit * HALF, HALF), HALF)
+    away = pl.ds(pl.multiple_of(HALF - core_bit * HALF, HALF), HALF)
+    for turn in range(2):
+        sent.plan(
+            ("F", turn), lambda turn=turn: g_ref.at[turn, :, away, :], lambda turn=turn: fore_core.at[turn],
+            {"dp": core},
+        )
+        sent.plan(
+            ("O", turn), lambda turn=turn: g_ref.at[2 + turn, :, away, :],
+            lambda turn=turn: own_core.at[turn], {"dp": core},
+        )
+    sent.plan("peer", lambda: fore_ref, lambda: own_peer, {"mp": peer})
     gain, shift = vec_ref[2:3, :], vec_ref[3:4, :]
     w_proj = wp_ref[...].reshape(512, 512)
 
@@ -644,6 +709,8 @@
 
     @pl.when(step == 0)
     def _():
+        greet([{"dp": core}, {"mp": peer}])
+
         def body(index, carry):
             x_rows = x_ref[pl.ds(row_block(index, mp), HALF), :].astype(F32)
             mixed = ot_ref[:, pl.ds(ext_cols(index), HALF)]
@@ -655,29 +722,54 @@
             dyc_ref[rows(index), :] = dy_ref[pl.ds(row_block(index, mp), HALF), :]
             return carry
 
-        lax.fori_loop(0, 5, body, 0)
-
-    w_up, w_down = wu_ref[0], wd_ref[0]
-    up_bias = small_ref[step // 2, 0:1, pl.ds(pl.multiple_of(lax.rem(step, 2) * 512, 512), 512)]
-
-    def body(index, total):
-        at = rows(index)
-        up_pre = mm_nn(n2_ref[at, :], w_up) + up_bias
+        lax.fori_loop(0, 5, body, 0, unroll=True)
+
+    lanes = pl.ds(pl.multiple_of(part * 512, 512), 512)
+    w_up, w_down = wu_ref[side, :, lanes], wd_ref[side, lanes, :]
+    up_bias = small_ref[side, 0:1, lanes]
+
+    def up_of(index):
+        return mm_nn(n2_ref[index * HALF : index * HALF + HALF, :], w_up) + up_bias
+
+    total = jnp.zeros((8, 512), F32)
+    pre = up_of(0)
+    for index in range(5):
+        at = slice(index * HALF, index * HALF + HALF)
+        up_pre = pre
+        if index < 4:
+            pre = up_of(index + 1)
+        dhid = mm_nt(dyc_ref[at, :], w_down)
         cumulative = 0.5 * (1.0 + lax.erf(up_pre * (0.5**0.5)))
         density = jnp.exp(-0.5 * up_pre * up_pre) * 0.3989422804014327
         hidden = (up_pre * cumulative).astype(BF)
         hid_ref[at, :] = hidden
+        slope = cumulative + up_pre * density
+        dup = (dhid * slope).astype(BF)
+        dup_ref[at, :] = dup
+        total = total + jnp.sum(dup.astype(F32).reshape(HALF // 8, 8, 512), axis=0)
         out_ref[at, :] += mm_nn(hidden, w_down)
-        slope = cumulative + up_pre * density
-        dup = (mm_nt(dyc_ref[at, :], w_down) * slope).astype(BF)
-        dup_ref[at, :] = dup
         dn_ref[at, :] += mm_nt(dup, w_up)
-        return total + jnp.sum(dup.astype(F32).reshape(HALF // 8, 8, 512), axis=0)
-
-    total = lax.fori_loop(0, 5, body, jnp.zeros((8, 512), F32))
-    bsum_ref[0] = total
-    gd_ref[0] = mm_tn(hid_ref[...], dyc_ref[...]).astype(BF)
-    gu_ref[0] = mm_tn(n2_ref[...], dup_ref[...]).astype(BF)
+        if index == 1:
+
+            @pl.when(step == 1)
+            def _():
+                sent.arrive(("F", 0))
+                fore_ref[...] = g_ref[0, :, kept, :] + fore_core[0]
+                sent.start("peer")
+
+            @pl.when(step == 2)
+            def _():
+                sent.arrive(("F", 1))
+                fore_out[...] = g_ref[1, :, kept, :] + fore_core[1]
+
+    bsum_ref[2 * side + part] = total
+    g_ref[step, 0] = mm_tn(hid_ref[...], dyc_ref[...]).astype(BF)
+    g_ref[step, 1] = mm_tn(n2_ref[...], dup_ref[...]).astype(BF)
+    for turn, key in enumerate((("F", 0), ("F", 1), ("O", 0), ("O", 1))):
+
+        @pl.when(step == turn)
+        def _():
+            sent.start(key)
 
     @pl.when(step == 3)
     def _():
@@ -699,173 +791,128 @@
                 vsum_ref[place] += jnp.sum(value.reshape(HALF // 8, 8, 512), axis=0)
             return carry
 
-        lax.fori_loop(0, 5, body, 0)
+        lax.fori_loop(0, 5, body, 0, unroll=True)
         mixed = jnp.concatenate([ot_ref[:, 0:HALF], ot_ref[:, SEQ:]], axis=1)
         gp_ref[...] = mm_nn(mixed, br_ref[...]).astype(BF).reshape(2, 256, 512)
+        sent.arrive(("O", 0))
+        sent.arrive(("O", 1))
+        sent.arrive("peer")
+        near = g_ref[2, :, kept, :].astype(F32) + own_core[0].astype(F32)
+        own_out[0] = (near + own_peer[...].astype(F32)).astype(BF)
+        own_out[1] = g_ref[3, :, kept, :] + own_core[1]
+        sent.finish()
 
 
 def mlp(patches, cotangent, ot, wp, wu, wd, vec_params, small):
     rows = patches.shape[0]
     ext = 3 * SEQ
-    up_spec = pl.BlockSpec((1, 512, 512), lambda f: (f // 2, 0, f % 2))
-    down_spec = pl.BlockSpec((1, 512, 512), lambda f: (f // 2, f % 2, 0))
     return pl.pallas_call(
         mlp_kernel,
         grid=(4,),
         out_shape=[
-            sds((rows, 512), BF), sds((rows, 512), F32), sds((512, ext), BF), sds((2, 1024, 512), BF),
-            sds((2, 512, 1024), BF), sds((2, 256, 512), BF), sds((4, 8, 512), F32), sds((4, 8, 512), F32),
+            sds((rows, 512), BF), sds((rows, 512), F32), sds((512, ext), BF), sds((2, 2, HALF, 512), BF),
+            sds((2, HALF, 512), BF), sds((2, 256, 512), BF), sds((4, 8, 512), F32), sds((4, 8, 512), F32),
         ],
         in_specs=[
             full_spec((rows, 512)), full_spec((rows, 512)), full_spec((512, ext)), full_spec(wp.shape),
-            up_spec, down_spec, full_spec(vec_params.shape), full_spec(small.shape),
+            full_spec(wu.shape), full_spec(wd.shape), full_spec(vec_params.shape), full_spec(small.shape),
         ],
         out_specs=[
-            full_spec((rows, 512)), full_spec((rows, 512)), full_spec((512, ext)), down_spec, up_spec,
-            full_spec((2, 256, 512)), full_spec((4, 8, 512)), pl.BlockSpec((1, 8, 512), lambda f: (f, 0, 0)),
+            full_spec((rows, 512)), full_spec((rows, 512)), full_spec((512, ext)),
+            full_spec((2, 2, HALF, 512)), full_spec((2, HALF, 512)),
+            full_spec((2, 256, 512)), full_spec((4, 8, 512)), full_spec((4, 8, 512)),
         ],
         scratch_shapes=[
             pltpu.VMEM((rows, 512), F32), pltpu.VMEM((rows, 512), BF), pltpu.VMEM((rows, 512), F32),
             pltpu.VMEM((rows, 512), F32), pltpu.VMEM((rows, 512), BF), pltpu.VMEM((rows, 512), BF),
-            pltpu.VMEM((rows, 512), BF), pltpu.VMEM((rows, 512), BF),
+            pltpu.VMEM((rows, 512), BF), pltpu.VMEM((rows, 512), BF), pltpu.VMEM((4, 2, 512, 512), BF),
+            pltpu.VMEM((2, HALF, 512), BF), pltpu.VMEM((2, 2, HALF, 512), BF),
+            pltpu.VMEM((2, 2, HALF, 512), BF), pltpu.VMEM((2, HALF, 512), BF),
+            pltpu.SemaphoreType.DMA((5,)), pltpu.SemaphoreType.DMA((5,)),
         ],
-        compiler_params=pltpu.CompilerParams(vmem_limit_bytes=VMEM_LIMIT),
+        compiler_params=pltpu.CompilerParams(
+            collective_id=2, has_side_effects=True, vmem_limit_bytes=VMEM_LIMIT
+        ),
         name="mlp",
     )(patches, cotangent, ot, wp, wu, wd, vec_params, small)
 
 
 SCHEDULE = (
     (
-        ("F", 0, 0), ("F", 1, 0), ("F", 2, 0), ("F", 3, 0), ("F", 4, 0), ("O", 0, 0), ("O", 1, 0),
-        ("O", 2, 0), ("O", 3, 0), ("O", 4, 0),
-    ),
-    (
-        ("F", 0, 1),
-    ),
-    (
-    ),
-    (
-        ("F", 1, 1),
-    ),
-    (
-        ("O", 0, 1),
-    ),
-    (
-    ),
-    (
-        ("F", 2, 1),
-    ),
-    (
-    ),
-    (
-        ("F", 5, 0), ("O", 0, 2), ("O", 1, 1),
+        ("F", 2, 1), ("F", 4, 0), ("O", 0, 1), ("O", 1, 1), ("O", 4, 0),
+    ),
+    (
     ),
     (
         ("F", 3, 1),
     ),
     (
-    ),
-    (
-        ("F", 4, 1), ("O", 0, 3), ("O", 2, 1),
-    ),
-    (
-        ("F", 6, 0), ("O", 1, 2),
-    ),
-    (
-        ("F", 5, 1), ("O", 0, 4), ("O", 2, 2),
-    ),
-    (
-        ("O", 3, 1),
-    ),
-    (
-        ("F", 6, 1), ("O", 1, 3),
-    ),
-    (
-        ("O", 0, 5), ("O", 2, 3), ("O", 4, 1), ("O", 5, 0),
-    ),
-    (
-        ("O", 1, 4),
-    ),
-    (
-        ("O", 3, 2), ("O", 5, 1),
-    ),
-    (
-        ("O", 0, 6), ("O", 4, 2),
-    ),
-    (
-        ("O", 1, 5), ("O", 6, 0),
-    ),
-    (
-    ),
-    (
-        ("O", 2, 4),
-    ),
-    (
-        ("O", 0, 7), ("O", 3, 3), ("O", 6, 1),
-    ),
-    (
-    ),
-    (
-        ("O", 0, 8), ("O", 1, 6), ("O", 4, 3), ("O", 5, 2),
-    ),
-    (
-        ("O", 2, 5), ("O", 6, 2), ("O", 3, 4), ("O", 4, 4), ("small", 0), ("O", 5, 3), ("O", 1, 7),
-        ("O", 2, 6), ("small", 1), ("O", 6, 3), ("O", 1, 8), ("small", 2), ("O", 3, 5), ("O", 4, 5),
-        ("small", 3), ("O", 5, 4), ("O", 2, 7), ("O", 6, 4), "square", ("small", 4), ("O", 2, 8), ("O", 3, 6),
-        ("O", 4, 6), ("square", 0), ("O", 5, 5), ("square", 1), ("O", 6, 5), ("O", 3, 7), ("square", 2),
-        ("O", 5, 6), ("O", 6, 6), ("O", 4, 7), ("O", 3, 8), ("square", 3), ("O", 4, 8), ("square", 4),
-        ("O", 5, 7), ("O", 5, 8), ("O", 6, 7), ("O", 6, 8),
+        ("O", 0, 2),
+    ),
+    (
+        ("F", 4, 1), ("O", 1, 2), ("O", 2, 1),
+    ),
+    (
+    ),
+    (
+    ),
+    (
+        ("O", 0, 3), ("O", 3, 1),
+    ),
+    (
+        ("F", 5, 0), ("O", 1, 3), ("O", 4, 1),
+    ),
+    (
+        ("F", 5, 1), ("O", 2, 2),
+    ),
+    (
+    ),
+    (
+        ("O", 0, 4), ("O", 3, 2),
+    ),
+    (
+        ("F", 6, 0), ("O", 1, 4), ("O", 4, 2),
+    ),
+    (
+        ("F", 6, 1),
+    ),
+    (
+        ("O", 0, 5), ("O", 2, 3),
+    ),
+    (
+        ("O", 3, 3),
+    ),
+    (
+        ("O", 0, 6), ("O", 1, 5), ("O", 4, 3), ("O", 5, 0),
+    ),
+    (
+    ),
+    (
+        ("O", 1, 6), ("O", 2, 4), ("O", 5, 1),
+    ),
+    (
+    ),
+    (
+        ("O", 3, 4), ("O", 6, 0),
+    ),
+    (
+    ),
+    (
+    ),
+    (
+        ("O", 2, 5), ("O", 4, 4), ("O", 6, 1),
+    ),
+    (
+    ),
+    (
+        ("O", 2, 6),
+    ),
+    (
+        ("O", 5, 3), ("O", 3, 5), ("small", 0), ("O", 4, 5), ("O", 3, 6), ("O", 4, 6), ("O", 6, 3),
+        ("square", 0), ("square", 1), ("small", 1), ("small", 2), ("O", 5, 5), ("square", 2), ("O", 5, 6),
+        ("O", 6, 5), ("O", 6, 6),
     ),
 )
-
-
-class Transfers:
-    def __init__(self, send_sem, recv_sem):
-        self.sems = (send_sem, recv_sem)
-        self.all = {}
-
-    def make(self, key):
-        index, src, dst, target = self.all[key]
-        return pltpu.make_async_remote_copy(
-            src_ref=src(), dst_ref=dst(), send_sem=self.sems[0].at[index], recv_sem=self.sems[1].at[index],
-            device_id=target, device_id_type=MESH,
-        )
-
-    def plan(self, key, src, dst, target):
-        self.all[key] = (len(self.all), src, dst, target)
-
-    def start(self, key, *views):
-        if views:
-            self.plan(key, *views)
-        self.make(key).start()
-
-    def arrive(self, key):
-        self.make(key).wait_recv()
-
-    def finish(self):
-        for key in self.all:
-            self.make(key).wait_send()
-
-
-class Loads:
-    def __init__(self, sem):
-        self.sem = sem
-        self.all = {}
-
-    def make(self, key):
-        index, src, dst = self.all[key]
-        return pltpu.make_async_copy(src(), dst(), self.sem.at[index])
-
-    def plan(self, key, src, dst):
-        self.all[key] = (len(self.all), src, dst)
-
-    def start(self, key, *views):
-        if views:
-            self.plan(key, *views)
-        self.make(key).start()
-
-    def wait(self, key):
-        self.make(key).wait()
 
 
 def cut(ref, start, size):
@@ -873,6 +920,7 @@
     return ref.at[:, rows, :] if len(ref.shape) == 3 else ref.at[rows, :]
 
 
+WIDE = (5, 6)
 PIECES = ((512, 512), (512, 512), (512, 512), (512, 512), (256, 512), (3, 512, 128), (3, 512, 128))
 
 
@@ -882,27 +930,28 @@
 
 def backward_kernel(
     count_ref, qt_in, kt_in, dot_in, ot_in, k_in, v_in, lse_ref, nt_in, wt_in,
-    gd_in, gu_in, gp_in, x_in, dres_in, vec_ref, two_ref, up_sum_ref,
+    own_in, fore_in, gp_in, x_in, dres_in, vec_ref, two_ref, up_sum_ref,
     grad_out, down_out, up_out, proj_out, qkv_out, small_out, norm_out,
     qt_ref, kt_ref, dot_ref, ot_ref, k_ref, v_ref, nt_ref, wt_ref, x_ref, dres_ref,
     shared_ref, grads_ref, acc_ref, bias_ref, s_ref, dp_ref, g_ref, bsum_ref,
-    far_send, far_recv, small_bufs, square_bufs, *rest,
+    far_send, far_recv, small_core, small_part, small_all, square_sum, square_core, square_all, *rest,
 ):
     buffers, (send_sem, recv_sem, local_sem) = rest[:-3], rest[-3:]
     dp, mp = lax.axis_index("dp"), lax.axis_index("mp")
     peer = 1 - mp
-    core, x_side, z_near, z_far = partners(dp)
-    targets = [{"dp": core}, {"mp": peer}, {"dp": x_side}, {"dp": z_near}, {"dp": z_far}]
-    bits = [lax.rem(dp, 2), None] + [lax.rem(lax.div(dp, size), 2) for size in (2, 4, 8)]
+    core, x_side, _, _ = partners(dp)
+    to_core, to_peer, to_x = {"dp": core}, {"mp": peer}, {"dp": x_side}
+    core_bit, x_bit = lax.rem(dp, 2), lax.rem(lax.div(dp, 2), 2)
+    chip, floor = lax.div(dp, 2), lax.div(dp, 4)
+
+    def ring(index):
+        return (chip, 8, 2) if index in WIDE else (floor, 4, 4)
     sent, loads = Transfers(send_sem, recv_sem), Loads(local_sem)
 
     def block_at(place):
         return 2 * jnp.where(place < 2, peer, mp) + lax.rem(place, 2)
 
     def source(index, side):
-        if index < 4:
-            lanes = slice(index // 2 * 512, index // 2 * 512 + 512)
-            return gu_in.at[side, :, lanes] if index % 2 else gd_in.at[side, lanes, :]
         if index == 4:
             return gp_in.at[side]
         return g_ref.at[index - 5 + (0 if side is peer else 2)]
@@ -916,15 +965,13 @@
         return qkv_out.at[:, :, slice((index - 5) * 128, (index - 5) * 128 + 128)]
 
     def piece_buffers(index):
-        return buffers[9 * index : 9 * index + 9]
-
-    def share(total, upto):
-        start, size = 0, total
-        for stage in (0, 2, 3, 4):
-            if stage <= upto:
-                size //= 2
-                start = start + bits[stage] * size
-        return start, size
+        return buffers[8 * index : 8 * index + 8]
+
+    def region(index):
+        half = PIECES[index][-2] // 2
+        if index in WIDE:
+            return core_bit * half, half
+        return core_bit * half + x_bit * (half // 2), half // 2
 
     for place in range(4):
         block = block_at(place)
@@ -944,83 +991,141 @@
         if place == 0:
             loads.start("wt", lambda: wt_in, lambda: wt_ref)
     loads.start("nt", lambda: nt_in, lambda: nt_ref)
-    for index in range(5):
+    for index in range(4):
+        loads.start(
+            ("kept", index, 2), lambda index=index: own_in.at[index // 2, index % 2],
+            lambda index=index: piece_buffers(index)[2],
+        )
+        if index > 1:
+            loads.start(
+                ("kept", index, 0), lambda index=index: fore_in.at[index % 2],
+                lambda index=index: piece_buffers(index)[0],
+            )
+    for index in (4,):
         total = PIECES[index][-2]
         for side, slot in ((peer, 0), (mp, 2)):
             loads.start(
                 ("kept", index, slot),
                 lambda index=index, side=side, total=total: cut(
-                    source(index, side), bits[0] * (total // 2), total // 2
+                    source(index, side), core_bit * (total // 2), total // 2
                 ),
                 lambda index=index, slot=slot: piece_buffers(index)[slot],
             )
     loads.start("x", lambda: x_in, lambda: x_ref)
     loads.start("dres", lambda: dres_in, lambda: dres_ref)
-    greet(targets)
+    chips = [
+        {"dp": lax.rem(dp + 2 * step, 16), "mp": side} for side in (mp, peer) for step in range(8)
+    ][1:]
+    greet([to_core] + chips)
 
     def plan_piece(index):
         total = PIECES[index][-2]
         half = total // 2
-        kept = bits[0] * half
-        fore, fore_core, own, own_core, own_peer, own_x, own_near, own_far, out = piece_buffers(index)
-        away = (1 - bits[0]) * half
-        sent.plan(("F", index, 0), lambda: cut(source(index, peer), away, half), lambda: fore_core, targets[0])
-        sent.plan(("F", index, 1), lambda: fore, lambda: own_peer, targets[1])
-        sent.plan(("O", index, 0), lambda: cut(source(index, mp), away, half), lambda: own_core, targets[0])
-        for stage, landing in ((1, own_x), (2, own_near), (3, own_far)):
-            level = stage + 1
-            outer, outer_size = share(total, level - 1)
-            size = outer_size // 2
-            start = outer - kept + (1 - bits[level]) * size
+        kept = core_bit * half
+        fore, fore_core, own, own_core, own_peer, own_x, landing, out = piece_buffers(index)
+        away = (1 - core_bit) * half
+        if index > 1:
+            sent.plan(("F", index, 1), lambda: fore, lambda: own_peer, to_peer)
+        if index > 3:
+            sent.plan(("F", index, 0), lambda: cut(source(index, peer), away, half), lambda: fore_core, to_core)
+            sent.plan(("O", index, 0), lambda: cut(source(index, mp), away, half), lambda: own_core, to_core)
+        if index not in WIDE:
+            other_x = (1 - x_bit) * (half // 2)
+            sent.plan(("O", index, 1), lambda: cut(own, other_x, half // 2), lambda: own_x, to_x)
+        first, size = region(index)
+        me, members, stride = ring(index)
+        size //= members
+        for step in range(1, members):
+            target = {"dp": lax.rem(dp + stride * step, 16)}
+            their = lax.rem(me + step, members) * size + first
+            mine = me * size + first
             sent.plan(
-                ("O", index, stage), lambda start=start, size=size: cut(own, start, size),
-                lambda landing=landing: landing, targets[level],
+                ("O", index, 2, step), lambda their=their: cut(own, their - kept, size),
+                lambda step=step: landing.at[step - 1], target,
             )
-        for stage, level in ((4, 4), (5, 3), (6, 2), (7, 0)):
-            start, size = share(total, level)
-            where = lambda start=start, size=size: cut(out, start, size)
-            sent.plan(("O", index, stage), where, where, targets[level])
+            place = lambda mine=mine: cut(out, mine, size)
+            sent.plan(("O", index, 3, step), place, place, target)
+        if index not in WIDE:
+            across = lambda: cut(out, region(index)[0], half // 2)
+            sent.plan(("O", index, 4), across, across, to_x)
+        whole = lambda: cut(out, kept, half)
+        sent.plan(("O", index, 5), whole, whole, to_core)
         loads.plan(("out", index), lambda: out, lambda: result(index))
 
     def event(kind, index, stage):
         total = PIECES[index][-2]
         half = total // 2
-        kept = bits[0] * half
-        fore, fore_core, own, own_core, own_peer, own_x, own_near, own_far, out = piece_buffers(index)
-        if stage > 0:
-            sent.arrive((kind, index, stage - 1))
-        if kind == "F" and stage == 1:
-            if index < 5:
+        kept = core_bit * half
+        wide = index in WIDE
+        fore, fore_core, own, own_core, own_peer, own_x, landing, out = piece_buffers(index)
+        first, size = region(index)
+        me, members, _ = ring(index)
+        size //= members
+
+        def each(stage, call):
+            for step in range(1, members):
+                call(("O", index, stage, step))
+
+        if stage == 0:
+            sent.start((kind, index, 0))
+        elif kind == "F":
+            if index > 3:
+                sent.arrive((kind, index, 0))
+            if index < 4:
+                loads.wait(("kept", index, 0))
+            elif index < 5:
                 loads.wait(("kept", index, 0))
                 fore[...] += fore_core[...]
             else:
                 fore[...] = cut(source(index, peer), kept, half)[...] + fore_core[...]
+            sent.start((kind, index, 1))
         elif stage == 1:
-            sent.arrive(("F", index, 1))
+            if index > 3:
+                sent.arrive((kind, index, 0))
+            if index > 1:
+                sent.arrive(("F", index, 1))
             if index < 5:
                 loads.wait(("kept", index, 2))
-                base = own[...]
+            if index > 1:
+                base = (own if index < 5 else cut(source(index, mp), kept, half))[...].astype(F32)
+                if index > 3:
+                    base = base + own_core[...].astype(F32)
+                own[...] = (base + own_peer[...].astype(F32)).astype(BF)
+            if wide:
+                each(2, sent.start)
             else:
-                base = cut(source(index, mp), kept, half)[...]
-            own[...] = (base.astype(F32) + own_core[...].astype(F32) + own_peer[...].astype(F32)).astype(BF)
-        elif 2 <= stage <= 4:
-            start, size = share(total, stage)
-            landing = (own_x, own_near, own_far)[stage - 2]
-            value = cut(own, start - kept, size)[...] + landing[...]
-            if stage < 4:
-                cut(own, start - kept, size)[...] = value
+                sent.start((kind, index, 1))
+        elif stage == 2:
+            sent.arrive((kind, index, 1))
+            at = x_bit * (half // 2)
+            cut(own, at, half // 2)[...] += own_x[...]
+            each(2, sent.start)
+        elif stage == 3:
+            each(2, sent.arrive)
+            value = cut(own, first - kept + me * size, size)[...].astype(F32)
+            for step in range(members - 1):
+                value = value + landing[step].astype(F32)
+            value = value.astype(BF)
+            cut(out, first + me * size, size)[...] = value
+            each(3, sent.start)
+            squared = value.astype(F32)
+            square = jnp.sum((squared * squared).reshape(-1, 8, squared.shape[-1]), axis=0)
+            folded = square[:, 0:128]
+            for lane in range(1, square.shape[1] // 128):
+                folded = folded + square[:, lane * 128 : lane * 128 + 128]
+            square_sum[...] += folded
+        elif stage == 4:
+            each(3, sent.arrive)
+            sent.start((kind, index, 4))
+        elif stage == 5:
+            if wide:
+                each(3, sent.arrive)
             else:
-                cut(out, start, size)[...] = value
-                wide = value.astype(F32)
-                square = jnp.sum((wide * wide).reshape(-1, 8, wide.shape[-1]), axis=0)
-                folded = square[:, 0:128]
-                for lane in range(1, square.shape[1] // 128):
-                    folded = folded + square[:, lane * 128 : lane * 128 + 128]
-                square_bufs[0, 0] += folded
-        if stage == 8:
+                sent.arrive((kind, index, 4))
+            sent.start((kind, index, 5))
+        else:
+            sent.arrive((kind, index, 5))
             loads.start(("out", index))
-        else:
-            sent.start((kind, index, stage))
 
     for index in range(7):
         plan_piece(index)
@@ -1029,7 +1134,7 @@
         for item in events:
             event(*item)
 
-    square_bufs[0, 0] = jnp.zeros((8, 128), F32)
+    square_sum[...] = jnp.zeros((8, 128), F32)
     bias_ref[0] = key_bias((SEQ, 128), mp, count_ref[2], True)
     for group in (1, 2):
         bias_ref[group] = key_bias((SEQ, 128), mp, count_ref[3 * mp + group - 1], False)
@@ -1100,7 +1205,7 @@
 
     lax.fori_loop(0, 4, shared_step, 0)
     far_send[...] = acc_ref[HALF:SEQ].astype(BF)
-    sent.start("far", lambda: far_send, lambda: far_recv, targets[1])
+    sent.start("far", lambda: far_send, lambda: far_recv, to_peer)
     loads.wait("nt")
 
     def main_step(step, carry):
@@ -1163,58 +1268,64 @@
     sums = finish_rows(0, acc_ref[0:HALF] + far_recv[...].astype(F32), sums)
 
     def small_row(place, value):
-        small_bufs[0, 0, place : place + 1, :] = value
-
-    small_bufs[0, 0] = jnp.zeros((16, 512), F32)
+        small_core[0, place : place + 1, :] = value
+
+    small_core[0] = jnp.zeros((16, 512), F32)
     for place in range(4):
         lanes = pl.ds(pl.multiple_of(block_at(place) * 128, 128), 128)
-        small_bufs[0, 0, 0:1, lanes] = bsum_ref[place, 0:1, 0:128]
-        small_bufs[0, 0, 1:2, lanes] = bsum_ref[place, 0:1, 256:384]
+        small_core[0, 0:1, lanes] = bsum_ref[place, 0:1, 0:128]
+        small_core[0, 1:2, lanes] = bsum_ref[place, 0:1, 256:384]
         small_row(2 + place, jnp.sum(up_sum_ref[place], axis=0, keepdims=True))
         small_row(8 + place, jnp.sum(two_ref[place], axis=0, keepdims=True))
     for place in range(2):
         small_row(6 + place, jnp.sum(sums[place], axis=0, keepdims=True))
 
-    def small_start(stage):
-        sent.start(
-            ("small", stage), lambda: small_bufs.at[0, stage], lambda: small_bufs.at[1, stage], targets[stage]
-        )
-
-    def small_end(stage):
-        sent.arrive(("small", stage))
-        value = small_bufs[0, stage] + small_bufs[1, stage]
-        if stage < 4:
-            small_bufs[0, stage + 1] = value
-            small_start(stage + 1)
+    me = mp * 8 + chip
+    rows_mine = pl.ds(pl.multiple_of(core_bit * 8, 8), 8)
+    rows_other = pl.ds(pl.multiple_of(8 - core_bit * 8, 8), 8)
+    sent.plan("small core", lambda: small_core.at[0, rows_other], lambda: small_core.at[1, rows_other], to_core)
+    sent.plan("square core", lambda: square_sum, lambda: square_core, to_core)
+    sent.plan("small back", lambda: small_part.at[rows_mine], lambda: small_part.at[rows_mine], to_core)
+    for place, target in enumerate(chips):
+        sent.plan(("small", place), lambda: small_all.at[me], lambda: small_all.at[me], target)
+        sent.plan(("square", place), lambda: square_all.at[me], lambda: square_all.at[me], target)
+
+    def everywhere(name, call):
+        for place in range(len(chips)):
+            call((name, place))
+
+    def small_stage(stage):
+        if stage == 0:
+            sent.arrive("small core")
+            small_all[me] = small_core[0, rows_mine] + small_core[1, rows_mine]
+            everywhere("small", sent.start)
+        elif stage == 1:
+            everywhere("small", sent.arrive)
+            small_part[rows_mine] = jnp.sum(small_all[...], axis=0)
+            sent.start("small back")
         else:
-            small_out[...] = value
-
-    order = (4, 3, 2, 0, 1)
-
-    def square_start(place):
-        sent.start(
-            ("square", place), lambda: square_bufs.at[0, place], lambda: square_bufs.at[1, place],
-            targets[order[place]],
-        )
-
-    def square_end(place):
-        sent.arrive(("square", place))
-        value = square_bufs[0, place] + square_bufs[1, place]
-        if place < 4:
-            square_bufs[0, place + 1] = value
-            square_start(place + 1)
+            sent.arrive("small back")
+
+    def square_stage(stage):
+        if stage == 0:
+            sent.start("square core")
+        elif stage == 1:
+            sent.arrive("square core")
+            square_all[me] = square_sum[...] + square_core[...]
+            everywhere("square", sent.start)
         else:
-            total = jnp.sum(small_out[...] * small_out[...]) + jnp.sum(value)
+            everywhere("square", sent.arrive)
+            small = small_part[...]
+            small_out[...] = small
+            total = jnp.sum(small * small) + jnp.sum(jnp.sum(square_all[...], axis=0))
             norm_out[...] = jnp.sqrt(jnp.full((8, 128), total, F32))
 
-    small_start(0)
+    sent.start("small core")
     for item in SCHEDULE[26]:
-        if item == "square":
-            square_start(0)
-        elif item[0] == "small":
-            small_end(item[1])
+        if item[0] == "small":
+            small_stage(item[1])
         elif item[0] == "square":
-            square_end(item[1])
+            square_stage(item[1])
         else:
             event(*item)
     sent.finish()
@@ -1222,13 +1333,16 @@
         loads.wait(("out", index))
 
 
-def backward(key_count, qt, kt, dot, ot, k, v, lse, nt, wt, gd, gu, gp, patches, dres, vec_params, two, ups):
+def backward(key_count, qt, kt, dot, ot, k, v, lse, nt, wt, owns, fores, gp, patches, dres, vec_params, two, ups):
     ext, rows = 3 * SEQ, patches.shape[0]
     vmem, hbm = pl.BlockSpec(memory_space=pltpu.VMEM), pl.BlockSpec(memory_space=pl.ANY)
     buffers = []
     for index in range(7):
-        for size in (2, 2, 2, 2, 2, 4, 8, 16, 1):
+        for size in (2, 2, 2, 2, 2, 4):
             buffers.append(pltpu.VMEM(piece_rows(index, size), BF))
+        members = 7 if index in WIDE else 3
+        buffers.append(pltpu.VMEM((members, *piece_rows(index, 16)), BF))
+        buffers.append(pltpu.VMEM(piece_rows(index, 1), BF))
     return pl.pallas_call(
         backward_kernel,
         out_shape=[
@@ -1243,15 +1357,16 @@
             pltpu.VMEM((rows, 512), F32), pltpu.VMEM((4, 384, SEQ), BF), pltpu.VMEM((384, 2 * SEQ), BF),
             pltpu.VMEM((ext, 512), F32), pltpu.VMEM((3, SEQ, 128), BF), pltpu.VMEM((2, SEQ, SEQ), F32),
             pltpu.VMEM((2, SEQ, SEQ), F32), pltpu.VMEM((4, 3, 512, 128), BF), pltpu.VMEM((4, 8, 384), F32),
-            pltpu.VMEM((HALF, 512), BF), pltpu.VMEM((HALF, 512), BF), pltpu.VMEM((2, 5, 16, 512), F32),
-            pltpu.VMEM((2, 5, 8, 128), F32), *buffers, pltpu.SemaphoreType.DMA((81,)),
-            pltpu.SemaphoreType.DMA((81,)), pltpu.SemaphoreType.DMA((48,)),
+            pltpu.VMEM((HALF, 512), BF), pltpu.VMEM((HALF, 512), BF), pltpu.VMEM((2, 16, 512), F32),
+            pltpu.VMEM((16, 512), F32), pltpu.VMEM((16, 8, 512), F32), pltpu.VMEM((8, 128), F32),
+            pltpu.VMEM((8, 128), F32), pltpu.VMEM((16, 8, 128), F32), *buffers,
+            pltpu.SemaphoreType.DMA((120,)), pltpu.SemaphoreType.DMA((120,)), pltpu.SemaphoreType.DMA((48,)),
         ],
         compiler_params=pltpu.CompilerParams(
             collective_id=1, has_side_effects=True, vmem_limit_bytes=VMEM_LIMIT
         ),
         name="backward",
-    )(key_count, qt, kt, dot, ot, k, v, lse, nt, wt, gd, gu, gp, patches, dres, vec_params, two, ups)
+    )(key_count, qt, kt, dot, ot, k, v, lse, nt, wt, owns, fores, gp, patches, dres, vec_params, two, ups)
 
 
 def adam_kernel(norm_ref, *refs):
@@ -1355,11 +1470,11 @@
     wt, wp, wu, wd, small_all, nt, qt, kt, k, v, ot, lse = forward(
         key_count, w_qkv, w_proj, w_up, w_down, small, patches, vec_params
     )
-    activations, dres, dot, g_down, g_up, g_proj, vsum_two, up_sums = mlp(
+    activations, dres, dot, owns, fores, g_proj, vsum_two, up_sums = mlp(
         patches, cotangent, ot, wp, wu, wd, vec_params, small_all
     )
     input_grad, down, up, proj, qkv, small_total, norm = backward(
-        key_count, qt, kt, dot, ot, k, v, lse, nt, wt, g_down, g_up, g_proj, patches, dres, vec_params,
+        key_count, qt, kt, dot, ot, k, v, lse, nt, wt, owns, fores, g_proj, patches, dres, vec_params,
         vsum_two, up_sums,
     )
     qkv = qkv.reshape(1536, 256)

time: 194 us -> 180 us (0.928)
  Pallas kernels: 186 us -> 169 us
  local copies, waits for them, and re-layouts: 2.82 us -> 5.29 us
    pallas_call x1, Pallas kernels: 92.2 us -> 80.7 us  [backward(): pl.pallas_call(backward_kernel, out_shape=[sds((rows, 512), F32), sds((10...]
    pallas_call x1, Pallas kernels: 38.6 us -> 33.7 us  [mlp(): pl.pallas_call(mlp_kernel, grid=(4,), out_shape=[sds((rows, 512), BF), sd...]
    unnamed x25 -> x26, local copies, waits for them, and re-layouts: 1.56 us -> 4.01 us
where the time goes in v3:
time: 180 us
  Pallas kernels  169 us (94%)
  local copies, waits for them, and re-layouts  5.29 us (3%)
  other arithmetic  3.27 us (2%)
    pallas_call x1, Pallas kernels, backward(): pl.pallas_call(backward_kernel, out_shape=[sds((rows, 512), F32), sds((10...  80.7 us
    pallas_call x1, Pallas kernels, forward(): pl.pallas_call(forward_kernel, out_shape=[sds((2, 3, 256, 512), BF), sds(...  37.9 us
    pallas_call x1, Pallas kernels, mlp(): pl.pallas_call(mlp_kernel, grid=(4,), out_shape=[sds((rows, 512), BF), sd...  33.7 us
    pallas_call x1, Pallas kernels, adam_matrices(): pl.pallas_call(adam_kernel, grid=(steps,), out_shape=out_shape, in_specs=...  16.9 us
    unnamed x26, local copies, waits for them, and re-layouts  4.01 us

profile of v3, /device:TPU:1, one launch (start us, length us, event | category | flops | bytes accessed | tf_op | source)
XLA Modules:
  0.0 179.5 jit_solution(7551168806516754224)
XLA Ops:
  0.7 0.1 pad.7.clone
  0.7 1.4 fusion.small_ref
  2.1 37.9 %forward.1 = (bf16[2,3,256,512]{3,2,1,0:T(8,128)(2,1)}, bf16[2,256,512]{2,1,0:T(8,128)(2,1)}, bf16[2,512,1024]{2,1,0:T(8,128)(2,1)}, bf16[2,1024,512]{2,1,0:T(8,...) custom-call(s32[5]{0:T(128)} %count_ref.3, ...), custom_call_target="tpu_custom_call" | custom-call | tf_op jit(solution)/shard_map/forward/pallas_call | solution.py:655
  40.1 33.7 %mlp.1 = (bf16[1280,512]{1,0:T(8,128)(2,1)}, f32[1280,512]{1,0:T(8,128)}, bf16[512,1536]{1,0:T(8,128)(2,1)}, bf16[2,2,256,512]{3,2,1,0:T(8,128)(2,1)}, bf16[2,25...) custom-call(bf16[1280,512]{1,0:T(8,128)(2,1)} %x_in.1, ...), custom_call_target="tpu_custom_call" | custom-call | tf_op jit(solution)/shard_map/mlp/pallas_call | solution.py:809
  73.8 80.7 %backward.1 = (f32[1280,512]{1,0:T(8,128)}, bf16[1024,512]{1,0:T(8,128)(2,1)}, bf16[512,1024]{1,0:T(8,128)(2,1)}, bf16[256,512]{1,0:T(8,128)(2,1)}, bf16[3,512,2...) custom-call(s32[5]{0:T(128)} %count_ref.3, bf16[512,1536]{1,0:T(8,128)(2,1)} %get-tuple-element.69.qt_in, ...), custom_call_target="tpu_custom_call" | custom-call | tf_op jit(solution)/shard_map/backward/pallas_call | solution.py:1346
  154.5 1.2 slice.12
  155.7 0.0 copy-start.2
  155.7 0.0 copy-start.6
  155.7 0.0 copy-start.5
  155.7 0.0 copy-start.7
  155.7 0.0 copy-start.8
  155.7 0.0 copy-start.1
  155.7 0.0 copy-start.3
  155.8 0.0 copy-start.4
  155.8 16.9 %adam_matrices.1 = (f32[1536,256]{1,0:T(8,128)}, f32[1536,256]{1,0:T(8,128)}, f32[1536,256]{1,0:T(8,128)}, f32[256,512]{1,0:T(8,128)}, f32[256,512]{1,0:T(8,128)...) custom-call(f32[8,128]{1,0:T(8,128)} %get-tuple-element.84.norm_ref,, ...), custom_call_target="tpu_custom_call" | custom-call | tf_op jit(solution)/shard_map/adam_matrices/pallas_call | solution.py:1395
  172.7 0.0 copy-start
  173.6 0.0 copy-done.2
  173.6 0.0 copy-done.6
  173.6 0.0 copy-done.9
  173.6 0.0 copy-done.10
  173.6 0.6 multiply_subtract_fusion.2
  174.2 0.0 copy-done.5
  174.3 0.0 copy-done.7
  174.3 0.0 copy-done.8
  174.3 0.6 multiply_subtract_fusion.1
  174.9 0.0 copy-done.1
  174.9 0.0 copy-done.3
  174.9 0.0 copy-done.4
  174.9 0.6 multiply_subtract_fusion
  175.6 2.5 %copy.51 = bf16[1280,512]{1,0:T(8,128)(2,1)} copy(bf16[1280,512]{1,0:T(8,128)(2,1)} %get-tuple-element.135) | data formatting | bytes 2621440
  178.0 0.0 copy-done
  178.0 1.5 copy.52
  (6 shorter events, 0.0 us)
Async XLA Ops:
  155.7 17.9 %copy-start.2 = (f32[16,512]{1,0:T(8,128)S(1)}, f32[16,512]{1,0:T(8,128)}, u32[]{:S(2)}) copy-start(f32[16,512]{1,0:T(8,128)} %get-tuple-element.101) | copy-start | bytes 98308
  155.7 17.9 %copy-start.6 = (f32[2,256]{1,0:T(2,128)S(1)}, f32[2,256]{1,0:T(2,128)}, u32[]{:S(2)}) copy-start(f32[2,256]{1,0:T(2,128)} %param.31) | copy-start | bytes 6148
  155.7 17.9 %copy-start.9 = (f32[2,256]{1,0:T(2,128)S(1)}, f32[2,256]{1,0:T(2,128)}, u32[]{:S(2)}) copy-start(f32[2,256]{1,0:T(2,128)} %param.42) | copy-start | bytes 6148
  155.7 17.9 %copy-start.10 = (f32[2,256]{1,0:T(2,128)S(1)}, f32[2,256]{1,0:T(2,128)}, u32[]{:S(2)}) copy-start(f32[2,256]{1,0:T(2,128)} %param.43) | copy-start | bytes 6148
  155.7 18.6 %copy-start.5 = (f32[1024]{0:T(1024)S(1)}, f32[1024]{0:T(1024)}, u32[]{:S(2)}) copy-start(f32[1024]{0:T(1024)} %param.32) | copy-start | bytes 12292
  155.7 18.6 %copy-start.7 = (f32[1024]{0:T(1024)S(1)}, f32[1024]{0:T(1024)}, u32[]{:S(2)}) copy-start(f32[1024]{0:T(1024)} %param.44) | copy-start | bytes 12292
  155.7 18.5 %copy-start.8 = (f32[1024]{0:T(1024)S(1)}, f32[1024]{0:T(1024)}, u32[]{:S(2)}) copy-start(f32[1024]{0:T(1024)} %param.45) | copy-start | bytes 12292
  155.7 19.2 %copy-start.1 = (f32[6,512]{1,0:T(8,128)S(1)}, f32[6,512]{1,0:T(8,128)}, u32[]{:S(2)}) copy-start(f32[6,512]{1,0:T(8,128)} %vec_ref.5) | copy-start | bytes 36868
  155.7 19.2 %copy-start.3 = (f32[6,512]{1,0:T(8,128)S(1)}, f32[6,512]{1,0:T(8,128)}, u32[]{:S(2)}) copy-start(f32[6,512]{1,0:T(8,128)} %param.46) | copy-start | bytes 36868
  155.8 19.2 %copy-start.4 = (f32[6,512]{1,0:T(8,128)S(1)}, f32[6,512]{1,0:T(8,128)}, u32[]{:S(2)}) copy-start(f32[6,512]{1,0:T(8,128)} %param.47) | copy-start | bytes 36868
  172.7 5.3 %copy-start = (f32[1280,512]{1,0:T(8,128)S(1)}, f32[1280,512]{1,0:T(8,128)}, u32[]{:S(2)}) copy-start(f32[1280,512]{1,0:T(8,128)} %get-tuple-element.136) | copy-start | bytes 7864324

commit v4 on v3

--- a/solution.py
+++ b/solution.py
@@ -434,7 +434,7 @@
 
 
 def forward_kernel(
-    count_ref, qkv_ref, proj_ref, up_ref, down_ref, small_ref, x_ref, vec_ref,
+    count_ref, qkv_ref, proj_ref, up_ref, down_ref, qv_ref, up_bias_ref, x_ref, vec_ref,
     wt_out, wp_out, wu_out, wd_out, sm_out,
     nt_out, qt_out, kt_out, k_out, v_out, ot_out, lse_out,
     wt_ref, own_proj, own_up, own_down, sm_ref, other_ref,
@@ -521,7 +521,9 @@
     for part in range(3):
         wt_ref[mp, part] = qkv_ref[part].T.astype(BF)
         to_peer(part)
-    sm_ref[mp] = small_ref[...]
+    sm_ref[mp] = jnp.zeros((8, 1024), F32)
+    sm_ref[mp, 0:1, :] = up_bias_ref[...]
+    sm_ref[mp, 1:3, 0:256] = qv_ref[...]
     small_copy = send(lambda: sm_ref.at[mp], lambda: sm_ref.at[mp], {"mp": peer})
     own_proj[...] = proj_ref[...].astype(BF)
     own_up[...] = up_ref[...].astype(BF)
@@ -649,7 +651,7 @@
         copy.wait()
 
 
-def forward(key_count, w_qkv, w_proj, w_up, w_down, small, patches, vec_params):
+def forward(key_count, w_qkv, w_proj, w_up, w_down, qv_bias, up_bias, patches, vec_params):
     ext = 3 * SEQ
     vmem, hbm = pl.BlockSpec(memory_space=pltpu.VMEM), pl.BlockSpec(memory_space=pl.ANY)
     return pl.pallas_call(
@@ -660,7 +662,7 @@
             sds((512, ext), BF), sds((512, ext), BF), sds((512, ext), BF), sds((ext, 512), BF),
             sds((ext, 512), BF), sds((512, ext), BF), sds((3, 4, 8, SEQ), F32),
         ],
-        in_specs=[pl.BlockSpec(memory_space=pltpu.SMEM)] + [vmem] * 7,
+        in_specs=[pl.BlockSpec(memory_space=pltpu.SMEM)] + [vmem] * 8,
         out_specs=[hbm] * 12,
         scratch_shapes=[
             pltpu.VMEM((2, 3, 256, 512), BF), pltpu.VMEM((256, 512), BF), pltpu.VMEM((512, 1024), BF),
@@ -675,7 +677,7 @@
             collective_id=0, has_side_effects=True, vmem_limit_bytes=VMEM_LIMIT
         ),
         name="forward",
-    )(key_count, w_qkv, w_proj, w_up, w_down, small, patches, vec_params)
+    )(key_count, w_qkv, w_proj, w_up, w_down, qv_bias, up_bias, patches, vec_params)
 
 
 def mlp_kernel(
@@ -850,6 +852,8 @@
         ("O", 0, 2),
     ),
     (
+    ),
+    (
         ("F", 4, 1), ("O", 1, 2), ("O", 2, 1),
     ),
     (
@@ -857,60 +861,61 @@
     (
     ),
     (
-        ("O", 0, 3), ("O", 3, 1),
-    ),
-    (
-        ("F", 5, 0), ("O", 1, 3), ("O", 4, 1),
-    ),
-    (
-        ("F", 5, 1), ("O", 2, 2),
-    ),
-    (
-    ),
-    (
-        ("O", 0, 4), ("O", 3, 2),
-    ),
-    (
-        ("F", 6, 0), ("O", 1, 4), ("O", 4, 2),
-    ),
-    (
-        ("F", 6, 1),
-    ),
-    (
-        ("O", 0, 5), ("O", 2, 3),
-    ),
-    (
-        ("O", 3, 3),
-    ),
-    (
-        ("O", 0, 6), ("O", 1, 5), ("O", 4, 3), ("O", 5, 0),
-    ),
-    (
-    ),
-    (
-        ("O", 1, 6), ("O", 2, 4), ("O", 5, 1),
-    ),
-    (
-    ),
-    (
-        ("O", 3, 4), ("O", 6, 0),
-    ),
-    (
-    ),
-    (
-    ),
-    (
-        ("O", 2, 5), ("O", 4, 4), ("O", 6, 1),
-    ),
-    (
-    ),
-    (
-        ("O", 2, 6),
-    ),
-    (
-        ("O", 5, 3), ("O", 3, 5), ("small", 0), ("O", 4, 5), ("O", 3, 6), ("O", 4, 6), ("O", 6, 3),
-        ("square", 0), ("square", 1), ("small", 1), ("small", 2), ("O", 5, 5), ("square", 2), ("O", 5, 6),
-        ("O", 6, 5), ("O", 6, 6),
+        ("F", 5, 0), ("O", 0, 3), ("O", 3, 1),
+    ),
+    (
+        ("O", 1, 3),
+    ),
+    (
+        ("F", 5, 1), ("O", 4, 1),
+    ),
+    (
+        ("O", 2, 2),
+    ),
+    (
+        ("F", 6, 0), ("O", 0, 4),
+    ),
+    (
+        ("O", 3, 2),
+    ),
+    (
+        ("F", 6, 1), ("O", 1, 4),
+    ),
+    (
+        ("O", 4, 2),
+    ),
+    (
+        ("O", 0, 5), ("O", 2, 3), ("O", 5, 0),
+    ),
+    (
+    ),
+    (
+        ("O", 0, 6), ("O", 1, 5), ("O", 3, 3),
+    ),
+    (
+        ("O", 4, 3),
+    ),
+    (
+        ("O", 1, 6), ("O", 2, 4), ("O", 6, 0),
+    ),
+    (
+        ("O", 5, 1),
+    ),
+    (
+    ),
+    (
+        ("O", 3, 4),
+    ),
+    (
+        ("O", 6, 1),
+    ),
+    (
+        ("O", 4, 4),
+    ),
+    (
+        ("O", 2, 5), ("small", 0), ("O", 5, 3), ("O", 2, 6), ("O", 3, 5), ("O", 4, 5), ("O", 3, 6),
+        ("small", 1), ("O", 4, 6), ("O", 6, 3), ("small", 2), ("square", 0), ("square", 1), ("O", 5, 5),
+        ("square", 2), ("O", 5, 6), ("O", 6, 5), ("O", 6, 6),
     ),
 )
 
@@ -933,8 +938,8 @@
     own_in, fore_in, gp_in, x_in, dres_in, vec_ref, two_ref, up_sum_ref,
     grad_out, down_out, up_out, proj_out, qkv_out, small_out, norm_out,
     qt_ref, kt_ref, dot_ref, ot_ref, k_ref, v_ref, nt_ref, wt_ref, x_ref, dres_ref,
-    shared_ref, grads_ref, acc_ref, bias_ref, s_ref, dp_ref, g_ref, bsum_ref,
-    far_send, far_recv, small_core, small_part, small_all, square_sum, square_core, square_all, *rest,
+    shared_ref, grads_ref, bias_ref, s_ref, dp_ref, g_ref, bsum_ref,
+    far_send, far_recv, early_core, early_part, early_all, late_core, late_part, late_all, square_sum, square_core, square_all, *rest,
 ):
     buffers, (send_sem, recv_sem, local_sem) = rest[:-3], rest[-3:]
     dp, mp = lax.axis_index("dp"), lax.axis_index("mp")
@@ -973,46 +978,49 @@
             return core_bit * half, half
         return core_bit * half + x_bit * (half // 2), half // 2
 
+    names = ("qt", "kt", "dot", "ot", "k", "v")
+    sources = (qt_in, kt_in, dot_in, ot_in, k_in, v_in)
+    homes = (qt_ref, kt_ref, dot_ref, ot_ref, k_ref, v_ref)
     for place in range(4):
-        block = block_at(place)
-        rows = pl.ds(pl.multiple_of(block * 128, 128), 128)
-        for name, src, dst in (
-            ("qt", qt_in, qt_ref), ("kt", kt_in, kt_ref), ("dot", dot_in, dot_ref), ("ot", ot_in, ot_ref)
-        ):
-            loads.start(
-                (name, place), lambda src=src, rows=rows: src.at[rows, :],
+        rows = pl.ds(pl.multiple_of(block_at(place) * 128, 128), 128)
+        for name, src, dst in zip(names, sources, homes):
+            loads.plan(
+                (name, place),
+                lambda src=src, rows=rows: src.at[rows, :] if src.shape[0] == 512 else src.at[:, rows],
                 lambda dst=dst, place=place: dst.at[place],
             )
-        for name, src, dst in (("k", k_in, k_ref), ("v", v_in, v_ref)):
-            loads.start(
-                (name, place), lambda src=src, rows=rows: src.at[:, rows],
-                lambda dst=dst, place=place: dst.at[place],
-            )
-        if place == 0:
-            loads.start("wt", lambda: wt_in, lambda: wt_ref)
-    loads.start("nt", lambda: nt_in, lambda: nt_ref)
+
+    def load_block(place):
+        for name in names:
+            loads.start((name, place))
+
+    def loaded(place):
+        for name in names:
+            loads.wait((name, place))
+
+    load_block(0)
+    loads.start("wt", lambda: wt_in, lambda: wt_ref)
     for index in range(4):
-        loads.start(
+        loads.plan(
             ("kept", index, 2), lambda index=index: own_in.at[index // 2, index % 2],
             lambda index=index: piece_buffers(index)[2],
         )
         if index > 1:
-            loads.start(
+            loads.plan(
                 ("kept", index, 0), lambda index=index: fore_in.at[index % 2],
                 lambda index=index: piece_buffers(index)[0],
             )
-    for index in (4,):
-        total = PIECES[index][-2]
-        for side, slot in ((peer, 0), (mp, 2)):
-            loads.start(
-                ("kept", index, slot),
-                lambda index=index, side=side, total=total: cut(
-                    source(index, side), core_bit * (total // 2), total // 2
-                ),
-                lambda index=index, slot=slot: piece_buffers(index)[slot],
-            )
-    loads.start("x", lambda: x_in, lambda: x_ref)
-    loads.start("dres", lambda: dres_in, lambda: dres_ref)
+    half = PIECES[4][-2] // 2
+    for side, slot in ((peer, 0), (mp, 2)):
+        loads.plan(
+            ("kept", 4, slot), lambda side=side: cut(source(4, side), core_bit * half, half),
+            lambda slot=slot: piece_buffers(4)[slot],
+        )
+    for key in ((2, 0), (0, 2), (1, 2), (3, 0), (2, 2), (3, 2), (4, 0), (4, 2)):
+        loads.start(("kept", *key))
+    loads.plan("nt", lambda: nt_in, lambda: nt_ref)
+    loads.plan("x", lambda: x_in, lambda: x_ref)
+    loads.plan("dres", lambda: dres_in, lambda: dres_ref)
     chips = [
         {"dp": lax.rem(dp + 2 * step, 16), "mp": side} for side in (mp, peer) for step in range(8)
     ][1:]
@@ -1130,6 +1138,46 @@
     for index in range(7):
         plan_piece(index)
 
+    me = mp * 8 + chip
+    rows_mine = pl.ds(pl.multiple_of(core_bit * 8, 8), 8)
+    rows_other = pl.ds(pl.multiple_of(8 - core_bit * 8, 8), 8)
+    sums_of = {"early": (early_core, early_part, early_all), "late": (late_core, late_part, late_all)}
+    sent.plan("square core", lambda: square_sum, lambda: square_core, to_core)
+    for name, (both, part, everyone) in sums_of.items():
+        sent.plan(
+            (name, "core"), lambda both=both: both.at[0, rows_other],
+            lambda both=both: both.at[1, rows_other], to_core,
+        )
+        back = lambda part=part: part.at[rows_mine]
+        sent.plan((name, "back"), back, back, to_core)
+        for place, target in enumerate(chips):
+            slot = lambda everyone=everyone: everyone.at[me]
+            sent.plan((name, place), slot, slot, target)
+    for place, target in enumerate(chips):
+        sent.plan(("square", place), lambda: square_all.at[me], lambda: square_all.at[me], target)
+
+    def everywhere(name, call):
+        for place in range(len(chips)):
+            call((name, place))
+
+    def spread(name, stage):
+        both, part, everyone = sums_of[name]
+        if stage == 0:
+            sent.arrive((name, "core"))
+            everyone[me] = both[0, rows_mine] + both[1, rows_mine]
+            everywhere(name, sent.start)
+        elif stage == 1:
+            everywhere(name, sent.arrive)
+            part[rows_mine] = jnp.sum(everyone[...], axis=0)
+            sent.start((name, "back"))
+        else:
+            sent.arrive((name, "back"))
+
+    for row in range(8):
+        value = jnp.sum(up_sum_ref[row] if row < 4 else two_ref[row - 4], axis=0, keepdims=True)
+        early_core[0, row : row + 1, :] = value[:, 0:256]
+        early_core[0, 8 + row : 9 + row, :] = value[:, 256:512]
+
     def run(events):
         for item in events:
             event(*item)
@@ -1138,29 +1186,31 @@
     bias_ref[0] = key_bias((SEQ, 128), mp, count_ref[2], True)
     for group in (1, 2):
         bias_ref[group] = key_bias((SEQ, 128), mp, count_ref[3 * mp + group - 1], False)
+    sent.start(("early", "core"))
     run(SCHEDULE[0])
 
-    def heads(place, group, queries, out, out_base, between):
+    def tiles(place, group, queries, sub):
+        base = pl.multiple_of(group * SEQ, SEQ)
+        keys_at, queries_at = pl.ds(base, SEQ), pl.ds(base, queries)
+        own = slice(sub * HD, sub * HD + HD)
+        s_ref[sub % 2, :, :queries] = score_tile(
+            k_ref[place, keys_at, :], bias_ref[group], qt_ref[place, own, queries_at], sub
+        )
+        dp_ref[sub % 2, :, :queries] = mm_nn(
+            v_ref[place, keys_at, :], widen_plain(dot_ref[place, own, queries_at], sub)
+        )
+
+    def heads(place, group, queries, out, out_base, following, between):
         block = block_at(place)
         base = pl.multiple_of(group * SEQ, SEQ)
         keys_at, queries_at = pl.ds(base, SEQ), pl.ds(base, queries)
         out_keys = pl.ds(out_base, SEQ)
         out_queries = pl.ds(out_base, queries)
-        bias = bias_ref[group]
-
-        def tiles(sub):
-            own = slice(sub * HD, sub * HD + HD)
-            s_ref[sub % 2, :, :queries] = score_tile(
-                k_ref[place, keys_at, :], bias, qt_ref[place, own, queries_at], sub
-            )
-            dp_ref[sub % 2, :, :queries] = mm_nn(
-                v_ref[place, keys_at, :], widen_plain(dot_ref[place, own, queries_at], sub)
-            )
-
-        tiles(0)
         for sub in range(4):
             if sub < 3:
-                tiles(sub + 1)
+                tiles(place, group, queries, sub + 1)
+            else:
+                tiles(*following, queries, 0)
             own = slice(sub * HD, sub * HD + HD)
             q_rows, do_rows = qt_ref[place, own, queries_at], dot_ref[place, own, queries_at]
             delta = jnp.sum(
@@ -1184,27 +1234,50 @@
         side, part = lax.div(block, 2), lax.rem(block, 2)
         return wt_ref[side, :, pl.ds(pl.multiple_of(part * 128, 128), 128), :].reshape(384, 512)
 
-    acc_ref[...] = jnp.zeros_like(acc_ref)
     for place in range(4):
-        for name in ("qt", "kt", "dot", "ot", "k", "v"):
-            loads.wait((name, place))
-        if place == 0:
-            loads.wait("wt")
         shared_ref[place, 0:128, HALF:SEQ] = jnp.zeros((128, HALF), BF)
 
+    loaded(0)
+    load_block(1)
+    loads.wait("wt")
+
     def shared_step(place, carry):
-        heads(place, 0, HALF, shared_ref.at[place], 0, lambda: None)
-        acc_ref[0:SEQ] += mm_tn(shared_ref[place], weights_of(place))
+        for turn in range(3):
+
+            @pl.when(place == turn)
+            def _():
+                loaded(turn + 1)
+                if turn < 2:
+                    load_block(turn + 2)
+                else:
+                    loads.start("nt")
+                    loads.start("x")
+                    loads.start("dres")
+
+        heads(place, 0, HALF, shared_ref.at[place], 0, (jnp.minimum(place + 1, 3), 0), lambda: None)
         for turn in range(4):
 
             @pl.when(place == turn)
             def _():
                 run(SCHEDULE[1 + turn])
+                if turn == 0:
+                    spread("early", 0)
+                elif turn == 3:
+                    spread("early", 1)
 
         return carry
 
+    tiles(0, 0, HALF, 0)
     lax.fori_loop(0, 4, shared_step, 0)
-    far_send[...] = acc_ref[HALF:SEQ].astype(BF)
+    tiles(0, 1, SEQ, 0)
+    def rows_grad(grads, columns):
+        total = mm_tn(grads[0, :, columns], weights_of(0))
+        for place in range(1, 4):
+            total += mm_tn(grads[place, :, columns], weights_of(place))
+        return total
+
+    far_send[...] = rows_grad(shared_ref, slice(HALF, SEQ)).astype(BF)
+    spread("early", 2)
     sent.start("far", lambda: far_send, lambda: far_recv, to_peer)
     loads.wait("nt")
 
@@ -1219,18 +1292,19 @@
                     run(SCHEDULE[first + 2 * turn])
 
         out_base = pl.multiple_of((group - 1) * SEQ, SEQ)
-        heads(place, group, SEQ, grads_ref, out_base, lambda: pump(5))
+        after = jnp.minimum(step + 1, 7)
+        following = (lax.div(after, 2), 1 + lax.rem(after, 2))
+        heads(place, group, SEQ, grads_ref.at[place], out_base, following, lambda: pump(5))
 
         @pl.when(group == 2)
         def _():
             for part in range(3):
                 rows = slice(part * 128, part * 128 + 128)
                 total = mm_nt(nt_ref[:, 0:SEQ], shared_ref[place, rows, :])
-                total += mm_nt(nt_ref[:, SEQ:], grads_ref[rows, :])
+                total += mm_nt(nt_ref[:, SEQ:], grads_ref[place, rows, :])
                 g_ref[place, part] = total.astype(BF)
             ones = jnp.ones((8, 2 * SEQ), BF)
-            bsum_ref[place] = mm_nt(ones[:, :SEQ], shared_ref[place]) + mm_nt(ones, grads_ref[...])
-            acc_ref[SEQ:] += mm_tn(grads_ref[...], weights_of(place))
+            bsum_ref[place] = mm_nt(ones[:, :SEQ], shared_ref[place]) + mm_nt(ones, grads_ref[place])
 
         pump(6)
         return carry
@@ -1251,9 +1325,8 @@
         return sums[0] + folded[0], sums[1] + folded[1]
 
     def finish_step(index, sums):
-        sums = finish_rows(
-            index, acc_ref[pl.ds(pl.multiple_of(HALF * index + HALF, HALF), HALF), :], sums
-        )
+        columns = pl.ds(pl.multiple_of(HALF * index - HALF, HALF), HALF)
+        sums = finish_rows(index, rows_grad(grads_ref, columns), sums)
         for turn in range(1, 5):
 
             @pl.when(index == turn)
@@ -1265,46 +1338,18 @@
     zero = jnp.zeros((8, 512), F32)
     sums = lax.fori_loop(1, 5, finish_step, (zero, zero))
     sent.arrive("far")
-    sums = finish_rows(0, acc_ref[0:HALF] + far_recv[...].astype(F32), sums)
-
-    def small_row(place, value):
-        small_core[0, place : place + 1, :] = value
-
-    small_core[0] = jnp.zeros((16, 512), F32)
+    sums = finish_rows(0, rows_grad(shared_ref, slice(0, HALF)) + far_recv[...].astype(F32), sums)
+
     for place in range(4):
-        lanes = pl.ds(pl.multiple_of(block_at(place) * 128, 128), 128)
-        small_core[0, 0:1, lanes] = bsum_ref[place, 0:1, 0:128]
-        small_core[0, 1:2, lanes] = bsum_ref[place, 0:1, 256:384]
-        small_row(2 + place, jnp.sum(up_sum_ref[place], axis=0, keepdims=True))
-        small_row(8 + place, jnp.sum(two_ref[place], axis=0, keepdims=True))
-    for place in range(2):
-        small_row(6 + place, jnp.sum(sums[place], axis=0, keepdims=True))
-
-    me = mp * 8 + chip
-    rows_mine = pl.ds(pl.multiple_of(core_bit * 8, 8), 8)
-    rows_other = pl.ds(pl.multiple_of(8 - core_bit * 8, 8), 8)
-    sent.plan("small core", lambda: small_core.at[0, rows_other], lambda: small_core.at[1, rows_other], to_core)
-    sent.plan("square core", lambda: square_sum, lambda: square_core, to_core)
-    sent.plan("small back", lambda: small_part.at[rows_mine], lambda: small_part.at[rows_mine], to_core)
-    for place, target in enumerate(chips):
-        sent.plan(("small", place), lambda: small_all.at[me], lambda: small_all.at[me], target)
-        sent.plan(("square", place), lambda: square_all.at[me], lambda: square_all.at[me], target)
-
-    def everywhere(name, call):
-        for place in range(len(chips)):
-            call((name, place))
-
-    def small_stage(stage):
-        if stage == 0:
-            sent.arrive("small core")
-            small_all[me] = small_core[0, rows_mine] + small_core[1, rows_mine]
-            everywhere("small", sent.start)
-        elif stage == 1:
-            everywhere("small", sent.arrive)
-            small_part[rows_mine] = jnp.sum(small_all[...], axis=0)
-            sent.start("small back")
-        else:
-            sent.arrive("small back")
+        lanes = slice(place * 128, place * 128 + 128)
+        for row, value in enumerate((sums[0], sums[1])):
+            late_core[0, 8 + 4 * row + place : 9 + 4 * row + place, :] = jnp.sum(
+                value[:, lanes], axis=0, keepdims=True
+            )
+        for row, columns in enumerate((slice(0, 128), slice(256, 384))):
+            late_core[0, 4 * row + place : 4 * row + place + 1, :] = jnp.where(
+                mp == 0, bsum_ref[(place + 2) % 4, 0:1, columns], bsum_ref[place, 0:1, columns]
+            )
 
     def square_stage(stage):
         if stage == 0:
@@ -1315,15 +1360,25 @@
             everywhere("square", sent.start)
         else:
             everywhere("square", sent.arrive)
-            small = small_part[...]
-            small_out[...] = small
+            for row in range(4):
+                at = (0, 1, 6, 7)[row]
+                for lane in range(4):
+                    small_out[at : at + 1, lane * 128 : lane * 128 + 128] = late_part[
+                        4 * row + lane : 4 * row + lane + 1, :
+                    ]
+            for row in range(8):
+                at = 2 + row if row < 4 else 4 + row
+                small_out[at : at + 1, 0:256] = early_part[row : row + 1, :]
+                small_out[at : at + 1, 256:512] = early_part[8 + row : 9 + row, :]
+            small_out[12:16, :] = jnp.zeros((4, 512), F32)
+            small = small_out[...]
             total = jnp.sum(small * small) + jnp.sum(jnp.sum(square_all[...], axis=0))
             norm_out[...] = jnp.sqrt(jnp.full((8, 128), total, F32))
 
-    sent.start("small core")
+    sent.start(("late", "core"))
     for item in SCHEDULE[26]:
         if item[0] == "small":
-            small_stage(item[1])
+            spread("late", item[1])
         elif item[0] == "square":
             square_stage(item[1])
         else:
@@ -1354,13 +1409,14 @@
         scratch_shapes=[
             *[pltpu.VMEM((4, 128, ext), BF)] * 4, *[pltpu.VMEM((4, ext, 128), BF)] * 2,
             pltpu.VMEM((512, ext), BF), pltpu.VMEM((2, 3, 256, 512), BF), pltpu.VMEM((rows, 512), BF),
-            pltpu.VMEM((rows, 512), F32), pltpu.VMEM((4, 384, SEQ), BF), pltpu.VMEM((384, 2 * SEQ), BF),
-            pltpu.VMEM((ext, 512), F32), pltpu.VMEM((3, SEQ, 128), BF), pltpu.VMEM((2, SEQ, SEQ), F32),
+            pltpu.VMEM((rows, 512), F32), pltpu.VMEM((4, 384, SEQ), BF), pltpu.VMEM((4, 384, 2 * SEQ), BF),
+            pltpu.VMEM((3, SEQ, 128), BF), pltpu.VMEM((2, SEQ, SEQ), F32),
             pltpu.VMEM((2, SEQ, SEQ), F32), pltpu.VMEM((4, 3, 512, 128), BF), pltpu.VMEM((4, 8, 384), F32),
-            pltpu.VMEM((HALF, 512), BF), pltpu.VMEM((HALF, 512), BF), pltpu.VMEM((2, 16, 512), F32),
-            pltpu.VMEM((16, 512), F32), pltpu.VMEM((16, 8, 512), F32), pltpu.VMEM((8, 128), F32),
+            pltpu.VMEM((HALF, 512), BF), pltpu.VMEM((HALF, 512), BF), pltpu.VMEM((2, 16, 256), F32),
+            pltpu.VMEM((16, 256), F32), pltpu.VMEM((16, 8, 256), F32), pltpu.VMEM((2, 16, 128), F32),
+            pltpu.VMEM((16, 128), F32), pltpu.VMEM((16, 8, 128), F32), pltpu.VMEM((8, 128), F32),
             pltpu.VMEM((8, 128), F32), pltpu.VMEM((16, 8, 128), F32), *buffers,
-            pltpu.SemaphoreType.DMA((120,)), pltpu.SemaphoreType.DMA((120,)), pltpu.SemaphoreType.DMA((48,)),
+            pltpu.SemaphoreType.DMA((137,)), pltpu.SemaphoreType.DMA((137,)), pltpu.SemaphoreType.DMA((48,)),
         ],
         compiler_params=pltpu.CompilerParams(
             collective_id=1, has_side_effects=True, vmem_limit_bytes=VMEM_LIMIT
@@ -1369,22 +1425,57 @@
     )(key_count, qt, kt, dot, ot, k, v, lse, nt, wt, owns, fores, gp, patches, dres, vec_params, two, ups)
 
 
-def adam_kernel(norm_ref, *refs):
+ADAM_STEPS = 4
+
+
+def adam_step(weight, gradient, moment_one, moment_two, step_rate, decay_rate):
+    first_new = BETA_FIRST * moment_one + (1.0 - BETA_FIRST) * gradient
+    second_new = BETA_SECOND * moment_two + (1.0 - BETA_SECOND) * gradient * gradient
+    root = jnp.sqrt(second_new * (1.0 / (1.0 - BETA_SECOND**ADAM_STEP))) + ADAM_EPS
+    change = first_new * (step_rate / (1.0 - BETA_FIRST**ADAM_STEP)) / root
+    return weight * (1.0 - step_rate * decay_rate) - change, first_new, second_new
+
+
+def adam_kernel(norm_ref, small_ref, *refs):
+    mp = lax.axis_index("mp")
     factor = jnp.minimum(1.0, CLIP_NORM / (norm_ref[0:1, 0:1] + 1e-06))
+    vectors, refs = refs[:9], refs[9:]
+    matrices, refs = refs[:16], refs[16:]
+    results, vector_results, norm_out = refs[:12], refs[12:21], refs[21]
     for index in range(4):
-        weight_ref, one_ref, two_ref, grad_ref = refs[4 * index : 4 * index + 4]
-        outs = refs[16 + 3 * index : 19 + 3 * index]
-        results = adam_update(
+        weight_ref, one_ref, two_ref, grad_ref = matrices[4 * index : 4 * index + 4]
+        values = adam_step(
             weight_ref[...], grad_ref[...].astype(F32) * factor, one_ref[...], two_ref[...],
             MATRIX_RATE, DECAY_RATE,
         )
-        for out, value in zip(outs, results):
+        for out, value in zip(results[3 * index : 3 * index + 3], values):
             out[...] = value
 
-
-def adam_matrices(norm, groups):
-    steps = 8
-    in_specs, out_specs, out_shape, args = [full_spec((8, 128))], [], [], [norm]
+    @pl.when(pl.program_id(0) == 0)
+    def _():
+        norm_out[...] = norm_ref[0:1, 0:1]
+        first = mp == 0
+        qv = jnp.where(first, small_ref[0:2, 0:256], small_ref[0:2, 256:512])
+        up = jnp.where(first, small_ref[2:4, :], small_ref[4:6, :])
+        up = jnp.concatenate(
+            [up[row : row + 1, lane * 128 : lane * 128 + 128] for row in range(2) for lane in range(4)], axis=0
+        )
+        for index, total in enumerate((qv, up, small_ref[6:12, :])):
+            weight_ref, one_ref, two_ref = vectors[3 * index : 3 * index + 3]
+            values = adam_step(
+                weight_ref[...], total * factor, one_ref[...], two_ref[...], VECTOR_RATE, 0.0
+            )
+            for out, value in zip(vector_results[3 * index : 3 * index + 3], values):
+                out[...] = value
+
+
+def adam_all(norm, small, vectors, groups):
+    steps = ADAM_STEPS
+    in_specs, out_specs, out_shape = [full_spec((8, 128)), full_spec(small.shape)], [], []
+    args = [norm, small]
+    for vector in vectors:
+        in_specs += [full_spec(array.shape) for array in vector]
+        args += list(vector)
     for group in groups:
         rows, width = group[0].shape
         spec = pl.BlockSpec((rows // steps, width), lambda i: (i, 0))
@@ -1392,16 +1483,18 @@
         out_specs += [spec] * 3
         out_shape += [sds((rows, width), F32)] * 3
         args += list(group)
-    outs = pl.pallas_call(
+    for vector in vectors:
+        out_specs += [full_spec(array.shape) for array in vector]
+        out_shape += [sds(array.shape, F32) for array in vector]
+    return pl.pallas_call(
         adam_kernel,
         grid=(steps,),
-        out_shape=out_shape,
+        out_shape=out_shape + [sds((1, 1), F32)],
         in_specs=in_specs,
-        out_specs=out_specs,
+        out_specs=out_specs + [full_spec((1, 1))],
         compiler_params=pltpu.CompilerParams(vmem_limit_bytes=VMEM_LIMIT),
-        name="adam_matrices",
+        name="adam_all",
     )(*args)
-    return [outs[3 * index : 3 * index + 3] for index in range(len(groups))]
 
 
 IN_SPECS = (
@@ -1463,12 +1556,8 @@
     first_qkv, second_qkv, first_proj, second_proj, first_up, second_up, first_down, second_down,
     first_qv_bias, second_qv_bias, first_up_bias, second_up_bias, first_vec, second_vec,
 ):
-    mp = lax.axis_index("mp")
-    small = jnp.concatenate(
-        [up_bias[None, :], jnp.pad(qv_bias, ((0, 0), (0, 768))), jnp.zeros((5, 1024), F32)], axis=0
-    )
     wt, wp, wu, wd, small_all, nt, qt, kt, k, v, ot, lse = forward(
-        key_count, w_qkv, w_proj, w_up, w_down, small, patches, vec_params
+        key_count, w_qkv, w_proj, w_up, w_down, qv_bias, up_bias.reshape(1, 1024), patches, vec_params
     )
     activations, dres, dot, owns, fores, g_proj, vsum_two, up_sums = mlp(
         patches, cotangent, ot, wp, wu, wd, vec_params, small_all
@@ -1485,19 +1574,16 @@
         (w_up, first_up, second_up, up),
         (w_down, first_down, second_down, down),
     ]
-    new_qkv, new_proj, new_up, new_down = adam_matrices(norm, groups)
-    grad_norm = norm[0, 0]
-    factor = jnp.minimum(1.0, CLIP_NORM / (grad_norm + 1e-06))
-    qv_total = lax.dynamic_slice_in_dim(small_total[0:2], mp * 256, 256, 1)
-    up_total = lax.dynamic_slice_in_dim(small_total[2:6].reshape(-1), mp * 1024, 1024, 0)
-    new_qvb = adam_update(qv_bias, qv_total * factor, first_qv_bias, second_qv_bias, VECTOR_RATE, 0.0)
-    new_upb = adam_update(up_bias, up_total * factor, first_up_bias, second_up_bias, VECTOR_RATE, 0.0)
-    new_vec = adam_update(
-        vec_params, small_total[6:12] * factor, first_vec, second_vec, VECTOR_RATE, 0.0
-    )
+    square = lambda array: array.reshape(8, 128)
+    vectors = [
+        (qv_bias, first_qv_bias, second_qv_bias),
+        (square(up_bias), square(first_up_bias), square(second_up_bias)),
+        (vec_params, first_vec, second_vec),
+    ]
+    outs = adam_all(norm, small_total, vectors, groups)
     return (
-        activations, input_grad, grad_norm, *[array.reshape(w_qkv.shape) for array in new_qkv],
-        *new_proj, *new_up, *new_down, *new_qvb, *new_upb, *new_vec,
+        activations, input_grad, outs[21].reshape(()), *[array.reshape(w_qkv.shape) for array in outs[0:3]],
+        *outs[3:12], *outs[12:15], *[array.reshape(up_bias.shape) for array in outs[15:18]], *outs[18:21],
     )
 
 

time: 180 us -> 174 us (0.967)
  other arithmetic: 3.27 us -> 0 us
    sub x3 -> x0, other arithmetic: 1.88 us -> none  [adam_update(): weight - step_rate * (first_hat / (jnp.sqrt(second_hat) + ADAM_EPS) + dec...]
    unnamed x26 -> x6, local copies, waits for them, and re-layouts: 4.01 us -> 3.69 us
where the time goes in v4:
time: 174 us
  Pallas kernels  170 us (98%)
  local copies, waits for them, and re-layouts  3.69 us (2%)
    pallas_call x1, Pallas kernels, backward(): pl.pallas_call(backward_kernel, out_shape=[sds((rows, 512), F32), sds((10...  79.6 us
    pallas_call x1, Pallas kernels, forward(): pl.pallas_call(forward_kernel, out_shape=[sds((2, 3, 256, 512), BF), sds(...  38 us
    pallas_call x1, Pallas kernels, mlp(): pl.pallas_call(mlp_kernel, grid=(4,), out_shape=[sds((rows, 512), BF), sd...  33.7 us
    pallas_call x1, Pallas kernels, adam_all(): pl.pallas_call(adam_kernel, grid=(steps,), out_shape=out_shape + [sds((1,...  18.1 us
    unnamed x6, local copies, waits for them, and re-layouts  3.69 us

profile of v4, /device:TPU:1, one launch (start us, length us, event | category | flops | bytes accessed | tf_op | source)
XLA Modules:
  0.0 173.9 jit_solution(16332077144013916383)
XLA Ops:
  0.7 38.0 %forward.1 = (bf16[2,3,256,512]{3,2,1,0:T(8,128)(2,1)}, bf16[2,256,512]{2,1,0:T(8,128)(2,1)}, bf16[2,512,1024]{2,1,0:T(8,128)(2,1)}, bf16[2,1024,512]{2,1,0:T(8,...) custom-call(s32[5]{0:T(128)} %count_ref.3, ...), custom_call_target="tpu_custom_call" | custom-call | tf_op jit(solution)/shard_map/forward/pallas_call | solution.py:657
  38.7 33.7 %mlp.1 = (bf16[1280,512]{1,0:T(8,128)(2,1)}, f32[1280,512]{1,0:T(8,128)}, bf16[512,1536]{1,0:T(8,128)(2,1)}, bf16[2,2,256,512]{3,2,1,0:T(8,128)(2,1)}, bf16[2,25...) custom-call(bf16[1280,512]{1,0:T(8,128)(2,1)} %x_in.1, ...), custom_call_target="tpu_custom_call" | custom-call | tf_op jit(solution)/shard_map/mlp/pallas_call | solution.py:811
  72.4 79.6 %backward.1 = (f32[1280,512]{1,0:T(8,128)}, bf16[1024,512]{1,0:T(8,128)(2,1)}, bf16[512,1024]{1,0:T(8,128)(2,1)}, bf16[256,512]{1,0:T(8,128)(2,1)}, bf16[3,512,2...) custom-call(s32[5]{0:T(128)} %count_ref.3, bf16[512,1536]{1,0:T(8,128)(2,1)} %get-tuple-element.79.qt_in, ...), custom_call_target="tpu_custom_call" | custom-call | tf_op jit(solution)/shard_map/backward/pallas_call | solution.py:1401
  152.1 0.0 copy-start.1
  152.1 18.1 %adam_all.1 = (f32[1536,256]{1,0:T(8,128)}, f32[1536,256]{1,0:T(8,128)}, f32[1536,256]{1,0:T(8,128)}, f32[256,512]{1,0:T(8,128)}, f32[256,512]{1,0:T(8,128)}, /*...) custom-call(f32[8,128]{1,0:T(8,128)} %get-tuple-element.94.norm_ref,, ...), custom_call_target="tpu_custom_call" | custom-call | tf_op jit(solution)/shard_map/adam_all/pallas_call | solution.py:1489
  170.2 0.0 copy-start
  170.2 0.0 copy-done.1
  170.2 1.1 copy.50
  171.3 1.1 copy-done
  172.4 1.5 copy.51
Async XLA Ops:
  152.1 18.2 %copy-start.1 = (bf16[1280,512]{1,0:T(8,128)(2,1)S(1)}, bf16[1280,512]{1,0:T(8,128)(2,1)}, u32[]{:S(2)}) copy-start(bf16[1280,512]{1,0:T(8,128)(2,1)} %get-tuple-element.146) | copy-start | bytes 3932164
  170.2 2.2 %copy-start = (f32[1280,512]{1,0:T(8,128)S(1)}, f32[1280,512]{1,0:T(8,128)}, u32[]{:S(2)}) copy-start(f32[1280,512]{1,0:T(8,128)} %get-tuple-element.147) | copy-start | bytes 7864324

commit v5 on v4

--- a/solution.py
+++ b/solution.py
@@ -434,14 +434,19 @@
 
 
 def forward_kernel(
-    count_ref, qkv_ref, proj_ref, up_ref, down_ref, qv_ref, up_bias_ref, x_ref, vec_ref,
+    count_ref, qkv_ref, proj_in, up_in, down_in, qv_ref, up_bias_ref, x_in, vec_ref,
     wt_out, wp_out, wu_out, wd_out, sm_out,
     nt_out, qt_out, kt_out, k_out, v_out, ot_out, lse_out,
     wt_ref, own_proj, own_up, own_down, sm_ref, other_ref,
     norm_ref, nt_ref, qt_ref, kt_ref, vt_ref, k_ref, v_ref, ot_ref, lse_ref, bias_ref, s_ref,
-    send_sem, recv_sem, local_sem,
+    proj_ref, up_ref, down_ref, x_ref, send_sem, recv_sem, local_sem, input_sem,
 ):
     dp, mp = lax.axis_index("dp"), lax.axis_index("mp")
+    inputs = Loads(input_sem)
+    for name, src, dst in (
+        ("x", x_in, x_ref), ("proj", proj_in, proj_ref), ("up", up_in, up_ref), ("down", down_in, down_ref)
+    ):
+        inputs.start(name, lambda src=src: src, lambda dst=dst: dst)
     peer = 1 - mp
     core, x_side, _, _ = partners(dp)
     quarter = lax.rem(dp, 4)
@@ -525,9 +530,13 @@
     sm_ref[mp, 0:1, :] = up_bias_ref[...]
     sm_ref[mp, 1:3, 0:256] = qv_ref[...]
     small_copy = send(lambda: sm_ref.at[mp], lambda: sm_ref.at[mp], {"mp": peer})
+    inputs.wait("proj")
     own_proj[...] = proj_ref[...].astype(BF)
+    inputs.wait("up")
     own_up[...] = up_ref[...].astype(BF)
+    inputs.wait("down")
     own_down[...] = down_ref[...].astype(BF)
+    inputs.wait("x")
     keep(wt_ref.at[mp], wt_out.at[mp])
     keep(own_proj, wp_out.at[mp])
     keep(own_up, wu_out.at[mp])
@@ -662,7 +671,7 @@
             sds((512, ext), BF), sds((512, ext), BF), sds((512, ext), BF), sds((ext, 512), BF),
             sds((ext, 512), BF), sds((512, ext), BF), sds((3, 4, 8, SEQ), F32),
         ],
-        in_specs=[pl.BlockSpec(memory_space=pltpu.SMEM)] + [vmem] * 8,
+        in_specs=[pl.BlockSpec(memory_space=pltpu.SMEM), vmem, hbm, hbm, hbm, vmem, vmem, hbm, vmem],
         out_specs=[hbm] * 12,
         scratch_shapes=[
             pltpu.VMEM((2, 3, 256, 512), BF), pltpu.VMEM((256, 512), BF), pltpu.VMEM((512, 1024), BF),
@@ -671,7 +680,9 @@
             pltpu.VMEM((512, ext), BF), pltpu.VMEM((512, SEQ), BF), pltpu.VMEM((ext, 512), BF),
             pltpu.VMEM((ext, 512), BF), pltpu.VMEM((512, ext), BF), pltpu.VMEM((3, 4, 8, SEQ), F32),
             pltpu.VMEM((3, SEQ, 128), BF), pltpu.VMEM((2, SEQ, SEQ), F32),
-            pltpu.SemaphoreType.DMA((34,)), pltpu.SemaphoreType.DMA((34,)), pltpu.SemaphoreType.DMA((40,)),
+            pltpu.VMEM((256, 512), F32), pltpu.VMEM((512, 1024), F32), pltpu.VMEM((1024, 512), F32),
+            pltpu.VMEM(patches.shape, BF), pltpu.SemaphoreType.DMA((34,)), pltpu.SemaphoreType.DMA((34,)),
+            pltpu.SemaphoreType.DMA((40,)), pltpu.SemaphoreType.DMA((4,)),
         ],
         compiler_params=pltpu.CompilerParams(
             collective_id=0, has_side_effects=True, vmem_limit_bytes=VMEM_LIMIT
@@ -681,10 +692,10 @@
 
 
 def mlp_kernel(
-    x_ref, dy_ref, ot_ref, wp_ref, wu_ref, wd_ref, vec_ref, small_ref,
+    x_ref, dy_ref, ot_ref, wp_ref, wu_in, wd_in, vec_ref, small_ref,
     act_ref, dres_ref, dot_ref, own_out, fore_out, gp_ref, vsum_ref, bsum_ref,
     res_ref, n2_ref, out_ref, dn_ref, hid_ref, dup_ref, dyc_ref, br_ref,
-    g_ref, fore_ref, fore_core, own_core, own_peer, send_sem, recv_sem,
+    g_ref, fore_ref, fore_core, own_core, own_peer, wu_ref, wd_ref, send_sem, recv_sem, input_sem,
 ):
     step = pl.program_id(0)
     dp, mp = lax.axis_index("dp"), lax.axis_index("mp")
@@ -709,8 +720,23 @@
     def rows(index):
         return pl.ds(pl.multiple_of(index * HALF, HALF), HALF)
 
+    inputs = Loads(input_sem)
+    for turn in range(4):
+        at, columns = (peer, mp)[turn // 2], slice(turn % 2 * 512, turn % 2 * 512 + 512)
+        inputs.plan(
+            ("up", turn), lambda at=at, columns=columns: wu_in.at[at, :, columns],
+            lambda at=at, columns=columns: wu_ref.at[at, :, columns],
+        )
+        inputs.plan(
+            ("down", turn), lambda at=at, columns=columns: wd_in.at[at, columns, :],
+            lambda at=at, columns=columns: wd_ref.at[at, columns, :],
+        )
+
     @pl.when(step == 0)
     def _():
+        for turn in range(4):
+            inputs.start(("up", turn))
+            inputs.start(("down", turn))
         greet([{"dp": core}, {"mp": peer}])
 
         def body(index, carry):
@@ -725,6 +751,13 @@
             return carry
 
         lax.fori_loop(0, 5, body, 0, unroll=True)
+
+    for turn in range(4):
+
+        @pl.when(step == turn)
+        def _():
+            inputs.wait(("up", turn))
+            inputs.wait(("down", turn))
 
     lanes = pl.ds(pl.multiple_of(part * 512, 512), 512)
     w_up, w_down = wu_ref[side, :, lanes], wd_ref[side, lanes, :]
@@ -808,6 +841,7 @@
 def mlp(patches, cotangent, ot, wp, wu, wd, vec_params, small):
     rows = patches.shape[0]
     ext = 3 * SEQ
+    hbm = pl.BlockSpec(memory_space=pl.ANY)
     return pl.pallas_call(
         mlp_kernel,
         grid=(4,),
@@ -817,7 +851,7 @@
         ],
         in_specs=[
             full_spec((rows, 512)), full_spec((rows, 512)), full_spec((512, ext)), full_spec(wp.shape),
-            full_spec(wu.shape), full_spec(wd.shape), full_spec(vec_params.shape), full_spec(small.shape),
+            hbm, hbm, full_spec(vec_params.shape), full_spec(small.shape),
         ],
         out_specs=[
             full_spec((rows, 512)), full_spec((rows, 512)), full_spec((512, ext)),
@@ -830,7 +864,8 @@
             pltpu.VMEM((rows, 512), BF), pltpu.VMEM((rows, 512), BF), pltpu.VMEM((4, 2, 512, 512), BF),
             pltpu.VMEM((2, HALF, 512), BF), pltpu.VMEM((2, 2, HALF, 512), BF),
             pltpu.VMEM((2, 2, HALF, 512), BF), pltpu.VMEM((2, HALF, 512), BF),
-            pltpu.SemaphoreType.DMA((5,)), pltpu.SemaphoreType.DMA((5,)),
+            pltpu.VMEM(wu.shape, BF), pltpu.VMEM(wd.shape, BF), pltpu.SemaphoreType.DMA((5,)),
+            pltpu.SemaphoreType.DMA((5,)), pltpu.SemaphoreType.DMA((8,)),
         ],
         compiler_params=pltpu.CompilerParams(
             collective_id=2, has_side_effects=True, vmem_limit_bytes=VMEM_LIMIT
@@ -937,7 +972,7 @@
     count_ref, qt_in, kt_in, dot_in, ot_in, k_in, v_in, lse_ref, nt_in, wt_in,
     own_in, fore_in, gp_in, x_in, dres_in, vec_ref, two_ref, up_sum_ref,
     grad_out, down_out, up_out, proj_out, qkv_out, small_out, norm_out,
-    qt_ref, kt_ref, dot_ref, ot_ref, k_ref, v_ref, nt_ref, wt_ref, x_ref, dres_ref,
+    qt_ref, kt_ref, dot_ref, ot_ref, k_ref, v_ref, nt_ref, wt_ref, x_ref, dres_ref, grad_ref,
     shared_ref, grads_ref, bias_ref, s_ref, dp_ref, g_ref, bsum_ref,
     far_send, far_recv, early_core, early_part, early_all, late_core, late_part, late_all, square_sum, square_core, square_all, *rest,
 ):
@@ -1316,11 +1351,18 @@
     loads.wait("dres")
     run(SCHEDULE[21])
 
+    for index in range(5):
+        where = pl.ds(row_block(index, mp), HALF)
+        loads.plan(
+            ("grad", index), lambda where=where: grad_ref.at[where, :],
+            lambda where=where: grad_out.at[where, :],
+        )
+
     def finish_rows(index, dn, sums):
         at = pl.ds(pl.multiple_of(index * HALF, HALF), HALF)
         place = pl.ds(row_block(index, mp), HALF)
         _, unit, inverse = layer_norm_rows(x_ref[place, :].astype(F32), gain, shift)
-        grad_out[place, :] = dres_ref[at, :] + layer_norm_back(dn, unit, inverse, gain)
+        grad_ref[place, :] = dres_ref[at, :] + layer_norm_back(dn, unit, inverse, gain)
         folded = [jnp.sum(value.reshape(HALF // 8, 8, 512), axis=0) for value in (dn * unit, dn)]
         return sums[0] + folded[0], sums[1] + folded[1]
 
@@ -1331,6 +1373,7 @@
 
             @pl.when(index == turn)
             def _():
+                loads.start(("grad", turn))
                 run(SCHEDULE[21 + turn])
 
         return sums
@@ -1339,6 +1382,7 @@
     sums = lax.fori_loop(1, 5, finish_step, (zero, zero))
     sent.arrive("far")
     sums = finish_rows(0, rows_grad(shared_ref, slice(0, HALF)) + far_recv[...].astype(F32), sums)
+    loads.start(("grad", 0))
 
     for place in range(4):
         lanes = slice(place * 128, place * 128 + 128)
@@ -1386,6 +1430,8 @@
     sent.finish()
     for index in range(7):
         loads.wait(("out", index))
+    for index in range(5):
+        loads.wait(("grad", index))
 
 
 def backward(key_count, qt, kt, dot, ot, k, v, lse, nt, wt, owns, fores, gp, patches, dres, vec_params, two, ups):
@@ -1405,11 +1451,11 @@
             sds((3, 512, 256), BF), sds((16, 512), F32), sds((8, 128), F32),
         ],
         in_specs=[pl.BlockSpec(memory_space=pltpu.SMEM)] + [hbm] * 6 + [vmem] + [hbm] * 7 + [vmem] * 3,
-        out_specs=[vmem] + [hbm] * 4 + [vmem] * 2,
+        out_specs=[hbm] * 5 + [vmem] * 2,
         scratch_shapes=[
             *[pltpu.VMEM((4, 128, ext), BF)] * 4, *[pltpu.VMEM((4, ext, 128), BF)] * 2,
             pltpu.VMEM((512, ext), BF), pltpu.VMEM((2, 3, 256, 512), BF), pltpu.VMEM((rows, 512), BF),
-            pltpu.VMEM((rows, 512), F32), pltpu.VMEM((4, 384, SEQ), BF), pltpu.VMEM((4, 384, 2 * SEQ), BF),
+            pltpu.VMEM((rows, 512), F32), pltpu.VMEM((rows, 512), F32), pltpu.VMEM((4, 384, SEQ), BF), pltpu.VMEM((4, 384, 2 * SEQ), BF),
             pltpu.VMEM((3, SEQ, 128), BF), pltpu.VMEM((2, SEQ, SEQ), F32),
             pltpu.VMEM((2, SEQ, SEQ), F32), pltpu.VMEM((4, 3, 512, 128), BF), pltpu.VMEM((4, 8, 384), F32),
             pltpu.VMEM((HALF, 512), BF), pltpu.VMEM((HALF, 512), BF), pltpu.VMEM((2, 16, 256), F32),

time: 174 us -> 170 us (0.977)
  Pallas kernels: 170 us -> 166 us
    pallas_call x1, Pallas kernels: 38 us -> 36.2 us  [forward(): pl.pallas_call(forward_kernel, out_shape=[sds((2, 3, 256, 512), BF), sds(...]
where the time goes in v5:
time: 170 us
  Pallas kernels  166 us (98%)
  local copies, waits for them, and re-layouts  3.69 us (2%)
    pallas_call x1, Pallas kernels, backward(): pl.pallas_call(backward_kernel, out_shape=[sds((rows, 512), F32), sds((10...  78.9 us
    pallas_call x1, Pallas kernels, forward(): pl.pallas_call(forward_kernel, out_shape=[sds((2, 3, 256, 512), BF), sds(...  36.2 us
    pallas_call x1, Pallas kernels, mlp(): pl.pallas_call(mlp_kernel, grid=(4,), out_shape=[sds((rows, 512), BF), sd...  32.6 us
    pallas_call x1, Pallas kernels, adam_all(): pl.pallas_call(adam_kernel, grid=(steps,), out_shape=out_shape + [sds((1,...  18.1 us
    unnamed x6, local copies, waits for them, and re-layouts  3.69 us

profile of v5, /device:TPU:1, one launch (start us, length us, event | category | flops | bytes accessed | tf_op | source)
XLA Modules:
  0.0 170.1 jit_solution(18104178214236242320)
XLA Ops:
  0.7 36.2 %forward.1 = (bf16[2,3,256,512]{3,2,1,0:T(8,128)(2,1)}, bf16[2,256,512]{2,1,0:T(8,128)(2,1)}, bf16[2,512,1024]{2,1,0:T(8,128)(2,1)}, bf16[2,1024,512]{2,1,0:T(8,...) custom-call(s32[5]{0:T(128)} %count_ref.3, ...), custom_call_target="tpu_custom_call" | custom-call | tf_op jit(solution)/shard_map/forward/pallas_call | solution.py:666
  36.8 32.6 %mlp.1 = (bf16[1280,512]{1,0:T(8,128)(2,1)}, f32[1280,512]{1,0:T(8,128)}, bf16[512,1536]{1,0:T(8,128)(2,1)}, bf16[2,2,256,512]{3,2,1,0:T(8,128)(2,1)}, bf16[2,25...) custom-call(bf16[1280,512]{1,0:T(8,128)(2,1)} %x_in.3, ...), custom_call_target="tpu_custom_call" | custom-call | tf_op jit(solution)/shard_map/mlp/pallas_call | solution.py:845
  69.4 78.9 %backward.1 = (f32[1280,512]{1,0:T(8,128)}, bf16[1024,512]{1,0:T(8,128)(2,1)}, bf16[512,1024]{1,0:T(8,128)(2,1)}, bf16[256,512]{1,0:T(8,128)(2,1)}, bf16[3,512,2...) custom-call(s32[5]{0:T(128)} %count_ref.3, bf16[512,1536]{1,0:T(8,128)(2,1)} %get-tuple-element.79.qt_in, ...), custom_call_target="tpu_custom_call" | custom-call | tf_op jit(solution)/shard_map/backward/pallas_call | solution.py:1447
  148.3 0.0 copy-start.1
  148.3 18.1 %adam_all.1 = (f32[1536,256]{1,0:T(8,128)}, f32[1536,256]{1,0:T(8,128)}, f32[1536,256]{1,0:T(8,128)}, f32[256,512]{1,0:T(8,128)}, f32[256,512]{1,0:T(8,128)}, /*...) custom-call(f32[8,128]{1,0:T(8,128)} %get-tuple-element.94.norm_ref,, ...), custom_call_target="tpu_custom_call" | custom-call | tf_op jit(solution)/shard_map/adam_all/pallas_call | solution.py:1535
  166.4 0.0 copy-start
  166.4 0.0 copy-done.1
  166.4 1.1 copy.50
  167.5 1.1 copy-done
  168.6 1.5 copy.51
Async XLA Ops:
  148.3 18.2 %copy-start.1 = (bf16[1280,512]{1,0:T(8,128)(2,1)S(1)}, bf16[1280,512]{1,0:T(8,128)(2,1)}, u32[]{:S(2)}) copy-start(bf16[1280,512]{1,0:T(8,128)(2,1)} %get-tuple-element.146) | copy-start | bytes 3932164
  166.4 2.2 %copy-start = (f32[1280,512]{1,0:T(8,128)S(1)}, f32[1280,512]{1,0:T(8,128)}, u32[]{:S(2)}) copy-start(f32[1280,512]{1,0:T(8,128)} %get-tuple-element.147) | copy-start | bytes 7864324

commit v6 on v5

--- a/solution.py
+++ b/solution.py
@@ -887,19 +887,18 @@
         ("O", 0, 2),
     ),
     (
-    ),
-    (
-        ("F", 4, 1), ("O", 1, 2), ("O", 2, 1),
-    ),
-    (
-    ),
-    (
-    ),
-    (
-        ("F", 5, 0), ("O", 0, 3), ("O", 3, 1),
-    ),
-    (
-        ("O", 1, 3),
+        ("O", 1, 2), ("O", 2, 1),
+    ),
+    (
+        ("F", 4, 1),
+    ),
+    (
+    ),
+    (
+        ("O", 0, 3),
+    ),
+    (
+        ("F", 5, 0), ("O", 1, 3), ("O", 3, 1),
     ),
     (
         ("F", 5, 1), ("O", 4, 1),
@@ -908,35 +907,34 @@
         ("O", 2, 2),
     ),
     (
-        ("F", 6, 0), ("O", 0, 4),
-    ),
-    (
-        ("O", 3, 2),
-    ),
-    (
-        ("F", 6, 1), ("O", 1, 4),
-    ),
-    (
-        ("O", 4, 2),
-    ),
-    (
-        ("O", 0, 5), ("O", 2, 3), ("O", 5, 0),
-    ),
-    (
-    ),
-    (
-        ("O", 0, 6), ("O", 1, 5), ("O", 3, 3),
+        ("O", 0, 4),
+    ),
+    (
+        ("F", 6, 0), ("O", 1, 4), ("O", 3, 2),
+    ),
+    (
+        ("F", 6, 1), ("O", 4, 2),
+    ),
+    (
+        ("O", 0, 5), ("O", 2, 3),
+    ),
+    (
+        ("O", 0, 6),
+    ),
+    (
+        ("O", 1, 5), ("O", 3, 3), ("O", 5, 0),
+    ),
+    (
+        ("O", 1, 6),
     ),
     (
         ("O", 4, 3),
     ),
     (
-        ("O", 1, 6), ("O", 2, 4), ("O", 6, 0),
-    ),
-    (
-        ("O", 5, 1),
-    ),
-    (
+        ("O", 2, 4), ("O", 5, 1),
+    ),
+    (
+        ("O", 6, 0),
     ),
     (
         ("O", 3, 4),
@@ -945,12 +943,17 @@
         ("O", 6, 1),
     ),
     (
-        ("O", 4, 4),
-    ),
-    (
-        ("O", 2, 5), ("small", 0), ("O", 5, 3), ("O", 2, 6), ("O", 3, 5), ("O", 4, 5), ("O", 3, 6),
-        ("small", 1), ("O", 4, 6), ("O", 6, 3), ("small", 2), ("square", 0), ("square", 1), ("O", 5, 5),
-        ("square", 2), ("O", 5, 6), ("O", 6, 5), ("O", 6, 6),
+        ("O", 2, 5), ("O", 4, 4),
+    ),
+    (
+        ("O", 2, 6),
+    ),
+    (
+        ("O", 3, 5), ("O", 5, 3),
+    ),
+    (
+        ("O", 4, 5), ("O", 3, 6), ("small", 0), ("O", 4, 6), ("O", 6, 3), ("square", 0), ("square", 1),
+        ("small", 1), ("small", 2), ("O", 5, 5), ("square", 2), ("O", 5, 6), ("O", 6, 5), ("O", 6, 6),
     ),
 )
 

time: 170 us -> 169 us (level)
  no operation moved by 1% of the time
where the time goes in v6:
time: 169 us
  Pallas kernels  165 us (98%)
  local copies, waits for them, and re-layouts  3.69 us (2%)
    pallas_call x1, Pallas kernels, backward(): pl.pallas_call(backward_kernel, out_shape=[sds((rows, 512), F32), sds((10...  77.7 us
    pallas_call x1, Pallas kernels, forward(): pl.pallas_call(forward_kernel, out_shape=[sds((2, 3, 256, 512), BF), sds(...  36.2 us
    pallas_call x1, Pallas kernels, mlp(): pl.pallas_call(mlp_kernel, grid=(4,), out_shape=[sds((rows, 512), BF), sd...  32.6 us
    pallas_call x1, Pallas kernels, adam_all(): pl.pallas_call(adam_kernel, grid=(steps,), out_shape=out_shape + [sds((1,...  18.1 us
    unnamed x6, local copies, waits for them, and re-layouts  3.69 us

profile of v6, /device:TPU:1, one launch (start us, length us, event | category | flops | bytes accessed | tf_op | source)
XLA Modules:
  0.0 168.9 jit_solution(11916638993810160884)
XLA Ops:
  0.7 36.2 %forward.1 = (bf16[2,3,256,512]{3,2,1,0:T(8,128)(2,1)}, bf16[2,256,512]{2,1,0:T(8,128)(2,1)}, bf16[2,512,1024]{2,1,0:T(8,128)(2,1)}, bf16[2,1024,512]{2,1,0:T(8,...) custom-call(s32[5]{0:T(128)} %count_ref.3, ...), custom_call_target="tpu_custom_call" | custom-call | tf_op jit(solution)/shard_map/forward/pallas_call | solution.py:666
  36.8 32.6 %mlp.1 = (bf16[1280,512]{1,0:T(8,128)(2,1)}, f32[1280,512]{1,0:T(8,128)}, bf16[512,1536]{1,0:T(8,128)(2,1)}, bf16[2,2,256,512]{3,2,1,0:T(8,128)(2,1)}, bf16[2,25...) custom-call(bf16[1280,512]{1,0:T(8,128)(2,1)} %x_in.3, ...), custom_call_target="tpu_custom_call" | custom-call | tf_op jit(solution)/shard_map/mlp/pallas_call | solution.py:845
  69.4 77.7 %backward.1 = (f32[1280,512]{1,0:T(8,128)}, bf16[1024,512]{1,0:T(8,128)(2,1)}, bf16[512,1024]{1,0:T(8,128)(2,1)}, bf16[256,512]{1,0:T(8,128)(2,1)}, bf16[3,512,2...) custom-call(s32[5]{0:T(128)} %count_ref.3, bf16[512,1536]{1,0:T(8,128)(2,1)} %get-tuple-element.79.qt_in, ...), custom_call_target="tpu_custom_call" | custom-call | tf_op jit(solution)/shard_map/backward/pallas_call | solution.py:1450
  147.1 0.0 copy-start.1
  147.1 18.1 %adam_all.1 = (f32[1536,256]{1,0:T(8,128)}, f32[1536,256]{1,0:T(8,128)}, f32[1536,256]{1,0:T(8,128)}, f32[256,512]{1,0:T(8,128)}, f32[256,512]{1,0:T(8,128)}, /*...) custom-call(f32[8,128]{1,0:T(8,128)} %get-tuple-element.94.norm_ref,, ...), custom_call_target="tpu_custom_call" | custom-call | tf_op jit(solution)/shard_map/adam_all/pallas_call | solution.py:1538
  165.2 0.0 copy-start
  165.2 0.0 copy-done.1
  165.2 1.1 copy.50
  166.3 1.1 copy-done
  167.4 1.5 copy.51
Async XLA Ops:
  147.1 18.2 %copy-start.1 = (bf16[1280,512]{1,0:T(8,128)(2,1)S(1)}, bf16[1280,512]{1,0:T(8,128)(2,1)}, u32[]{:S(2)}) copy-start(bf16[1280,512]{1,0:T(8,128)(2,1)} %get-tuple-element.146) | copy-start | bytes 3932164
  165.2 2.2 %copy-start = (f32[1280,512]{1,0:T(8,128)S(1)}, f32[1280,512]{1,0:T(8,128)}, u32[]{:S(2)}) copy-start(f32[1280,512]{1,0:T(8,128)} %get-tuple-element.147) | copy-start | bytes 7864324
